TPU v7x, 512 devices: a whole 4x4x16 slice. The times are simulated.
512 devices in a mesh: dp: 4 (over y), frames: 16 (over z), height: 8 (over x, core).
Axes of the slice: x: 4, y: 4, z: 16, core: 2. Of those that a mesh axis runs over, the one named last changes fastest.
Arguments:
- video: bfloat16 [512, 8, 16, 640], P(('dp', 'frames'), 'height'), parts along dimension 0
- window_gaps: int32 [112], P('dp'), parts along dimension 0, may hold values from 1 to 8, 112 in all
- gn_gain: float32 [640], replicated, may hold values from 0.25 to 1.75
- gn_bias: float32 [640], replicated, may hold values from -3 to 3
- conv_weight: bfloat16 [5760, 640], P('frames', 'height'), may hold values from -0.078125 to 0.078125
- conv_bias: float32 [640], replicated, may hold values from -3 to 3
- ln_gain: float32 [640], replicated, may hold values from 0.25 to 1.75
- ln_bias: float32 [640], replicated, may hold values from -3 to 3
- qkv_weight: bfloat16 [640, 1920], replicated, may hold values from -0.25 to 0.25
- out_weight: bfloat16 [640, 640], replicated, may hold values from -0.5 to 0.5
- out_bias: float32 [640], replicated, may hold values from -3 to 3
Outputs:
- output: bfloat16 [512, 8, 16, 640], P(('dp', 'frames'), 'height'), parts along dimension 0
There are 4 independent parts, one for each index of `dp`. A program takes and returns all parts, laid end to end along the dimension named above; an argument that names none is the same for every part. Nothing has to cross between parts.
Inputs may be any that keep to these rules, and one draw needn't show every extreme that they name: `window_gaps`: the first window starts at frame 0 and the last at 112; the largest gap 16 // 2 is reached in every draw.
All inputs are finite; a program needn't handle non-finite values.
Results may differ from a plain program's by a relative error of at most 0.008.
Values may be sent and summed in bfloat16 or wider, within the bound.
No kernel may reach another device: no remote copies, remote signals or barrier semaphores. Data moves between devices by JAX's collectives and lax.ppermute only.
A program may use at most 64 MiB of HBM per device.

v0:
```python
import jax
import jax.numpy as jnp
from jax import lax
from jax.sharding import PartitionSpec as P

HEADS = 10
GROUPS = 32
WIN = 16
HEAD_DIM = 64


EPSILON = 1e-05


def passed_along(shard, axis, by):
    size = lax.axis_size(axis)
    pairs = [(i, i + by) for i in range(size) if 0 <= i + by < size]
    return lax.ppermute(shard, axis, pairs)


def extended_2(cells, sides, width):
    for axis, dim in sides:
        count = lax.axis_size(axis)
        ends = count - 1
        head = lax.slice_in_dim(cells, 0, width, axis=dim)
        tail = lax.slice_in_dim(cells, cells.shape[dim] - width, cells.shape[dim], axis=dim)
        cells = jnp.concatenate(
            [
                lax.ppermute(tail, axis, [(i, (i + 1) % count) for i in range(ends)]),
                cells,
                lax.ppermute(head, axis, [((i + 1) % count, i) for i in range(ends)]),
            ],
            axis=dim,
        )
    return cells


def fetch_neighbour(keys, values, offset):
    return passed_along((keys, values), "frames", offset)


def window_starts(window_gaps):
    return jnp.concatenate([jnp.zeros((1,), jnp.int32), jnp.cumsum(window_gaps)])


def on_device(
    video,
    window_gaps,
    gn_gain,
    gn_bias,
    conv_weight,
    conv_bias,
    ln_gain,
    ln_bias,
    qkv_weight,
    out_weight,
    out_bias,
):
    frames_dev, rows_dev, width, chans = video.shape
    bands = lax.axis_size("height")
    floats = video.astype(jnp.float32)
    grouped = floats.reshape(frames_dev, rows_dev, width, GROUPS, chans // GROUPS)
    cell_count = rows_dev * bands * width * (chans // GROUPS)
    mean = lax.psum(jnp.sum(grouped, axis=(1, 2, 4)), "height") / cell_count
    centred = grouped - mean[:, None, None, :, None]
    variance = lax.psum(jnp.sum(centred * centred, axis=(1, 2, 4)), "height") / cell_count
    scaled = (grouped - mean[:, None, None, :, None]) * lax.rsqrt(variance + EPSILON)[
        :, None, None, :, None
    ]
    normed = scaled.reshape(floats.shape) * gn_gain + gn_bias
    activated = jax.nn.silu(normed).astype(jnp.bfloat16)
    columns = lax.all_gather(conv_weight, "height", axis=1, tiled=True)
    extended = extended_2(activated, (("height", 1),), 1)
    extended = jnp.pad(extended, ((0, 0), (0, 0), (1, 1), (0, 0)))
    patches = jnp.concatenate(
        [
            extended[:, row_off : row_off + rows_dev, col_off : col_off + width]
            for row_off in range(3)
            for col_off in range(3)
        ],
        axis=3,
    ).reshape(-1, 9 * chans)
    conv_sum = jnp.dot(
        patches,
        lax.all_gather(columns, "frames", axis=0, tiled=True),
        preferred_element_type=jnp.float32,
    )
    conv_out = (
        (conv_sum + conv_bias).astype(jnp.bfloat16).reshape(frames_dev, rows_dev, width, chans)
    )
    conv_out = lax.optimization_barrier(conv_out)
    resid_state = (floats + conv_out.astype(jnp.float32)).astype(jnp.bfloat16)
    resid_float = resid_state.astype(jnp.float32)
    centre = jnp.mean(resid_float, axis=-1, keepdims=True)
    deviation = resid_float - centre
    spread = jnp.mean(deviation * deviation, axis=-1, keepdims=True)
    normalized = (deviation * lax.rsqrt(spread + EPSILON) * ln_gain + ln_bias).astype(jnp.bfloat16)
    cells = rows_dev * width
    project = jnp.dot(
        normalized.reshape(-1, chans), qkv_weight, preferred_element_type=jnp.float32
    ).astype(jnp.bfloat16)
    scale = HEAD_DIM ** (-0.5)
    starts = window_starts(window_gaps)
    project = project.reshape(frames_dev, cells, 3 * chans)
    query = project[:, :, :chans]
    keys = project[:, :, chans : 2 * chans]
    values = project[:, :, 2 * chans :]
    gathered = [fetch_neighbour(keys, values, offset) for offset in (2, 1)]
    gathered.append((keys, values))
    gathered = gathered + [fetch_neighbour(keys, values, offset) for offset in (-1, -2)]
    keys_near = jnp.concatenate([pair[0] for pair in gathered], axis=0).reshape(
        -1, cells, HEADS, HEAD_DIM
    )
    values_near = jnp.concatenate([pair[1] for pair in gathered], axis=0).reshape(
        -1, cells, HEADS, HEAD_DIM
    )
    near_ids = (lax.axis_index("frames") - 2) * frames_dev + jnp.arange(
        5 * frames_dev, dtype=jnp.int32
    )
    inside = (near_ids[None, :] >= starts[:, None]) & (near_ids[None, :] < starts[:, None] + WIN)
    member = inside.astype(jnp.float32)
    cover = member[:, 2 * frames_dev : 3 * frames_dev].T
    frame_count = jnp.sum(cover, axis=1)
    scores = (
        jnp.einsum(
            "nshd,mshd->shnm",
            query.reshape(frames_dev, cells, HEADS, HEAD_DIM),
            keys_near,
            preferred_element_type=jnp.float32,
        )
        * scale
    )
    expo = jnp.exp(scores)
    window_sum = jnp.einsum("shnm,wm->shnw", expo, member, precision=lax.Precision.HIGHEST)
    coef = cover / (frame_count[:, None] * jnp.where(cover > 0, window_sum, 1.0))
    spread_back = jnp.einsum("shnw,wm->shnm", coef, member, precision=lax.Precision.HIGHEST)
    attn_weight = (expo * spread_back).astype(jnp.bfloat16)
    mixed = (
        jnp.einsum("shnm,mshd->nshd", attn_weight, values_near, preferred_element_type=jnp.float32)
        .astype(jnp.bfloat16)
        .reshape(-1, chans)
    )
    projected = jnp.dot(mixed, out_weight, preferred_element_type=jnp.float32)
    output = resid_float.reshape(-1, chans) + projected + out_bias
    return output.astype(jnp.bfloat16).reshape(frames_dev, rows_dev, width, chans)


def solution(mesh):
    placed = (
        P(("dp", "frames"), "height", None, None),
        P("dp"),
        P(),
        P(),
        P("frames", "height"),
        P(),
        P(),
        P(),
        P(),
        P(),
        P(),
    )
    return jax.shard_map(
        on_device,
        mesh=mesh,
        in_specs=placed,
        out_specs=P(("dp", "frames"), "height", None, None),
        check_vma=False,
    )
```

profile of v0, /device:TPU:24, one launch (start us, length us, event | category | flops | bytes accessed | tf_op | source)
XLA Modules:
  0.0 188.2 jit_solution(935710017307930549)
XLA Ops:
  6.5 13.8 %all_gather.6 = bf16[360,640]{0,1:T(8,128)(2,1)S(1)} all-gather(bf16[360,80]{0,1:T(8,128)(2,1)} %param.15), channel_id=1, replica_groups=mesh['dp'=4,'frames'=16,'height'=8] {'height'}, dimensions={1}, use_global_device_ids=true | all-gather | bytes 518400 | tf_op jit(solution)/shard_map/all_gather | solution.py:72
  20.3 1.0 copy.46
  21.7 14.8 %psum.14 = f32[8,32]{1,0:T(8,128)S(1)} all-reduce(f32[8,32]{1,0:T(8,128)S(1)} %reduce_sum.61), channel_id=1, replica_groups=mesh['dp'=4,'frames'=16,'height'=8] {'height'}, use_global_device_ids=true, to_apply=%region_2.0 | all-reduce | flops 256 | bytes 2048 | tf_op jit(solution)/shard_map/psum | solution.py:64
  37.1 12.4 %psum.15 = f32[8,32]{1,0:T(8,128)S(1)} all-reduce(f32[8,32]{1,0:T(8,128)S(1)} %reduce_sum.64), channel_id=1, replica_groups=mesh['dp'=4,'frames'=16,'height'=8] {'height'}, use_global_device_ids=true, to_apply=%region_5.6 | all-reduce | flops 256 | bytes 2048 | tf_op jit(solution)/shard_map/psum | solution.py:66
  49.9 1.8 collective-permute-start
  51.7 1.3 collective-permute-start.1
  53.4 1.5 collective-permute-done.1
  55.3 0.7 slice_dynamic-update-slice_fusion.5
  55.9 0.7 constant_dynamic-update-slice_fusion.2
  56.6 0.7 slice_dynamic-update-slice_fusion.4
  57.4 0.7 slice_dynamic-update-slice_fusion.3
  58.1 0.8 constant_dynamic-update-slice_fusion.1
  58.9 0.8 slice_dynamic-update-slice_fusion.2
  59.6 0.7 slice_dynamic-update-slice_fusion.1
  60.3 0.7 constant_dynamic-update-slice_fusion
  61.0 0.8 slice_dynamic-update-slice_fusion
  61.8 59.0 %all-gather.2.cloned.1.call-done = bf16[5760,640]{1,0:T(8,128)(2,1)} async-done(((bf16[360,640]{1,0:T(8,128)(2,1)}), bf16[5760,640]{1,0:T(8,128)(2,1)}) %all-gather.2.cloned.1.call-update) | async-done | bytes 7372816 | tf_op jit(solution)/shard_map/all_gather | solution.py:85
  120.8 4.9 %fusion.21 = bf16[128,640]{1,0:T(8,128)(2,1)S(1)} fusion(bf16[128,5760]{1,0:T(8,128)(2,1)} %bitcast, bf16[5760,640]{1,0:T(8,128)(2,1)} %all-gather.2.cloned.1.call-done, f32[640]{0:T(1024)S(1)} %copy-done.6), kind=kOutput, calls=%fused_computation.20 | convolution fusion | flops 943882240 | bytes 9013760 | tf_op jit(solution)/shard_map/dot_general | solution.py:83
  126.2 0.6 convolution_convert_fusion
  126.8 2.7 %collective-permute-start.6 = (bf16[8,16,640]{2,1,0:T(8,128)(2,1)S(1)}, bf16[8,16,640]{2,1,0:T(8,128)(2,1)S(1)}, u32[]{:S(2)}, u32[]{:S(2)}) collective-permute-start(bf16[8,16,640]{2,1,0:T(8,128)(2,1)S(1)} %get-tuple-element.11), channel_id=1, source_target_pairs={{0,16},{8,24},{16,32},{24,40},{32,48},{40,56},{48,64},{56,72},{64,... | collective-permute-start | bytes 491528 | tf_op jit(solution)/shard_map/ppermute | solution.py:18
  129.5 4.9 %collective-permute-start.2 = (bf16[8,16,640]{2,1,0:T(8,128)(2,1)S(1)}, bf16[8,16,640]{2,1,0:T(8,128)(2,1)S(1)}, u32[]{:S(2)}, u32[]{:S(2)}) collective-permute-start(bf16[8,16,640]{2,1,0:T(8,128)(2,1)S(1)} %get-tuple-element.10), channel_id=1, source_target_pairs={{0,16},{8,24},{16,32},{24,40},{32,48},{40,56},{48,64},{56,72},{64,... | collective-permute-start | bytes 491528 | tf_op jit(solution)/shard_map/ppermute | solution.py:18
  134.6 3.8 %collective-permute-start.7 = (bf16[8,16,640]{2,1,0:T(8,128)(2,1)S(1)}, bf16[8,16,640]{2,1,0:T(8,128)(2,1)S(1)}, u32[]{:S(2)}, u32[]{:S(2)}) collective-permute-start(bf16[8,16,640]{2,1,0:T(8,128)(2,1)S(1)} %get-tuple-element.11), channel_id=1, source_target_pairs={{0,8},{8,16},{16,24},{24,32},{32,40},{40,48},{48,56},{56,64},{64,7... | collective-permute-start | bytes 491528 | tf_op jit(solution)/shard_map/ppermute | solution.py:18
  138.3 3.8 %collective-permute-start.3 = (bf16[8,16,640]{2,1,0:T(8,128)(2,1)S(1)}, bf16[8,16,640]{2,1,0:T(8,128)(2,1)S(1)}, u32[]{:S(2)}, u32[]{:S(2)}) collective-permute-start(bf16[8,16,640]{2,1,0:T(8,128)(2,1)S(1)} %get-tuple-element.10), channel_id=1, source_target_pairs={{0,8},{8,16},{16,24},{24,32},{32,40},{40,48},{48,56},{56,64},{64,7... | collective-permute-start | bytes 491528 | tf_op jit(solution)/shard_map/ppermute | solution.py:18
  142.1 1.3 collective-permute-start.4
  143.4 1.3 collective-permute-start.5
  144.8 1.3 collective-permute-start.8
  146.1 0.7 constant_dynamic-update-slice_fusion.7
  146.7 1.3 collective-permute-start.9
  148.1 0.7 constant_dynamic-update-slice_fusion.6
  148.7 0.7 constant_dynamic-update-slice_fusion.5
  149.5 0.9 copy-done.3
  150.4 0.9 collective-permute-done.4
  151.3 0.7 constant_dynamic-update-slice_fusion.4
  152.0 7.9 %collective-permute-done.5 = bf16[8,16,640]{2,1,0:T(8,128)(2,1)S(1)} collective-permute-done((bf16[8,16,640]{2,1,0:T(8,128)(2,1)S(1)}, bf16[8,16,640]{2,1,0:T(8,128)(2,1)S(1)}, u32[]{:S(2)}, u32[]{:S(2)}) %collective-permute-start.5) | collective-permute-done | bytes 163872 | tf_op jit(solution)/shard_map/ppermute | solution.py:18
  159.9 0.7 constant_dynamic-update-slice_fusion.3
  160.6 4.1 %reshape.144 = bf16[40,16,10,64]{3,2,1,0:T(8,128)(2,1)} reshape(bf16[40,16,640]{2,1,0:T(8,128)(2,1)} %constant_dynamic-update-slice_fusion.3) | data formatting | bytes 1638400 | tf_op jit(solution)/shard_map/reshape | solution.py:114
  164.6 0.7 constant_dynamic-update-slice_fusion.9
  165.3 2.7 %collective-permute-done.9 = bf16[8,16,640]{2,1,0:T(8,128)(2,1)S(1)} collective-permute-done((bf16[8,16,640]{2,1,0:T(8,128)(2,1)S(1)}, bf16[8,16,640]{2,1,0:T(8,128)(2,1)S(1)}, u32[]{:S(2)}, u32[]{:S(2)}) %collective-permute-start.9) | collective-permute-done | bytes 163872 | tf_op jit(solution)/shard_map/ppermute | solution.py:18
  168.0 0.7 constant_dynamic-update-slice_fusion.8
  168.7 4.1 %reshape.146 = bf16[40,16,10,64]{3,2,1,0:T(8,128)(2,1)} reshape(bf16[40,16,640]{2,1,0:T(8,128)(2,1)} %constant_dynamic-update-slice_fusion.8) | data formatting | bytes 1638400 | tf_op jit(solution)/shard_map/reshape | solution.py:111
  172.8 0.3 reshape.145
  173.1 3.0 %fusion.8 = f32[16,10,8,40]{3,2,1,0:T(8,128)S(1)} fusion(bf16[40,16,10,64]{3,2,1,0:T(8,128)(2,1)} %reshape.146, bf16[8,16,10,64]{3,2,1,0:T(8,128)(2,1)S(1)} %reshape.145), kind=kOutput, calls=%fused_computation.10 | convolution fusion | flops 6604800 | bytes 1187840 | tf_op jit(solution)/shard_map/nshd,mshd->shnm/dot_general | solution.py:125
  176.0 0.5 fusion.12
  176.6 0.5 fusion.16
  177.1 0.7 copy-done.2
  177.8 1.0 fusion.18
  178.9 0.3 reshape.149
  179.3 2.1 %fusion.22 = bf16[128,640]{1,0:T(8,128)(2,1)} fusion(bf16[128,640]{1,0:T(8,128)(2,1)S(1)} %reshape.149, bf16[640,640]{1,0:T(8,128)(2,1)} %param.20, f32[640]{0:T(1024)S(1)} %copy-done.9, bf16[128,640]{1,0:T(8,128)(2,1)S(1)} %bitcast.36), kind=kOutput, calls=%fused_computation.21 | convolution fusion | flops 105185280 | bytes 1313280 | tf_op jit(solution)/shard_map/dot_general | solution.py:143
  (60 shorter events, 2.7 us)
Async XLA Ops:
  6.5 119.7 %copy-start = (bf16[640,1920]{1,0:T(8,128)(2,1)S(1)}, bf16[640,1920]{1,0:T(8,128)(2,1)}, u32[]{:S(2)}) copy-start(bf16[640,1920]{1,0:T(8,128)(2,1)} %param.19) | copy-start | bytes 7372804
  6.5 14.8 %copy-start.1 = (bf16[8,1,16,640]{3,2,1,0:T(8,128)(2,1)S(1)}, bf16[8,1,16,640]{3,2,1,0:T(8,128)(2,1)}, u32[]{:S(2)}) copy-start(bf16[8,1,16,640]{3,2,1,0:T(8,128)(2,1)} %param.11) | copy-start | bytes 491524
  6.5 114.2 %all-gather.2.cloned.1.call-start = ((), (), s32[]{:S(2)}) async-start(), calls=%async_computation | async-start | bytes 7833600 | tf_op jit(solution)/shard_map/all_gather | solution.py:85
  20.3 29.4 %copy-start.4 = (f32[640]{0:T(1024)S(1)}, f32[640]{0:T(1024)}, u32[]{:S(2)}) copy-start(f32[640]{0:T(1024)} %param.14) | copy-start | bytes 7684
  20.3 29.4 %copy-start.5 = (f32[640]{0:T(1024)S(1)}, f32[640]{0:T(1024)}, u32[]{:S(2)}) copy-start(f32[640]{0:T(1024)} %param.13) | copy-start | bytes 7684
  20.3 32.7 %copy-start.10 = (s32[28]{0:T(128)S(1)}, s32[28]{0:T(128)}, u32[]{:S(2)}) copy-start(s32[28]{0:T(128)} %param.12) | copy-start | bytes 340
  49.9 3.5 %collective-permute-start = (bf16[8,1,16,640]{3,2,1,0:T(8,128)(2,1)S(1)}, bf16[8,1,16,640]{3,2,1,0:T(8,128)(2,1)S(1)}, u32[]{:S(2)}, u32[]{:S(2)}) collective-permute-start(bf16[8,1,16,640]{3,2,1,0:T(8,128)(2,1)S(1)} %fusion.38), channel_id=1, source_target_pairs={{0,1},{1,2},{2,3},{3,4},{4,5},{5,6},{6,7},{8,9},{9,10},{10,11},{11... | collective-permute-start | bytes 491528 | tf_op jit(solution)/shard_map/ppermute | solution.py:29
  51.7 3.3 %collective-permute-start.1 = (bf16[8,1,16,640]{3,2,1,0:T(8,128)(2,1)S(1)}, bf16[8,1,16,640]{3,2,1,0:T(8,128)(2,1)S(1)}, u32[]{:S(2)}, u32[]{:S(2)}) collective-permute-start(bf16[8,1,16,640]{3,2,1,0:T(8,128)(2,1)S(1)} %fusion.38), channel_id=1, source_target_pairs={{1,0},{2,1},{3,2},{4,3},{5,4},{6,5},{7,6},{9,8},{10,9},{11,10},{12... | collective-permute-start | bytes 491528 | tf_op jit(solution)/shard_map/ppermute | solution.py:31
  55.2 65.5 %copy-start.6 = (f32[640]{0:T(1024)S(1)}, f32[640]{0:T(1024)}, u32[]{:S(2)}) copy-start(f32[640]{0:T(1024)} %param.16) | copy-start | bytes 7684
  120.8 5.3 %copy-start.7 = (f32[640]{0:T(1024)S(1)}, f32[640]{0:T(1024)}, u32[]{:S(2)}) copy-start(f32[640]{0:T(1024)} %param.18) | copy-start | bytes 7684
  120.8 5.3 %copy-start.8 = (f32[640]{0:T(1024)S(1)}, f32[640]{0:T(1024)}, u32[]{:S(2)}) copy-start(f32[640]{0:T(1024)} %param.17) | copy-start | bytes 7684
  126.8 16.6 %collective-permute-start.6 = (bf16[8,16,640]{2,1,0:T(8,128)(2,1)S(1)}, bf16[8,16,640]{2,1,0:T(8,128)(2,1)S(1)}, u32[]{:S(2)}, u32[]{:S(2)}) collective-permute-start(bf16[8,16,640]{2,1,0:T(8,128)(2,1)S(1)} %get-tuple-element.11), channel_id=1, source_target_pairs={{0,16},{8,24},{16,32},{24,40},{32,48},{40,56},{48,64},{56,72},{64,... | collective-permute-start | bytes 491528 | tf_op jit(solution)/shard_map/ppermute | solution.py:18
  129.5 15.2 %collective-permute-start.2 = (bf16[8,16,640]{2,1,0:T(8,128)(2,1)S(1)}, bf16[8,16,640]{2,1,0:T(8,128)(2,1)S(1)}, u32[]{:S(2)}, u32[]{:S(2)}) collective-permute-start(bf16[8,16,640]{2,1,0:T(8,128)(2,1)S(1)} %get-tuple-element.10), channel_id=1, source_target_pairs={{0,16},{8,24},{16,32},{24,40},{32,48},{40,56},{48,64},{56,72},{64,... | collective-permute-start | bytes 491528 | tf_op jit(solution)/shard_map/ppermute | solution.py:18
  134.6 12.2 %collective-permute-start.7 = (bf16[8,16,640]{2,1,0:T(8,128)(2,1)S(1)}, bf16[8,16,640]{2,1,0:T(8,128)(2,1)S(1)}, u32[]{:S(2)}, u32[]{:S(2)}) collective-permute-start(bf16[8,16,640]{2,1,0:T(8,128)(2,1)S(1)} %get-tuple-element.11), channel_id=1, source_target_pairs={{0,8},{8,16},{16,24},{24,32},{32,40},{40,48},{48,56},{56,64},{64,7... | collective-permute-start | bytes 491528 | tf_op jit(solution)/shard_map/ppermute | solution.py:18
  138.3 9.7 %collective-permute-start.3 = (bf16[8,16,640]{2,1,0:T(8,128)(2,1)S(1)}, bf16[8,16,640]{2,1,0:T(8,128)(2,1)S(1)}, u32[]{:S(2)}, u32[]{:S(2)}) collective-permute-start(bf16[8,16,640]{2,1,0:T(8,128)(2,1)S(1)} %get-tuple-element.10), channel_id=1, source_target_pairs={{0,8},{8,16},{16,24},{24,32},{32,40},{40,48},{48,56},{56,64},{64,7... | collective-permute-start | bytes 491528 | tf_op jit(solution)/shard_map/ppermute | solution.py:18
  142.1 9.2 %collective-permute-start.4 = (bf16[8,16,640]{2,1,0:T(8,128)(2,1)S(1)}, bf16[8,16,640]{2,1,0:T(8,128)(2,1)S(1)}, u32[]{:S(2)}, u32[]{:S(2)}) collective-permute-start(bf16[8,16,640]{2,1,0:T(8,128)(2,1)S(1)} %get-tuple-element.10), channel_id=1, source_target_pairs={{8,0},{16,8},{24,16},{32,24},{40,32},{48,40},{56,48},{64,56},{72,6... | collective-permute-start | bytes 491528 | tf_op jit(solution)/shard_map/ppermute | solution.py:18
  143.4 16.5 %collective-permute-start.5 = (bf16[8,16,640]{2,1,0:T(8,128)(2,1)S(1)}, bf16[8,16,640]{2,1,0:T(8,128)(2,1)S(1)}, u32[]{:S(2)}, u32[]{:S(2)}) collective-permute-start(bf16[8,16,640]{2,1,0:T(8,128)(2,1)S(1)} %get-tuple-element.10), channel_id=1, source_target_pairs={{16,0},{24,8},{32,16},{40,24},{48,32},{56,40},{64,48},{72,56},{80,... | collective-permute-start | bytes 491528 | tf_op jit(solution)/shard_map/ppermute | solution.py:18
  144.8 19.9 %collective-permute-start.8 = (bf16[8,16,640]{2,1,0:T(8,128)(2,1)S(1)}, bf16[8,16,640]{2,1,0:T(8,128)(2,1)S(1)}, u32[]{:S(2)}, u32[]{:S(2)}) collective-permute-start(bf16[8,16,640]{2,1,0:T(8,128)(2,1)S(1)} %get-tuple-element.11), channel_id=1, source_target_pairs={{8,0},{16,8},{24,16},{32,24},{40,32},{48,40},{56,48},{64,56},{72,6... | collective-permute-start | bytes 491528 | tf_op jit(solution)/shard_map/ppermute | solution.py:18
  146.7 21.2 %collective-permute-start.9 = (bf16[8,16,640]{2,1,0:T(8,128)(2,1)S(1)}, bf16[8,16,640]{2,1,0:T(8,128)(2,1)S(1)}, u32[]{:S(2)}, u32[]{:S(2)}) collective-permute-start(bf16[8,16,640]{2,1,0:T(8,128)(2,1)S(1)} %get-tuple-element.11), channel_id=1, source_target_pairs={{16,0},{24,8},{32,16},{40,24},{48,32},{56,40},{64,48},{72,56},{80,... | collective-permute-start | bytes 491528 | tf_op jit(solution)/shard_map/ppermute | solution.py:18
  149.5 0.9 copy-start.3
  176.0 1.8 copy-start.2
  177.8 1.5 copy-start.9
Sparse Core Ops, SparseCore 0:
  21.5 99.2 all-gather.1
where the time goes:
time: 189 us; the launch traced here: 188 us
  waiting for transfers between devices  72 us (38%)
  blocking collectives  41 us (22%)
  starting transfers between devices  23.4 us (12%)
  local copies, waits for them, and re-layouts  23 us (12%)
  between operations  13.8 us (7%)
  matrix products  12.6 us (7%)
  other arithmetic  2.48 us (1%)
    all_gather x1, waiting for transfers between devices, on_device(): lax.all_gather(columns, 'frames', axis=0, tiled=True)  59 us
    ppermute x8, starting transfers between devices, passed_along(): return lax.ppermute(shard, axis, pairs)  20.3 us
    psum x1, blocking collectives, on_device(): mean = lax.psum(jnp.sum(grouped, axis=(1, 2, 4)), 'height') / cell_count  14.8 us
    all_gather x1, blocking collectives, on_device(): columns = lax.all_gather(conv_weight, 'height', axis=1, tiled=True)  13.8 us
    psum x1, blocking collectives, on_device(): lax.psum(jnp.sum(centred * centred, axis=(1, 2, 4)), 'height') / cell_count  12.4 us
    ppermute x8, waiting for transfers between devices, passed_along(): return lax.ppermute(shard, axis, pairs)  11.5 us
    unnamed x36, local copies, waits for them, and re-layouts  10.1 us
    dot_general x1, matrix products, on_device(): jnp.dot(patches, lax.all_gather(columns, 'frames', axis=0, tiled=True), p...  4.9 us
  transfers between devices with their start and end apart: 11, of which 5 were waited for; matrix products, arithmetic and copies ran while one was open for 9% of the time, Pallas kernels for 0%

commit v1 on v0

v1 whole, which is shorter than its diff:
```python
import jax
import jax.numpy as jnp
from jax import lax
from jax.experimental import pallas as pl
from jax.experimental.pallas import tpu as pltpu
from jax.sharding import PartitionSpec as P

HEADS = 10
GROUPS = 32
WIN = 16
HEAD_DIM = 64
LANES = 128

EPSILON = 1e-05
F32 = jnp.float32
BF16 = jnp.bfloat16
VMEM = pl.BlockSpec(memory_space=pltpu.VMEM)
SMEM = pl.BlockSpec(memory_space=pltpu.SMEM)
NT = (((1,), (1,)), ((), ()))


def dot(a, b):
    return jnp.dot(a, b, preferred_element_type=F32)


def exact_dot(a, b, dims=(((1,), (0,)), ((), ()))):
    return lax.dot_general(a, b, dims, precision=lax.Precision.HIGHEST, preferred_element_type=F32)


def iota(shape, dim):
    return lax.broadcasted_iota(jnp.int32, shape, dim)


def conv_kernel(
    place_ref, own_ref, left_ref, right_ref, far_ref, weight_ref, other_ref, gain_ref, bias_ref, cbias_ref,
    out_ref, cells, padded, shifted,
):
    frames, rows, width, chans = cells.shape
    chips = rows // 2
    outs = out_ref.shape[-1]
    chip, core = place_ref[0], place_ref[1]
    for ref, back in ((own_ref, 0), (left_ref, 1), (far_ref, 2), (right_ref, 3)):
        row = 2 * lax.rem(chip + chips - back, chips)
        for f in range(frames):
            cells[f, row + core] = ref[0, f]
            cells[f, row + 1 - core] = ref[1, f]
    groups = (iota((chans, LANES), 0).astype(F32) + 0.5) * (GROUPS / chans)
    groups = (jnp.floor(groups) == iota((chans, LANES), 1).astype(F32)).astype(F32)
    count = rows * width * (chans // GROUPS)

    def group_mean(sums):
        per_group = exact_dot(jnp.concatenate(sums + sums, axis=0), groups) / count
        return exact_dot(per_group, groups, NT)

    def frame(f):
        return cells[f].reshape(rows * width, chans).astype(F32)

    mean = group_mean([jnp.sum(frame(f), axis=0, keepdims=True) for f in range(frames)])
    sums = []
    for f in range(frames):
        centred = frame(f) - mean[f : f + 1]
        sums.append(jnp.sum(centred * centred, axis=0, keepdims=True))
    inverse = lax.rsqrt(group_mean(sums) + EPSILON)
    gain, bias = gain_ref[...], bias_ref[...]
    edge = jnp.zeros((width, chans), BF16)
    for f in range(frames):
        padded[f, 0] = edge
        padded[f, rows + 1] = edge
        for r in range(rows):
            normed = (cells[f, r].astype(F32) - mean[f : f + 1]) * inverse[f : f + 1] * gain + bias
            padded[f, r + 1] = (normed / (1.0 + jnp.exp(-normed))).astype(BF16)
    flat = frames * rows * width
    column = lax.rem(iota((flat, 1), 0), width)
    total = None
    for col in (1, 0, 2):
        part = None
        for row in range(3):
            tap = (3 * row + col) * chans
            term = dot(
                padded[:, row : row + rows].reshape(flat, chans),
                jnp.concatenate(
                    [weight_ref[tap : tap + chans], other_ref[tap : tap + chans]], axis=1
                ),
            )
            part = term if part is None else part + term
        if col == 1:
            total = part + cbias_ref[...]
        else:
            shifted[8 : 8 + flat] = part
            moved = shifted[6 + 2 - 1 : 6 + 2 - 1 + flat] if col == 0 else shifted[9 : 9 + flat]
            total = total + jnp.where(column == (0 if col == 0 else width - 1), 0.0, moved)
    result = total.astype(BF16).reshape(frames, rows, width, outs)
    for r in range(rows):
        for f in range(frames):
            out_ref[r, f * width : (f + 1) * width] = result[f, r]


def swap_matrix(frames, width, back):
    cells = frames * width
    near, far = iota((cells, cells), 1 if back else 0), iota((cells, cells), 0 if back else 1)
    same = (lax.div(near, frames) == lax.rem(far, width)) & (
        lax.rem(near, frames) == lax.div(far, width)
    )
    return same.astype(F32).astype(BF16)


def norm_kernel(part_ref, video_ref, gain_ref, bias_ref, resid_ref, norm_ref):
    cells, chans = video_ref.shape
    half = part_ref.shape[2] // 2
    parts = part_ref.shape[0]
    top = [part_ref[s].astype(F32) for s in range(0, parts, 2)]
    low = []
    for s in range(1, parts, 2):
        piece = part_ref[s].astype(F32)
        low += [piece[:, half:], piece[:, :half]]
    conv_out = jnp.concatenate(
        [jnp.concatenate(top, axis=1), jnp.concatenate(low, axis=1)], axis=0
    )
    resid = (video_ref[...].astype(F32) + conv_out).astype(BF16)
    resid_ref[...] = resid
    floats = resid.astype(F32)
    deviation = floats - jnp.mean(floats, axis=-1, keepdims=True)
    spread = jnp.mean(deviation * deviation, axis=-1, keepdims=True)
    norm = (deviation * lax.rsqrt(spread + EPSILON) * gain_ref[...] + bias_ref[...]).astype(BF16)
    norm_ref[...] = dot(swap_matrix(8, cells // 8, False), norm).astype(BF16)


def attend_kernel(
    b0_ref, b1_ref, b2_ref, b3_ref, b4_ref, resid_ref, qkv_ref, out_w_ref, out_b_ref,
    member_ref, cover_ref,
    out_ref, keys, values, query, scores, mixed,
):
    blocks, width, frames, chans = keys.shape
    near = blocks * frames
    stack = HEADS * frames

    def by_cell(product):
        return product.astype(BF16).astype(F32).reshape(width, frames, chans)

    query[...] = by_cell(dot(b2_ref[...], qkv_ref[:, :chans]))
    for b, ref in enumerate((b0_ref, b1_ref, b2_ref, b3_ref, b4_ref)):
        keys[b] = by_cell(dot(ref[...], qkv_ref[:, chans : 2 * chans]))
        values[b] = by_cell(dot(ref[...], qkv_ref[:, 2 * chans :]))
    head_of = lax.div(iota((HEADS, 1, chans), 2), HEAD_DIM) == iota((HEADS, 1, chans), 0)
    own = head_of.astype(F32)
    for c in range(width):
        spread = (query[c][None] * own).reshape(stack, chans).astype(BF16)
        key = keys[:, c].reshape(near, chans).astype(BF16)
        scores[c] = lax.dot_general(spread, key, NT, preferred_element_type=F32)
    flat = width * stack
    expo = jnp.exp(scores[...].reshape(flat, near) * HEAD_DIM ** (-0.5))
    member = member_ref[...].astype(BF16)

    def split_dot(a, dims):
        high = a.astype(BF16)
        rest = (a - high.astype(F32)).astype(BF16)
        return lax.dot_general(high, member, dims, preferred_element_type=F32) + lax.dot_general(
            rest, member, dims, preferred_element_type=F32
        )

    sums = split_dot(expo, NT).reshape(width * HEADS, frames, LANES)
    cover = cover_ref[...][None]
    frame_count = jnp.sum(cover, axis=2, keepdims=True)
    coef = (cover / (frame_count * jnp.where(cover > 0, sums, 1.0))).reshape(flat, LANES)
    back = split_dot(coef, (((1,), (0,)), ((), ())))
    scores[...] = (expo * back).reshape(width, stack, near)
    for c in range(width):
        value = values[:, c].reshape(near, chans).astype(BF16)
        product = dot(scores[c].astype(BF16), value).reshape(HEADS, frames, chans)
        mixed[c] = jnp.sum(jnp.where(head_of, product, 0.0), axis=0)
    joined = mixed[...].reshape(width * frames, chans).astype(BF16)
    joined = dot(swap_matrix(frames, width, True), joined).astype(BF16)
    projected = dot(joined, out_w_ref[...])
    out_ref[...] = (resid_ref[...].astype(F32) + projected + out_b_ref[...]).astype(BF16)


def passed(shard, axis, by):
    size = lax.axis_size(axis)
    pairs = [(i, i + by) for i in range(size) if 0 <= i + by < size]
    return lax.ppermute(shard, axis, pairs)


def on_device(
    video, window_gaps, gn_gain, gn_bias, conv_weight, conv_bias,
    ln_gain, ln_bias, qkv_weight, out_weight, out_bias,
):
    frames, _, width, chans = video.shape
    bands = lax.axis_size("height")
    place = lax.axis_index("height")
    core = place % 2
    half = frames // 2
    cols = conv_weight.shape[1]
    swap = [(i, i ^ 1) for i in range(bands)]

    def ring(shard, by):
        return lax.ppermute(shard, "height", [(i, (i + 2 * by) % bands) for i in range(bands)])

    row = video.reshape(frames, width, chans)
    kept = lax.dynamic_slice_in_dim(row, half * core, half, axis=0)
    sent = lax.dynamic_slice_in_dim(row, half * (1 - core), half, axis=0)
    pair = jnp.stack([kept, lax.ppermute(sent, "height", swap)])
    left, right, far = ring(pair, 1), ring(pair, -1), ring(pair, 2)
    weight = lax.all_gather(conv_weight, "frames", axis=0, tiled=True)
    other = lax.ppermute(weight, "height", swap)
    by_band = conv_bias.reshape(bands, cols)
    cbias = jnp.concatenate([by_band[place], by_band[place ^ 1]])[None]
    where = jnp.stack([place // 2, core]).astype(jnp.int32)
    parts = pl.pallas_call(
        conv_kernel,
        out_shape=jax.ShapeDtypeStruct((bands, half * width, 2 * cols), BF16),
        in_specs=[SMEM] + [VMEM] * 9,
        out_specs=VMEM,
        scratch_shapes=[
            pltpu.VMEM((half, bands, width, chans), BF16),
            pltpu.VMEM((half, bands + 2, width, chans), BF16),
            pltpu.VMEM((half * bands * width + 16, 2 * cols), F32),
        ],
    )(where, pair, left, right, far, weight, other, gn_gain[None], gn_bias[None], cbias)
    parts = lax.all_to_all(parts, "height", 0, 0, tiled=True)
    cells = frames * width
    resid, norm = pl.pallas_call(
        norm_kernel,
        out_shape=[jax.ShapeDtypeStruct((cells, chans), BF16)] * 2,
        in_specs=[VMEM] * 4,
        out_specs=[VMEM] * 2,
    )(parts, row.reshape(cells, chans), ln_gain[None], ln_bias[None])
    starts = jnp.concatenate([jnp.zeros((1,), jnp.int32), jnp.cumsum(window_gaps)])
    starts = jnp.pad(starts, (0, LANES - starts.shape[0]), constant_values=-(1 << 20))
    near_ids = (lax.axis_index("frames") - 2) * frames + jnp.arange(5 * frames, dtype=jnp.int32)
    inside = (near_ids[None, :] >= starts[:, None]) & (near_ids[None, :] < starts[:, None] + WIN)
    member = inside.astype(F32)
    cover = member[:, 2 * frames : 3 * frames].T
    near = [passed(norm, "frames", by) for by in (2, 1)] + [norm]
    near += [passed(norm, "frames", by) for by in (-1, -2)]
    out = pl.pallas_call(
        attend_kernel,
        out_shape=jax.ShapeDtypeStruct((cells, chans), BF16),
        in_specs=[VMEM] * 11,
        out_specs=VMEM,
        scratch_shapes=[
            pltpu.VMEM((5, width, frames, chans), F32),
            pltpu.VMEM((5, width, frames, chans), F32),
            pltpu.VMEM((width, frames, chans), F32),
            pltpu.VMEM((width, HEADS * frames, 5 * frames), F32),
            pltpu.VMEM((width, frames, chans), F32),
        ],
    )(*near, resid, qkv_weight, out_weight, out_bias[None], member, cover)
    return out.reshape(frames, 1, width, chans)


def solution(mesh):
    placed = (
        P(("dp", "frames"), "height", None, None),
        P("dp"),
        P(),
        P(),
        P("frames", "height"),
        P(),
        P(),
        P(),
        P(),
        P(),
        P(),
    )
    return jax.shard_map(
        on_device,
        mesh=mesh,
        in_specs=placed,
        out_specs=P(("dp", "frames"), "height", None, None),
        check_vma=False,
    )
```

time: 189 us -> 117 us (0.62)
  waiting for transfers between devices: 72 us -> 19.6 us
  Pallas kernels: 0 us -> 16.1 us
  between operations: 13.8 us -> 0.3 us
  matrix products: 12.6 us -> 0 us
  local copies, waits for them, and re-layouts: 23 us -> 11.6 us
    all_gather x1 -> x0, waiting for transfers between devices: 59 us -> none  [on_device(): lax.all_gather(columns, 'frames', axis=0, tiled=True)]
    all_gather x1, blocking collectives: 13.8 us -> 41.3 us  [on_device(): weight = lax.all_gather(conv_weight, 'frames', axis=0, tiled=True)]
    psum x2 -> x0, blocking collectives: 27.2 us -> none  [the longest x1 14.8 us: on_device(): mean = lax.psum(jnp.sum(grouped, axis=(1, 2, 4)), 'height') / cell_count]
    pallas_call x0 -> x3, Pallas kernels: none -> 16.1 us  [the longest x1 7 us: on_device(): pl.pallas_call(attend_kernel, out_shape=jax.ShapeDtypeStruct((cells, chan...]
    dot_general x7 -> x0, matrix products: 12.6 us -> none  [the longest x1 4.9 us: on_device(): jnp.dot(patches, lax.all_gather(columns, 'frames', axis=0, tiled=True), p...]
    reshape x4 -> x1, local copies, waits for them, and re-layouts: 8.78 us -> 0.07 us  [on_device(): by_band = conv_bias.reshape(bands, cols)]
    all_to_all x0 -> x1, waiting for transfers between devices: none -> 6.04 us  [on_device(): parts = lax.all_to_all(parts, 'height', 0, 0, tiled=True)]
    unnamed x36 -> x37, local copies, waits for them, and re-layouts: 10.1 us -> 4.13 us
  transfers between devices with their start and end apart: 11 -> 10, of which waited for: 5 -> 6; matrix products, arithmetic and copies ran while one was open for 9% -> 8% of each run, Pallas kernels for 0% -> 0%
where the time goes in v1:
time: 117 us
  blocking collectives  41.3 us (35%)
  starting transfers between devices  25.2 us (22%)
  waiting for transfers between devices  19.6 us (17%)
  Pallas kernels  16.1 us (14%)
  local copies, waits for them, and re-layouts  11.6 us (10%)
  other arithmetic  2.51 us (2%)
    all_gather x1, blocking collectives, on_device(): weight = lax.all_gather(conv_weight, 'frames', axis=0, tiled=True)  41.3 us
    ppermute x4, waiting for transfers between devices, passed(): return lax.ppermute(shard, axis, pairs)  12.5 us
    ppermute x3, starting transfers between devices, ring(): lax.ppermute(shard, 'height', [(i, (i + 2 * by) % bands) for i in range(b...  10.8 us
    pallas_call x1, Pallas kernels, on_device(): pl.pallas_call(attend_kernel, out_shape=jax.ShapeDtypeStruct((cells, chan...  7 us
    pallas_call x1, Pallas kernels, on_device(): pl.pallas_call(conv_kernel, out_shape=jax.ShapeDtypeStruct((bands, half *...  6.89 us
    ppermute x4, starting transfers between devices, passed(): return lax.ppermute(shard, axis, pairs)  6.74 us
    all_to_all x1, waiting for transfers between devices, on_device(): parts = lax.all_to_all(parts, 'height', 0, 0, tiled=True)  6.04 us
    unnamed x37, local copies, waits for them, and re-layouts  4.13 us
  transfers between devices with their start and end apart: 10, of which 6 were waited for; matrix products, arithmetic and copies ran while one was open for 8% of the time, Pallas kernels for 0%

profile of v1, /device:TPU:24, one launch (start us, length us, event | category | flops | bytes accessed | tf_op | source)
XLA Modules:
  0.0 116.7 jit_solution(10396194723165989310)
XLA Ops:
  0.0 41.3 %all-gather = bf16[16,360,80]{1,2,0:T(8,128)(2,1)S(1)} all-gather(bf16[1,360,80]{1,2,0:T(8,128)(2,1)} %bitcast.25), channel_id=1, replica_groups=mesh['dp'=4,'frames'=16,'height'=8] {'frames'}, dimensions={0}, use_global_device_ids=true | all-gather | bytes 979200 | tf_op jit(solution)/shard_map/all_gather | solution.py:203
  41.3 0.8 copy.20
  42.2 0.0 copy-start.3
  42.2 0.0 copy-start.12
  42.2 0.0 copy-start.13
  42.3 1.4 %copy.21 = bf16[5760,80]{0,1:T(8,128)(2,1)S(1)} copy(bf16[5760,80]{1,0:T(8,128)(2,1)S(1)} %bitcast.21) | data formatting | bytes 1843200
  43.7 1.9 %collective-permute-start.4 = (bf16[5760,80]{0,1:T(8,128)(2,1)S(1)}, bf16[5760,80]{0,1:T(8,128)(2,1)S(1)}, u32[]{:S(2)}, u32[]{:S(2)}) collective-permute-start(bf16[5760,80]{0,1:T(8,128)(2,1)S(1)} %copy.21), channel_id=1, source_target_pairs={{0,1},{1,0},{2,3},{3,2},{4,5},{5,4},{6,7},{7,6},{8,9},{9,8},{10,11... | collective-permute-start | bytes 2764808 | tf_op jit(solution)/shard_map/ppermute | solution.py:204
  45.6 0.7 dynamic-slice_bitcast_fusion.1
  46.3 2.4 %collective-permute-start = (bf16[4,16,640]{2,1,0:T(8,128)(2,1)}, bf16[4,16,640]{2,1,0:T(8,128)(2,1)S(1)}, u32[]{:S(2)}, u32[]{:S(2)}) collective-permute-start(bf16[4,16,640]{2,1,0:T(8,128)(2,1)} %get-tuple-element.10), channel_id=1, source_target_pairs={{0,1},{1,0},{2,3},{3,2},{4,5},{5,4},{6,7},{7,6},{8,9},{9,8},{10,11... | collective-permute-start | bytes 245768 | tf_op jit(solution)/shard_map/ppermute | solution.py:201
  48.7 0.1 reshape.43
  48.8 0.1 copy.23
  48.9 0.1 reduce-window.9
  49.0 0.1 reduce
  49.1 0.1 pad_add_fusion.1
  49.2 0.6 collective-permute-done
  49.8 0.6 copy-done.10
  50.5 0.9 pad_maximum_fusion.own_ref
  51.4 3.4 %collective-permute-start.1 = (bf16[2,4,16,640]{3,2,1,0:T(8,128)(2,1)S(1)}, bf16[2,4,16,640]{3,2,1,0:T(8,128)(2,1)}, u32[]{:S(2)}, u32[]{:S(2)}) collective-permute-start(bf16[2,4,16,640]{3,2,1,0:T(8,128)(2,1)S(1)} %pad_maximum_fusion.own_ref), channel_id=1, source_target_pairs={{0,2},{1,3},{2,4},{3,5},{4,6},{5,7},{6,0},{7,1},{8,10},{9,11},{10,... | collective-permute-start | bytes 491528 | tf_op jit(solution)/shard_map/ppermute | solution.py:196
  54.8 3.7 %collective-permute-start.2 = (bf16[2,4,16,640]{3,2,1,0:T(8,128)(2,1)S(1)}, bf16[2,4,16,640]{3,2,1,0:T(8,128)(2,1)S(1)}, u32[]{:S(2)}, u32[]{:S(2)}) collective-permute-start(bf16[2,4,16,640]{3,2,1,0:T(8,128)(2,1)S(1)} %pad_maximum_fusion.own_ref), channel_id=1, source_target_pairs={{0,6},{1,7},{2,0},{3,1},{4,2},{5,3},{6,4},{7,5},{8,14},{9,15},{10,... | collective-permute-start | bytes 491528 | tf_op jit(solution)/shard_map/ppermute | solution.py:196
  58.5 3.7 %collective-permute-start.3 = (bf16[2,4,16,640]{3,2,1,0:T(8,128)(2,1)S(1)}, bf16[2,4,16,640]{3,2,1,0:T(8,128)(2,1)S(1)}, u32[]{:S(2)}, u32[]{:S(2)}) collective-permute-start(bf16[2,4,16,640]{3,2,1,0:T(8,128)(2,1)S(1)} %pad_maximum_fusion.own_ref), channel_id=1, source_target_pairs={{0,4},{1,5},{2,6},{3,7},{4,0},{5,1},{6,2},{7,3},{8,12},{9,13},{10,... | collective-permute-start | bytes 491528 | tf_op jit(solution)/shard_map/ppermute | solution.py:196
  62.2 0.6 pad_add_fusion.place_ref
  62.8 0.6 broadcast_in_dim.22.gain_ref
  63.4 0.6 broadcast_in_dim.23.bias_ref
  64.0 0.6 broadcast_in_dim.25.gain_ref
  64.6 0.6 broadcast_in_dim.26.bias_ref
  65.2 0.7 pad_maximum_fusion.1
  65.8 1.6 %copy.22.other_ref = bf16[5760,80]{1,0:T(8,128)(2,1)} copy(bf16[5760,80]{0,1:T(8,128)(2,1)S(1)} %collective-permute-done.4) | data formatting | bytes 1843200 | tf_op jit(solution)/shard_map/ppermute | solution.py:204
  67.4 0.4 collective-permute-done.3.far_ref
  67.8 0.2 copy-done.4
  68.1 0.4 copy-done.6
  68.5 6.9 %shard_map.109 = bf16[8,64,160]{2,1,0:T(8,128)(2,1)} custom-call(s32[2]{0:T(128)} %pad_add_fusion.place_ref, bf16[2,4,16,640]{3,2,1,0:T(8,128)(2,1)} %copy-done.2, bf16[2,4,16,640]{3,2,1,0:T(8,128)(2,1)} %collective-permute-done.1.left_ref, bf16[2,4,16,640]{3,2,1,0:T(8,128)(2,1)} %copy-done.4, bf16[2,4,16,640]{3,2,1,0:T(8,128)(2,1)} %copy-done.6, ...), custom_call_target="tpu_custom_call" | custom-call | tf_op jit(solution)/shard_map/pallas_call | solution.py:208
  75.4 3.4 %all-to-all-start = ((bf16[8,64,160]{2,1,0:T(8,128)(2,1)}), bf16[8,64,160]{2,1,0:T(8,128)(2,1)S(1)}, u32[]{:S(2)}, u32[]{:S(2)}) async-start(bf16[8,64,160]{2,1,0:T(8,128)(2,1)} %shard_map.109), calls=%async_computation | async-start | bytes 524288 | tf_op jit(solution)/shard_map/all_to_all | solution.py:219
  78.8 0.1 and_convert_fusion
  78.9 0.7 copy.24.member_ref
  79.6 0.6 broadcast_in_dim.27.out_b_ref
  80.2 6.0 %all-to-all-done.part_ref = bf16[8,64,160]{2,1,0:T(8,128)(2,1)S(1)} async-done(((bf16[8,64,160]{2,1,0:T(8,128)(2,1)}), bf16[8,64,160]{2,1,0:T(8,128)(2,1)S(1)}, u32[]{:S(2)}, u32[]{:S(2)}) %all-to-all-start) | async-done | bytes 163872 | tf_op jit(solution)/shard_map/all_to_all | solution.py:219
  86.2 0.7 copy-done.1
  86.9 2.2 %shard_map.110 = (bf16[128,640]{1,0:T(8,128)(2,1)}, bf16[128,640]{1,0:T(8,128)(2,1)}) custom-call(bf16[8,64,160]{2,1,0:T(8,128)(2,1)} %copy-done.1, bf16[128,640]{1,0:T(8,128)(2,1)} %bitcast.23, f32[1,640]{1,0:T(1,128)} %broadcast_in_dim.25.gain_ref, f32[1,640]{1,0:T(1,128)} %broadcast_in_dim.26.bias_ref), custom_call_target="tpu_custom_call" | custom-call | tf_op jit(solution)/shard_map/pallas_call | solution.py:221
  89.1 2.2 %collective-permute-start.5 = (bf16[128,640]{1,0:T(8,128)(2,1)}, bf16[128,640]{1,0:T(8,128)(2,1)S(1)}, u32[]{:S(2)}, u32[]{:S(2)}) collective-permute-start(bf16[128,640]{1,0:T(8,128)(2,1)} %get-tuple-element.7.b2_ref), channel_id=1, source_target_pairs={{0,16},{8,24},{16,32},{24,40},{32,48},{40,56},{48,64},{56,72},{64,... | collective-permute-start | bytes 491528 | tf_op jit(solution)/shard_map/ppermute | solution.py:180
  91.3 2.0 %collective-permute-start.6 = (bf16[128,640]{1,0:T(8,128)(2,1)}, bf16[128,640]{1,0:T(8,128)(2,1)S(1)}, u32[]{:S(2)}, u32[]{:S(2)}) collective-permute-start(bf16[128,640]{1,0:T(8,128)(2,1)} %get-tuple-element.7.b2_ref), channel_id=1, source_target_pairs={{0,8},{8,16},{16,24},{24,32},{32,40},{40,48},{48,56},{56,64},{64,7... | collective-permute-start | bytes 491528 | tf_op jit(solution)/shard_map/ppermute | solution.py:180
  93.3 1.3 %collective-permute-start.7 = (bf16[128,640]{1,0:T(8,128)(2,1)}, bf16[128,640]{1,0:T(8,128)(2,1)S(1)}, u32[]{:S(2)}, u32[]{:S(2)}) collective-permute-start(bf16[128,640]{1,0:T(8,128)(2,1)} %get-tuple-element.7.b2_ref), channel_id=1, source_target_pairs={{8,0},{16,8},{24,16},{32,24},{40,32},{48,40},{56,48},{64,56},{72,6... | collective-permute-start | bytes 491528 | tf_op jit(solution)/shard_map/ppermute | solution.py:180
  94.6 1.3 %collective-permute-start.8 = (bf16[128,640]{1,0:T(8,128)(2,1)}, bf16[128,640]{1,0:T(8,128)(2,1)S(1)}, u32[]{:S(2)}, u32[]{:S(2)}) collective-permute-start(bf16[128,640]{1,0:T(8,128)(2,1)} %get-tuple-element.7.b2_ref), channel_id=1, source_target_pairs={{16,0},{24,8},{32,16},{40,24},{48,32},{56,40},{64,48},{72,56},{80,... | collective-permute-start | bytes 491528 | tf_op jit(solution)/shard_map/ppermute | solution.py:180
  95.9 0.6 slice_bitcast_fusion.cover_ref
  96.5 1.7 %collective-permute-done.6.b1_ref = bf16[128,640]{1,0:T(8,128)(2,1)S(1)} collective-permute-done((bf16[128,640]{1,0:T(8,128)(2,1)}, bf16[128,640]{1,0:T(8,128)(2,1)S(1)}, u32[]{:S(2)}, u32[]{:S(2)}) %collective-permute-start.6) | collective-permute-done | bytes 163872 | tf_op jit(solution)/shard_map/ppermute | solution.py:180
  98.2 3.1 %collective-permute-done.7.b3_ref = bf16[128,640]{1,0:T(8,128)(2,1)S(1)} collective-permute-done((bf16[128,640]{1,0:T(8,128)(2,1)}, bf16[128,640]{1,0:T(8,128)(2,1)S(1)}, u32[]{:S(2)}, u32[]{:S(2)}) %collective-permute-start.7) | collective-permute-done | bytes 163872 | tf_op jit(solution)/shard_map/ppermute | solution.py:180
  101.3 7.7 %collective-permute-done.8.b4_ref = bf16[128,640]{1,0:T(8,128)(2,1)S(1)} collective-permute-done((bf16[128,640]{1,0:T(8,128)(2,1)}, bf16[128,640]{1,0:T(8,128)(2,1)S(1)}, u32[]{:S(2)}, u32[]{:S(2)}) %collective-permute-start.8) | collective-permute-done | bytes 163872 | tf_op jit(solution)/shard_map/ppermute | solution.py:180
  109.0 0.7 copy-done.9
  109.7 7.0 %shard_map.111 = bf16[128,640]{1,0:T(8,128)(2,1)} custom-call(bf16[128,640]{1,0:T(8,128)(2,1)} %copy-done.5, bf16[128,640]{1,0:T(8,128)(2,1)} %copy-done.7, bf16[128,640]{1,0:T(8,128)(2,1)} %get-tuple-element.7.b2_ref, bf16[128,640]{1,0:T(8,128)(2,1)} %copy-done.8, bf16[128,640]{1,0:T(8,128)(2,1)} %copy-done.9, bf16[128,640]{1,0:T(8,128)(2,1)} %get-tuple-element.8.resid_ref, ...), custom_call_target="tpu_custom_call" | custom-call | tf_op jit(solution)/shard_map/pallas_call | solution.py:235
  (35 shorter events, 0.1 us)
Async XLA Ops:
  42.2 9.3 %copy-start = (bf16[16,360,80]{2,1,0:T(8,128)(2,1)}, bf16[16,360,80]{2,1,0:T(8,128)(2,1)S(1)}, u32[]{:S(2)}) copy-start(bf16[16,360,80]{2,1,0:T(8,128)(2,1)S(1)} %copy.20) | copy-start | bytes 2764804
  42.2 3.4 %copy-start.3 = (bf16[8,1,16,640]{3,2,1,0:T(8,128)(2,1)S(1)}, bf16[8,1,16,640]{3,2,1,0:T(8,128)(2,1)}, u32[]{:S(2)}) copy-start(bf16[8,1,16,640]{3,2,1,0:T(8,128)(2,1)} %param.11) | copy-start | bytes 491524
  42.2 6.5 %copy-start.11 = (f32[640]{0:T(1024)S(1)}, f32[640]{0:T(1024)}, u32[]{:S(2)}) copy-start(f32[640]{0:T(1024)} %param.16) | copy-start | bytes 7684
  42.2 6.6 %copy-start.17 = (s32[28]{0:T(128)S(1)}, s32[28]{0:T(128)}, u32[]{:S(2)}) copy-start(s32[28]{0:T(128)} %param.12) | copy-start | bytes 340
  42.2 20.6 %copy-start.12 = (f32[640]{0:T(1024)S(1)}, f32[640]{0:T(1024)}, u32[]{:S(2)}) copy-start(f32[640]{0:T(1024)} %param.13) | copy-start | bytes 7684
  42.2 21.2 %copy-start.13 = (f32[640]{0:T(1024)S(1)}, f32[640]{0:T(1024)}, u32[]{:S(2)}) copy-start(f32[640]{0:T(1024)} %param.14) | copy-start | bytes 7684
  42.2 21.8 %copy-start.14 = (f32[640]{0:T(1024)S(1)}, f32[640]{0:T(1024)}, u32[]{:S(2)}) copy-start(f32[640]{0:T(1024)} %param.17) | copy-start | bytes 7684
  42.2 22.3 %copy-start.15 = (f32[640]{0:T(1024)S(1)}, f32[640]{0:T(1024)}, u32[]{:S(2)}) copy-start(f32[640]{0:T(1024)} %param.18) | copy-start | bytes 7684
  43.7 22.1 %collective-permute-start.4 = (bf16[5760,80]{0,1:T(8,128)(2,1)S(1)}, bf16[5760,80]{0,1:T(8,128)(2,1)S(1)}, u32[]{:S(2)}, u32[]{:S(2)}) collective-permute-start(bf16[5760,80]{0,1:T(8,128)(2,1)S(1)} %copy.21), channel_id=1, source_target_pairs={{0,1},{1,0},{2,3},{3,2},{4,5},{5,4},{6,7},{7,6},{8,9},{9,8},{10,11... | collective-permute-start | bytes 2764808 | tf_op jit(solution)/shard_map/ppermute | solution.py:204
  46.3 3.5 %collective-permute-start = (bf16[4,16,640]{2,1,0:T(8,128)(2,1)}, bf16[4,16,640]{2,1,0:T(8,128)(2,1)S(1)}, u32[]{:S(2)}, u32[]{:S(2)}) collective-permute-start(bf16[4,16,640]{2,1,0:T(8,128)(2,1)} %get-tuple-element.10), channel_id=1, source_target_pairs={{0,1},{1,0},{2,3},{3,2},{4,5},{5,4},{6,7},{7,6},{8,9},{9,8},{10,11... | collective-permute-start | bytes 245768 | tf_op jit(solution)/shard_map/ppermute | solution.py:201
  49.8 0.6 copy-start.10
  51.4 16.4 %copy-start.2 = (bf16[2,4,16,640]{3,2,1,0:T(8,128)(2,1)}, bf16[2,4,16,640]{3,2,1,0:T(8,128)(2,1)S(1)}, u32[]{:S(2)}) copy-start(bf16[2,4,16,640]{3,2,1,0:T(8,128)(2,1)S(1)} %pad_maximum_fusion.own_ref) | copy-start | bytes 491524
  51.4 16.0 %collective-permute-start.1 = (bf16[2,4,16,640]{3,2,1,0:T(8,128)(2,1)S(1)}, bf16[2,4,16,640]{3,2,1,0:T(8,128)(2,1)}, u32[]{:S(2)}, u32[]{:S(2)}) collective-permute-start(bf16[2,4,16,640]{3,2,1,0:T(8,128)(2,1)S(1)} %pad_maximum_fusion.own_ref), channel_id=1, source_target_pairs={{0,2},{1,3},{2,4},{3,5},{4,6},{5,7},{6,0},{7,1},{8,10},{9,11},{10,... | collective-permute-start | bytes 491528 | tf_op jit(solution)/shard_map/ppermute | solution.py:196
  54.8 12.5 %collective-permute-start.2 = (bf16[2,4,16,640]{3,2,1,0:T(8,128)(2,1)S(1)}, bf16[2,4,16,640]{3,2,1,0:T(8,128)(2,1)S(1)}, u32[]{:S(2)}, u32[]{:S(2)}) collective-permute-start(bf16[2,4,16,640]{3,2,1,0:T(8,128)(2,1)S(1)} %pad_maximum_fusion.own_ref), channel_id=1, source_target_pairs={{0,6},{1,7},{2,0},{3,1},{4,2},{5,3},{6,4},{7,5},{8,14},{9,15},{10,... | collective-permute-start | bytes 491528 | tf_op jit(solution)/shard_map/ppermute | solution.py:196
  58.5 9.3 %collective-permute-start.3 = (bf16[2,4,16,640]{3,2,1,0:T(8,128)(2,1)S(1)}, bf16[2,4,16,640]{3,2,1,0:T(8,128)(2,1)S(1)}, u32[]{:S(2)}, u32[]{:S(2)}) collective-permute-start(bf16[2,4,16,640]{3,2,1,0:T(8,128)(2,1)S(1)} %pad_maximum_fusion.own_ref), channel_id=1, source_target_pairs={{0,4},{1,5},{2,6},{3,7},{4,0},{5,1},{6,2},{7,3},{8,12},{9,13},{10,... | collective-permute-start | bytes 491528 | tf_op jit(solution)/shard_map/ppermute | solution.py:196
  67.4 0.7 copy-start.4
  67.8 0.7 copy-start.6
  68.5 11.1 %copy-start.16 = (f32[640]{0:T(1024)S(1)}, f32[640]{0:T(1024)}, u32[]{:S(2)}) copy-start(f32[640]{0:T(1024)} %param.21) | copy-start | bytes 7684
  75.4 10.8 %all-to-all-start = ((bf16[8,64,160]{2,1,0:T(8,128)(2,1)}), bf16[8,64,160]{2,1,0:T(8,128)(2,1)S(1)}, u32[]{:S(2)}, u32[]{:S(2)}) async-start(bf16[8,64,160]{2,1,0:T(8,128)(2,1)} %shard_map.109), calls=%async_computation | async-start | bytes 524288 | tf_op jit(solution)/shard_map/all_to_all | solution.py:219
  86.2 0.7 copy-start.1
  89.1 7.4 %collective-permute-start.5 = (bf16[128,640]{1,0:T(8,128)(2,1)}, bf16[128,640]{1,0:T(8,128)(2,1)S(1)}, u32[]{:S(2)}, u32[]{:S(2)}) collective-permute-start(bf16[128,640]{1,0:T(8,128)(2,1)} %get-tuple-element.7.b2_ref), channel_id=1, source_target_pairs={{0,16},{8,24},{16,32},{24,40},{32,48},{40,56},{48,64},{56,72},{64,... | collective-permute-start | bytes 491528 | tf_op jit(solution)/shard_map/ppermute | solution.py:180
  91.3 6.9 %collective-permute-start.6 = (bf16[128,640]{1,0:T(8,128)(2,1)}, bf16[128,640]{1,0:T(8,128)(2,1)S(1)}, u32[]{:S(2)}, u32[]{:S(2)}) collective-permute-start(bf16[128,640]{1,0:T(8,128)(2,1)} %get-tuple-element.7.b2_ref), channel_id=1, source_target_pairs={{0,8},{8,16},{16,24},{24,32},{32,40},{40,48},{48,56},{56,64},{64,7... | collective-permute-start | bytes 491528 | tf_op jit(solution)/shard_map/ppermute | solution.py:180
  93.3 8.0 %collective-permute-start.7 = (bf16[128,640]{1,0:T(8,128)(2,1)}, bf16[128,640]{1,0:T(8,128)(2,1)S(1)}, u32[]{:S(2)}, u32[]{:S(2)}) collective-permute-start(bf16[128,640]{1,0:T(8,128)(2,1)} %get-tuple-element.7.b2_ref), channel_id=1, source_target_pairs={{8,0},{16,8},{24,16},{32,24},{40,32},{48,40},{56,48},{64,56},{72,6... | collective-permute-start | bytes 491528 | tf_op jit(solution)/shard_map/ppermute | solution.py:180
  94.6 14.4 %collective-permute-start.8 = (bf16[128,640]{1,0:T(8,128)(2,1)}, bf16[128,640]{1,0:T(8,128)(2,1)S(1)}, u32[]{:S(2)}, u32[]{:S(2)}) collective-permute-start(bf16[128,640]{1,0:T(8,128)(2,1)} %get-tuple-element.7.b2_ref), channel_id=1, source_target_pairs={{16,0},{24,8},{32,16},{40,24},{48,32},{56,40},{64,48},{72,56},{80,... | collective-permute-start | bytes 491528 | tf_op jit(solution)/shard_map/ppermute | solution.py:180
  96.5 12.5 %copy-start.5 = (bf16[128,640]{1,0:T(8,128)(2,1)}, bf16[128,640]{1,0:T(8,128)(2,1)S(1)}, u32[]{:S(2)}) copy-start(bf16[128,640]{1,0:T(8,128)(2,1)S(1)} %collective-permute-done.5.b0_ref) | copy-start | bytes 491524
  98.2 10.8 %copy-start.7 = (bf16[128,640]{1,0:T(8,128)(2,1)}, bf16[128,640]{1,0:T(8,128)(2,1)S(1)}, u32[]{:S(2)}) copy-start(bf16[128,640]{1,0:T(8,128)(2,1)S(1)} %collective-permute-done.6.b1_ref) | copy-start | bytes 491524
  101.3 7.7 %copy-start.8 = (bf16[128,640]{1,0:T(8,128)(2,1)}, bf16[128,640]{1,0:T(8,128)(2,1)S(1)}, u32[]{:S(2)}) copy-start(bf16[128,640]{1,0:T(8,128)(2,1)S(1)} %collective-permute-done.7.b3_ref) | copy-start | bytes 491524
  109.0 0.7 copy-start.9

commit v2 on v1

v2 whole, which is shorter than its diff:
```python
import jax
import jax.numpy as jnp
from jax import lax
from jax.experimental import pallas as pl
from jax.experimental.pallas import tpu as pltpu
from jax.sharding import PartitionSpec as P

HEADS = 10
GROUPS = 32
WIN = 16
HEAD_DIM = 64
LANES = 128

EPSILON = 1e-05
F32 = jnp.float32
BF16 = jnp.bfloat16
VMEM = pl.BlockSpec(memory_space=pltpu.VMEM)
SMEM = pl.BlockSpec(memory_space=pltpu.SMEM)
GRANT = pltpu.CompilerParams(vmem_limit_bytes=32 << 20)
NT = (((1,), (1,)), ((), ()))


def on_chip(array):
    return pltpu.with_memory_space_constraint(array, pltpu.VMEM)


def dot(a, b):
    return jnp.dot(a, b, preferred_element_type=F32)


def exact_dot(a, b, dims=(((1,), (0,)), ((), ()))):
    return lax.dot_general(a, b, dims, precision=lax.Precision.HIGHEST, preferred_element_type=F32)


def iota(shape, dim):
    return lax.broadcasted_iota(jnp.int32, shape, dim)


def conv_kernel(
    cells_ref, weight_ref, gain_ref, bias_ref, cbias_ref, out_ref, padded, taps, shifted
):
    rows, frames, width, chans = cells_ref.shape
    chunks, outs, chunk = weight_ref.shape
    for z in range(chunks):
        taps[:, z * chunk : (z + 1) * chunk] = weight_ref[z]
    groups = (iota((chans, LANES), 0).astype(F32) + 0.5) * (GROUPS / chans)
    groups = (jnp.floor(groups) == iota((chans, LANES), 1).astype(F32)).astype(F32)
    count = rows * width * (chans // GROUPS)

    def group_mean(sums):
        per_group = exact_dot(jnp.concatenate(sums, axis=0), groups) / count
        return exact_dot(per_group, groups, NT)

    def frame(f):
        return cells_ref[:, f].reshape(rows * width, chans).astype(F32)

    mean = group_mean([jnp.sum(frame(f), axis=0, keepdims=True) for f in range(frames)])
    sums = []
    for f in range(frames):
        centred = frame(f) - mean[f : f + 1]
        sums.append(jnp.sum(centred * centred, axis=0, keepdims=True))
    inverse = lax.rsqrt(group_mean(sums) + EPSILON)
    gain, bias = gain_ref[...].reshape(1, chans), bias_ref[...].reshape(1, chans)
    edge = jnp.zeros((frames, width, chans), BF16)
    padded[0] = edge
    padded[rows + 1] = edge
    for f in range(frames):
        for r in range(rows):
            normed = cells_ref[r, f].astype(F32) - mean[f : f + 1]
            normed = normed * inverse[f : f + 1] * gain + bias
            padded[r + 1, f] = (normed / (1.0 + jnp.exp(-normed))).astype(BF16)
    flat = rows * frames * width
    column = lax.rem(iota((flat, 1), 0), width)
    total = None
    for row in range(3):
        tap = [taps[:, (3 * row + col) * chans : (3 * row + col + 1) * chans] for col in range(3)]
        term = lax.dot_general(
            padded[row : row + rows].reshape(flat, chans),
            jnp.concatenate(tap, axis=0),
            NT,
            preferred_element_type=F32,
        )
        total = term if total is None else total + term
    shifted[8 : 8 + flat] = total
    before = jnp.where(column == 0, 0.0, shifted[7 : 7 + flat, :outs])
    after = jnp.where(column == width - 1, 0.0, shifted[9 : 9 + flat, 2 * outs :])
    result = total[:, outs : 2 * outs] + before + after + cbias_ref[...]
    result = result.reshape(rows, frames * width, outs)
    for r in range(rows):
        out_ref[r] = result[r].T.astype(BF16)


def swap_matrix(frames, width, back):
    cells = frames * width
    near, far = iota((cells, cells), 1 if back else 0), iota((cells, cells), 0 if back else 1)
    same = (lax.div(near, frames) == lax.rem(far, width)) & (
        lax.rem(near, frames) == lax.div(far, width)
    )
    return same.astype(F32).astype(BF16)


def norm_kernel(part_ref, video_ref, gain_ref, bias_ref, resid_ref, norm_ref):
    frames, width, chans = video_ref.shape
    cells = frames * width
    conv_out = part_ref[...].reshape(chans, cells).astype(F32).T
    resid = (video_ref[...].reshape(cells, chans).astype(F32) + conv_out).astype(BF16)
    resid_ref[...] = resid
    floats = resid.astype(F32)
    deviation = floats - jnp.mean(floats, axis=-1, keepdims=True)
    spread = jnp.mean(deviation * deviation, axis=-1, keepdims=True)
    gain, bias = gain_ref[...].reshape(1, chans), bias_ref[...].reshape(1, chans)
    norm = (deviation * lax.rsqrt(spread + EPSILON) * gain + bias).astype(BF16)
    norm_ref[...] = dot(swap_matrix(frames, width, False), norm).astype(BF16)


def attend_kernel(
    gaps_ref, b0_ref, b1_ref, b2_ref, b3_ref, b4_ref, resid_ref, qkv_ref, out_w_ref, out_b_ref,
    out_ref, keys, values, query, scores, mixed,
):
    blocks, width, frames, chans = keys.shape
    near = blocks * frames
    stack = HEADS * frames

    def by_cell(product):
        return product.astype(BF16).astype(F32).reshape(width, frames, chans)

    query[...] = by_cell(dot(b2_ref[...], qkv_ref[:, :chans]))
    for b, ref in enumerate((b0_ref, b1_ref, b2_ref, b3_ref, b4_ref)):
        keys[b] = by_cell(dot(ref[...], qkv_ref[:, chans : 2 * chans]))
        values[b] = by_cell(dot(ref[...], qkv_ref[:, 2 * chans :]))
    window = iota((1, LANES), 1)
    start, starts = jnp.int32(0), jnp.where(window == 0, 0, -(1 << 20))
    for w in range(gaps_ref.shape[0]):
        start = start + gaps_ref[w]
        starts = jnp.where(window == w + 1, start, starts)
    ids = (lax.axis_index("frames") - 2) * frames + iota((near, LANES), 0)
    member = ((ids >= starts) & (ids < starts + WIN)).astype(F32)
    cover = member[2 * frames : 3 * frames][None]
    member = member.astype(BF16)
    head_of = lax.div(iota((HEADS, 1, chans), 2), HEAD_DIM) == iota((HEADS, 1, chans), 0)
    own = head_of.astype(F32)
    for c in range(width):
        spread = (query[c][None] * own).reshape(stack, chans).astype(BF16)
        key = keys[:, c].reshape(near, chans).astype(BF16)
        scores[c] = lax.dot_general(spread, key, NT, preferred_element_type=F32)
    flat = width * stack
    expo = jnp.exp(scores[...].reshape(flat, near) * HEAD_DIM ** (-0.5))

    def split_dot(a, dims):
        high = a.astype(BF16)
        rest = (a - high.astype(F32)).astype(BF16)
        return lax.dot_general(high, member, dims, preferred_element_type=F32) + lax.dot_general(
            rest, member, dims, preferred_element_type=F32
        )

    sums = split_dot(expo, (((1,), (0,)), ((), ()))).reshape(width * HEADS, frames, LANES)
    frame_count = jnp.sum(cover, axis=2, keepdims=True)
    coef = (cover / (frame_count * jnp.where(cover > 0, sums, 1.0))).reshape(flat, LANES)
    back = split_dot(coef, NT)
    scores[...] = (expo * back).reshape(width, stack, near)
    for c in range(width):
        value = values[:, c].reshape(near, chans).astype(BF16)
        product = dot(scores[c].astype(BF16), value).reshape(HEADS, frames, chans)
        mixed[c] = jnp.sum(jnp.where(head_of, product, 0.0), axis=0)
    joined = mixed[...].reshape(width * frames, chans).astype(BF16)
    joined = dot(swap_matrix(frames, width, True), joined).astype(BF16)
    projected = dot(joined, out_w_ref[...])
    output = resid_ref[...].astype(F32) + projected + out_b_ref[...].reshape(1, chans)
    out_ref[...] = output.astype(BF16).reshape(frames, width, chans)


def passed(shard, by):
    size = lax.axis_size("frames")
    pairs = [(i, i + by) for i in range(size) if 0 <= i + by < size]
    return lax.ppermute(shard, "frames", pairs)


def on_device(
    video, window_gaps, gn_gain, gn_bias, conv_weight, conv_bias,
    ln_gain, ln_bias, qkv_weight, out_weight, out_bias,
):
    frames, _, width, chans = video.shape
    bands = lax.axis_size("height")
    place = lax.axis_index("height")
    outs = conv_weight.shape[1]
    cells = frames * width
    row = video.reshape(frames, width, chans)
    copies = jnp.broadcast_to(row[None], (bands, frames, width, chans))
    whole = lax.all_to_all(copies, "height", 0, 0, tiled=True)
    weight = lax.all_gather(conv_weight.T, "frames", axis=0, tiled=False)
    cbias = lax.dynamic_slice_in_dim(conv_bias, place * outs, outs)[None]
    parts = pl.pallas_call(
        conv_kernel,
        out_shape=jax.ShapeDtypeStruct((bands, outs, cells), BF16),
        in_specs=[VMEM] * 5,
        out_specs=VMEM,
        compiler_params=GRANT,
        scratch_shapes=[
            pltpu.VMEM((bands + 2, frames, width, chans), BF16),
            pltpu.VMEM((outs, 9 * chans), BF16),
            pltpu.VMEM((bands * cells + 16, 3 * outs), F32),
        ],
    )(on_chip(whole), on_chip(weight), gn_gain, gn_bias, cbias)
    parts = lax.all_to_all(parts, "height", 0, 0, tiled=True)
    resid, norm = pl.pallas_call(
        norm_kernel,
        out_shape=[jax.ShapeDtypeStruct((cells, chans), BF16)] * 2,
        in_specs=[VMEM] * 4,
        out_specs=[VMEM] * 2,
        compiler_params=GRANT,
    )(on_chip(parts), row, ln_gain, ln_bias)
    near = [passed(norm, by) for by in (2, 1)] + [norm] + [passed(norm, by) for by in (-1, -2)]
    out = pl.pallas_call(
        attend_kernel,
        out_shape=jax.ShapeDtypeStruct((frames, width, chans), BF16),
        in_specs=[SMEM] + [VMEM] * 9,
        out_specs=VMEM,
        compiler_params=GRANT,
        scratch_shapes=[
            pltpu.VMEM((5, width, frames, chans), F32),
            pltpu.VMEM((5, width, frames, chans), F32),
            pltpu.VMEM((width, frames, chans), F32),
            pltpu.VMEM((width, HEADS * frames, 5 * frames), F32),
            pltpu.VMEM((width, frames, chans), F32),
        ],
    )(window_gaps, *[on_chip(n) for n in near], resid, on_chip(qkv_weight), on_chip(out_weight), out_bias)
    return out.reshape(frames, 1, width, chans)


def solution(mesh):
    placed = (
        P(("dp", "frames"), "height", None, None),
        P("dp"),
        P(),
        P(),
        P("frames", "height"),
        P(),
        P(),
        P(),
        P(),
        P(),
        P(),
    )
    return jax.shard_map(
        on_device,
        mesh=mesh,
        in_specs=placed,
        out_specs=P(("dp", "frames"), "height", None, None),
        check_vma=False,
    )
```

time: 117 us -> 89.5 us (0.76)
  starting transfers between devices: 25.2 us -> 11 us
  blocking collectives: 41.3 us -> 52.4 us
  local copies, waits for them, and re-layouts: 11.6 us -> 2.25 us
  waiting for transfers between devices: 19.6 us -> 13.4 us
  Pallas kernels: 16.1 us -> 10.1 us
  other arithmetic: 2.51 us -> 0 us
    ppermute x9 -> x4, starting transfers between devices: 21.8 us -> 6.57 us  [passed(): return lax.ppermute(shard, 'frames', pairs)]
    all_to_all x0 -> x1, blocking collectives: none -> 11 us  [on_device(): parts = lax.all_to_all(parts, 'height', 0, 0, tiled=True)]
    all_to_all x1, waiting for transfers between devices: 6.04 us -> 0.01 us  [on_device(): whole = lax.all_to_all(copies, 'height', 0, 0, tiled=True)]
    pallas_call x2, Pallas kernels: 13.9 us -> 9.62 us  [the longest x1 5.25 us: on_device(): pl.pallas_call(attend_kernel, out_shape=jax.ShapeDtypeStruct((frames, wid...]
    unnamed x37 -> x22, local copies, waits for them, and re-layouts: 4.13 us -> 0.06 us
    pallas_call x1, Pallas kernels: 2.22 us -> 0.49 us  [on_device(): pl.pallas_call(norm_kernel, out_shape=[jax.ShapeDtypeStruct((cells, chans...]
    another operation x4 -> x0, other arithmetic: 1.69 us -> none  [the longest x1 0.95 us: on_device(): pair = jnp.stack([kept, lax.ppermute(sent, 'height', swap)])]
    ppermute x1 -> x0, local copies, waits for them, and re-layouts: 1.57 us -> none  [on_device(): other = lax.ppermute(weight, 'height', swap)]
  transfers between devices with their start and end apart: 10 -> 5, of which waited for: 6 -> 4; matrix products, arithmetic and copies ran while one was open for 8% -> 0% of each run, Pallas kernels for 0% -> 0%
where the time goes in v2:
time: 89.5 us; the launch traced here: 89.2 us
  blocking collectives  52.4 us (59%)
  waiting for transfers between devices  13.4 us (15%)
  starting transfers between devices  11 us (12%)
  Pallas kernels  10.1 us (11%)
  local copies, waits for them, and re-layouts  2.25 us (3%)
    all_gather x1, blocking collectives, on_device(): weight = lax.all_gather(conv_weight.T, 'frames', axis=0, tiled=False)  41.4 us
    ppermute x4, waiting for transfers between devices, passed(): return lax.ppermute(shard, 'frames', pairs)  13.4 us
    all_to_all x1, blocking collectives, on_device(): parts = lax.all_to_all(parts, 'height', 0, 0, tiled=True)  11 us
    ppermute x4, starting transfers between devices, passed(): return lax.ppermute(shard, 'frames', pairs)  6.57 us
    pallas_call x1, Pallas kernels, on_device(): pl.pallas_call(attend_kernel, out_shape=jax.ShapeDtypeStruct((frames, wid...  5.25 us
    all_to_all x1, starting transfers between devices, on_device(): whole = lax.all_to_all(copies, 'height', 0, 0, tiled=True)  4.43 us
    pallas_call x1, Pallas kernels, on_device(): pl.pallas_call(conv_kernel, out_shape=jax.ShapeDtypeStruct((bands, outs,...  4.38 us
    broadcast_in_dim x1, local copies, waits for them, and re-layouts, on_device(): copies = jnp.broadcast_to(row[None], (bands, frames, width, chans))  2.12 us
  transfers between devices with their start and end apart: 5, of which 4 were waited for; matrix products, arithmetic and copies ran while one was open for 0% of the time, Pallas kernels for 0%

profile of v2, /device:TPU:24, one launch (start us, length us, event | category | flops | bytes accessed | tf_op | source)
XLA Modules:
  0.0 89.2 jit_solution(1744566352204927679)
XLA Ops:
  0.0 0.0 copy-start
  0.0 2.1 %broadcast_in_dim.11 = bf16[8,8,16,640]{3,2,1,0:T(8,128)(2,1)} broadcast(bf16[8,16,640]{2,1,0:T(8,128)(2,1)} %bitcast.9), dimensions={1,2,3} | broadcast | bytes 1474560 | tf_op jit(solution)/shard_map/broadcast_in_dim | solution.py:188
  2.1 0.0 copy-start.10
  2.1 0.0 copy-start.4
  2.1 0.0 copy-start.5
  2.1 4.4 %all-to-all-start = ((bf16[8,8,16,640]{3,2,1,0:T(8,128)(2,1)}), bf16[8,8,16,640]{3,2,1,0:T(8,128)(2,1)S(1)}, u32[]{:S(2)}, u32[]{:S(2)}) async-start(bf16[8,8,16,640]{3,2,1,0:T(8,128)(2,1)} %broadcast_in_dim.11), calls=%async_computation | async-start | bytes 2621440 | tf_op jit(solution)/shard_map/all_to_all | solution.py:189
  6.6 0.0 copy-done
  6.6 0.1 dynamic-slice_bitcast_fusion.cbias_ref
  6.6 0.0 copy-done.10
  6.6 0.0 copy-start.2
  6.6 41.4 %all-gather = bf16[1280,360]{1,0:T(8,128)(2,1)S(1)} all-gather(bf16[80,360]{1,0:T(8,128)(2,1)S(1)} %bitcast.11), channel_id=2, replica_groups=mesh['dp'=4,'frames'=16,'height'=8] {'frames'}, dimensions={0}, use_global_device_ids=true | all-gather | bytes 979200 | tf_op jit(solution)/shard_map/all_gather | solution.py:190
  48.1 0.0 all-to-all-done.cells_ref
  48.1 0.0 copy-done.4
  48.1 0.0 copy-done.5
  48.1 0.0 copy-start.3
  48.1 0.0 copy-start.6
  48.1 0.0 copy-start.7
  48.1 0.0 copy-start.1
  48.1 0.0 copy-start.8
  48.1 0.0 copy-start.9
  48.1 4.4 %shard_map.109 = bf16[8,80,128]{2,1,0:T(8,128)(2,1)S(1)} custom-call(bf16[8,8,16,640]{3,2,1,0:T(8,128)(2,1)S(1)} %all-to-all-done.cells_ref, bf16[16,80,360]{2,1,0:T(8,128)(2,1)S(1)} %bitcast.8, f32[640]{0:T(1024)S(1)} %copy-done.4, f32[640]{0:T(1024)S(1)} %copy-done.5, f32[1,80]{1,0:T(1,128)S(1)} %dynamic-slice_bitcast_fusion.cbias_ref), custom_call_target="tpu_custom_call" | custom-call | tf_op jit(solution)/shard_map/pallas_call | solution.py:192
  52.5 11.0 %all_to_all.10.part_ref = bf16[8,80,128]{2,1,0:T(8,128)(2,1)S(1)} all-to-all(bf16[8,80,128]{2,1,0:T(8,128)(2,1)S(1)} %shard_map.109), channel_id=1, replica_groups=mesh['dp'=4,'frames'=16,'height'=8] {'height'}, dimensions={0} | all-to-all | bytes 327680 | tf_op jit(solution)/shard_map/all_to_all | solution.py:204
  63.5 0.0 copy-done.3
  63.5 0.0 copy-done.6
  63.5 0.0 copy-done.7
  63.5 0.5 shard_map.110
  64.0 2.2 %collective-permute-start = (bf16[128,640]{1,0:T(8,128)(2,1)S(1)}, bf16[128,640]{1,0:T(8,128)(2,1)S(1)}, u32[]{:S(2)}, u32[]{:S(2)}) collective-permute-start(bf16[128,640]{1,0:T(8,128)(2,1)S(1)} %get-tuple-element.7.b2_ref), channel_id=1, source_target_pairs={{0,16},{8,24},{16,32},{24,40},{32,48},{40,56},{48,64},{56,72},{64,... | collective-permute-start | bytes 491528 | tf_op jit(solution)/shard_map/ppermute | solution.py:175
  66.1 1.8 %collective-permute-start.1 = (bf16[128,640]{1,0:T(8,128)(2,1)S(1)}, bf16[128,640]{1,0:T(8,128)(2,1)S(1)}, u32[]{:S(2)}, u32[]{:S(2)}) collective-permute-start(bf16[128,640]{1,0:T(8,128)(2,1)S(1)} %get-tuple-element.7.b2_ref), channel_id=1, source_target_pairs={{0,8},{8,16},{16,24},{24,32},{32,40},{40,48},{48,56},{56,64},{64,7... | collective-permute-start | bytes 491528 | tf_op jit(solution)/shard_map/ppermute | solution.py:175
  68.0 1.3 %collective-permute-start.2 = (bf16[128,640]{1,0:T(8,128)(2,1)S(1)}, bf16[128,640]{1,0:T(8,128)(2,1)S(1)}, u32[]{:S(2)}, u32[]{:S(2)}) collective-permute-start(bf16[128,640]{1,0:T(8,128)(2,1)S(1)} %get-tuple-element.7.b2_ref), channel_id=1, source_target_pairs={{8,0},{16,8},{24,16},{32,24},{40,32},{48,40},{56,48},{64,56},{72,6... | collective-permute-start | bytes 491528 | tf_op jit(solution)/shard_map/ppermute | solution.py:175
  69.3 1.3 %collective-permute-start.3 = (bf16[128,640]{1,0:T(8,128)(2,1)S(1)}, bf16[128,640]{1,0:T(8,128)(2,1)S(1)}, u32[]{:S(2)}, u32[]{:S(2)}) collective-permute-start(bf16[128,640]{1,0:T(8,128)(2,1)S(1)} %get-tuple-element.7.b2_ref), channel_id=1, source_target_pairs={{16,0},{24,8},{32,16},{40,24},{48,32},{56,40},{64,48},{72,56},{80,... | collective-permute-start | bytes 491528 | tf_op jit(solution)/shard_map/ppermute | solution.py:175
  70.6 0.1 collective-permute-done.b0_ref
  70.7 2.2 %collective-permute-done.1.b1_ref = bf16[128,640]{1,0:T(8,128)(2,1)S(1)} collective-permute-done((bf16[128,640]{1,0:T(8,128)(2,1)S(1)}, bf16[128,640]{1,0:T(8,128)(2,1)S(1)}, u32[]{:S(2)}, u32[]{:S(2)}) %collective-permute-start.1) | collective-permute-done | bytes 163872 | tf_op jit(solution)/shard_map/ppermute | solution.py:175
  72.9 3.1 %collective-permute-done.2.b3_ref = bf16[128,640]{1,0:T(8,128)(2,1)S(1)} collective-permute-done((bf16[128,640]{1,0:T(8,128)(2,1)S(1)}, bf16[128,640]{1,0:T(8,128)(2,1)S(1)}, u32[]{:S(2)}, u32[]{:S(2)}) %collective-permute-start.2) | collective-permute-done | bytes 163872 | tf_op jit(solution)/shard_map/ppermute | solution.py:175
  76.0 8.0 %collective-permute-done.3.b4_ref = bf16[128,640]{1,0:T(8,128)(2,1)S(1)} collective-permute-done((bf16[128,640]{1,0:T(8,128)(2,1)S(1)}, bf16[128,640]{1,0:T(8,128)(2,1)S(1)}, u32[]{:S(2)}, u32[]{:S(2)}) %collective-permute-start.3) | collective-permute-done | bytes 163872 | tf_op jit(solution)/shard_map/ppermute | solution.py:175
  83.9 0.0 copy-done.2
  83.9 0.0 copy-done.1
  83.9 0.0 copy-done.8
  84.0 0.0 copy-done.9
  84.0 5.2 %shard_map.111 = bf16[8,16,640]{2,1,0:T(8,128)(2,1)} custom-call(s32[28]{0:T(128)S(1)} %copy-done.9, bf16[128,640]{1,0:T(8,128)(2,1)S(1)} %collective-permute-done.b0_ref, bf16[128,640]{1,0:T(8,128)(2,1)S(1)} %collective-permute-done.1.b1_ref, bf16[128,640]{1,0:T(8,128)(2,1)S(1)} %get-tuple-element.7.b2_ref, ...), custom_call_target="tpu_custom_call" | custom-call | tf_op jit(solution)/shard_map/pallas_call | solution.py:213
Async XLA Ops:
  0.0 6.6 %copy-start = (f32[640]{0:T(1024)S(1)}, f32[640]{0:T(1024)}, u32[]{:S(2)}) copy-start(f32[640]{0:T(1024)} %param.16) | copy-start | bytes 7684
  2.1 4.5 %copy-start.10 = (bf16[360,80]{0,1:T(8,128)(2,1)S(1)}, bf16[360,80]{0,1:T(8,128)(2,1)}, u32[]{:S(2)}) copy-start(bf16[360,80]{0,1:T(8,128)(2,1)} %param.15) | copy-start | bytes 172804
  2.1 45.9 %copy-start.4 = (f32[640]{0:T(1024)S(1)}, f32[640]{0:T(1024)}, u32[]{:S(2)}) copy-start(f32[640]{0:T(1024)} %gain_ref.2) | copy-start | bytes 7684
  2.1 45.9 %copy-start.5 = (f32[640]{0:T(1024)S(1)}, f32[640]{0:T(1024)}, u32[]{:S(2)}) copy-start(f32[640]{0:T(1024)} %bias_ref.2) | copy-start | bytes 7684
  2.1 45.9 %all-to-all-start = ((bf16[8,8,16,640]{3,2,1,0:T(8,128)(2,1)}), bf16[8,8,16,640]{3,2,1,0:T(8,128)(2,1)S(1)}, u32[]{:S(2)}, u32[]{:S(2)}) async-start(bf16[8,8,16,640]{3,2,1,0:T(8,128)(2,1)} %broadcast_in_dim.11), calls=%async_computation | async-start | bytes 2621440 | tf_op jit(solution)/shard_map/all_to_all | solution.py:189
  6.6 77.3 %copy-start.2 = (bf16[640,640]{1,0:T(8,128)(2,1)S(1)}, bf16[640,640]{1,0:T(8,128)(2,1)}, u32[]{:S(2)}) copy-start(bf16[640,640]{1,0:T(8,128)(2,1)} %out_w_ref.1) | copy-start | bytes 2457604
  48.1 15.4 %copy-start.3 = (bf16[8,1,16,640]{3,2,1,0:T(8,128)(2,1)S(1)}, bf16[8,1,16,640]{3,2,1,0:T(8,128)(2,1)}, u32[]{:S(2)}) copy-start(bf16[8,1,16,640]{3,2,1,0:T(8,128)(2,1)} %param.11) | copy-start | bytes 491524
  48.1 15.4 %copy-start.6 = (f32[640]{0:T(1024)S(1)}, f32[640]{0:T(1024)}, u32[]{:S(2)}) copy-start(f32[640]{0:T(1024)} %gain_ref.3) | copy-start | bytes 7684
  48.1 15.4 %copy-start.7 = (f32[640]{0:T(1024)S(1)}, f32[640]{0:T(1024)}, u32[]{:S(2)}) copy-start(f32[640]{0:T(1024)} %bias_ref.3) | copy-start | bytes 7684
  48.1 35.8 %copy-start.1 = (bf16[640,1920]{1,0:T(8,128)(2,1)S(1)}, bf16[640,1920]{1,0:T(8,128)(2,1)}, u32[]{:S(2)}) copy-start(bf16[640,1920]{1,0:T(8,128)(2,1)} %qkv_ref.1) | copy-start | bytes 7372804
  48.1 35.8 %copy-start.8 = (f32[640]{0:T(1024)S(1)}, f32[640]{0:T(1024)}, u32[]{:S(2)}) copy-start(f32[640]{0:T(1024)} %out_b_ref.1) | copy-start | bytes 7684
  48.1 35.8 %copy-start.9 = (s32[28]{0:T(128)S(1)}, s32[28]{0:T(128)}, u32[]{:S(2)}) copy-start(s32[28]{0:T(128)} %gaps_ref.1) | copy-start | bytes 340
  64.0 6.7 %collective-permute-start = (bf16[128,640]{1,0:T(8,128)(2,1)S(1)}, bf16[128,640]{1,0:T(8,128)(2,1)S(1)}, u32[]{:S(2)}, u32[]{:S(2)}) collective-permute-start(bf16[128,640]{1,0:T(8,128)(2,1)S(1)} %get-tuple-element.7.b2_ref), channel_id=1, source_target_pairs={{0,16},{8,24},{16,32},{24,40},{32,48},{40,56},{48,64},{56,72},{64,... | collective-permute-start | bytes 491528 | tf_op jit(solution)/shard_map/ppermute | solution.py:175
  66.1 6.8 %collective-permute-start.1 = (bf16[128,640]{1,0:T(8,128)(2,1)S(1)}, bf16[128,640]{1,0:T(8,128)(2,1)S(1)}, u32[]{:S(2)}, u32[]{:S(2)}) collective-permute-start(bf16[128,640]{1,0:T(8,128)(2,1)S(1)} %get-tuple-element.7.b2_ref), channel_id=1, source_target_pairs={{0,8},{8,16},{16,24},{24,32},{32,40},{40,48},{48,56},{56,64},{64,7... | collective-permute-start | bytes 491528 | tf_op jit(solution)/shard_map/ppermute | solution.py:175
  68.0 8.0 %collective-permute-start.2 = (bf16[128,640]{1,0:T(8,128)(2,1)S(1)}, bf16[128,640]{1,0:T(8,128)(2,1)S(1)}, u32[]{:S(2)}, u32[]{:S(2)}) collective-permute-start(bf16[128,640]{1,0:T(8,128)(2,1)S(1)} %get-tuple-element.7.b2_ref), channel_id=1, source_target_pairs={{8,0},{16,8},{24,16},{32,24},{40,32},{48,40},{56,48},{64,56},{72,6... | collective-permute-start | bytes 491528 | tf_op jit(solution)/shard_map/ppermute | solution.py:175
  69.3 14.7 %collective-permute-start.3 = (bf16[128,640]{1,0:T(8,128)(2,1)S(1)}, bf16[128,640]{1,0:T(8,128)(2,1)S(1)}, u32[]{:S(2)}, u32[]{:S(2)}) collective-permute-start(bf16[128,640]{1,0:T(8,128)(2,1)S(1)} %get-tuple-element.7.b2_ref), channel_id=1, source_target_pairs={{16,0},{24,8},{32,16},{40,24},{48,32},{56,40},{64,48},{72,56},{80,... | collective-permute-start | bytes 491528 | tf_op jit(solution)/shard_map/ppermute | solution.py:175

commit v3 on v2

--- a/solution.py
+++ b/solution.py
@@ -60,15 +60,15 @@
         centred = frame(f) - mean[f : f + 1]
         sums.append(jnp.sum(centred * centred, axis=0, keepdims=True))
     inverse = lax.rsqrt(group_mean(sums) + EPSILON)
-    gain, bias = gain_ref[...].reshape(1, chans), bias_ref[...].reshape(1, chans)
+    scale, bias = inverse * gain_ref[...].reshape(1, chans), bias_ref[...].reshape(1, chans)
     edge = jnp.zeros((frames, width, chans), BF16)
     padded[0] = edge
     padded[rows + 1] = edge
     for f in range(frames):
         for r in range(rows):
             normed = cells_ref[r, f].astype(F32) - mean[f : f + 1]
-            normed = normed * inverse[f : f + 1] * gain + bias
-            padded[r + 1, f] = (normed / (1.0 + jnp.exp(-normed))).astype(BF16)
+            normed = 0.5 * (normed * scale[f : f + 1] + bias)
+            padded[r + 1, f] = (normed + normed * jnp.tanh(normed)).astype(BF16)
     flat = rows * frames * width
     column = lax.rem(iota((flat, 1), 0), width)
     total = None
@@ -113,21 +113,35 @@
     norm_ref[...] = dot(swap_matrix(frames, width, False), norm).astype(BF16)
 
 
+def by_cell(product, shape):
+    return product.astype(BF16).astype(F32).reshape(shape)
+
+
+def early_kernel(before_ref, norm_ref, after_ref, qkv_ref, query_ref, key_ref, value_ref):
+    chans = norm_ref.shape[1]
+    shape = query_ref.shape
+    query_ref[...] = by_cell(dot(norm_ref[...], qkv_ref[:, :chans]), shape)
+    for b, ref in enumerate((before_ref, norm_ref, after_ref)):
+        key_ref[b] = by_cell(dot(ref[...], qkv_ref[:, chans : 2 * chans]), shape)
+        value_ref[b] = by_cell(dot(ref[...], qkv_ref[:, 2 * chans :]), shape)
+
+
 def attend_kernel(
-    gaps_ref, b0_ref, b1_ref, b2_ref, b3_ref, b4_ref, resid_ref, qkv_ref, out_w_ref, out_b_ref,
-    out_ref, keys, values, query, scores, mixed,
+    gaps_ref, b4_ref, b0_ref, query, mid_keys, mid_values, resid_ref, qkv_ref, out_w_ref,
+    out_b_ref, out_ref, far_keys, far_values, scores, mixed,
 ):
-    blocks, width, frames, chans = keys.shape
-    near = blocks * frames
+    mids, width, frames, chans = mid_keys.shape
+    near = (mids + 2) * frames
     stack = HEADS * frames
-
-    def by_cell(product):
-        return product.astype(BF16).astype(F32).reshape(width, frames, chans)
-
-    query[...] = by_cell(dot(b2_ref[...], qkv_ref[:, :chans]))
-    for b, ref in enumerate((b0_ref, b1_ref, b2_ref, b3_ref, b4_ref)):
-        keys[b] = by_cell(dot(ref[...], qkv_ref[:, chans : 2 * chans]))
-        values[b] = by_cell(dot(ref[...], qkv_ref[:, 2 * chans :]))
+    shape = (width, frames, chans)
+    for b, ref in enumerate((b0_ref, b4_ref)):
+        far_keys[b] = by_cell(dot(ref[...], qkv_ref[:, chans : 2 * chans]), shape)
+        far_values[b] = by_cell(dot(ref[...], qkv_ref[:, 2 * chans :]), shape)
+
+    def at_cell(far, mid, c):
+        blocks = [far[0, c]] + [mid[b, c] for b in range(mids)] + [far[1, c]]
+        return jnp.concatenate(blocks, axis=0).astype(BF16)
+
     window = iota((1, LANES), 1)
     start, starts = jnp.int32(0), jnp.where(window == 0, 0, -(1 << 20))
     for w in range(gaps_ref.shape[0]):
@@ -141,7 +155,7 @@
     own = head_of.astype(F32)
     for c in range(width):
         spread = (query[c][None] * own).reshape(stack, chans).astype(BF16)
-        key = keys[:, c].reshape(near, chans).astype(BF16)
+        key = at_cell(far_keys, mid_keys, c)
         scores[c] = lax.dot_general(spread, key, NT, preferred_element_type=F32)
     flat = width * stack
     expo = jnp.exp(scores[...].reshape(flat, near) * HEAD_DIM ** (-0.5))
@@ -159,7 +173,7 @@
     back = split_dot(coef, NT)
     scores[...] = (expo * back).reshape(width, stack, near)
     for c in range(width):
-        value = values[:, c].reshape(near, chans).astype(BF16)
+        value = at_cell(far_values, mid_values, c)
         product = dot(scores[c].astype(BF16), value).reshape(HEADS, frames, chans)
         mixed[c] = jnp.sum(jnp.where(head_of, product, 0.0), axis=0)
     joined = mixed[...].reshape(width * frames, chans).astype(BF16)
@@ -209,7 +223,18 @@
         out_specs=[VMEM] * 2,
         compiler_params=GRANT,
     )(on_chip(parts), row, ln_gain, ln_bias)
-    near = [passed(norm, by) for by in (2, 1)] + [norm] + [passed(norm, by) for by in (-1, -2)]
+    b3, b1 = passed(norm, -1), passed(norm, 1)
+    b4, b0 = passed(b3, -1), passed(b1, 1)
+    qkv = on_chip(qkv_weight)
+    own = jax.ShapeDtypeStruct((width, frames, chans), F32)
+    mid = jax.ShapeDtypeStruct((3, width, frames, chans), F32)
+    early = pl.pallas_call(
+        early_kernel,
+        out_shape=[own, mid, mid],
+        in_specs=[VMEM] * 4,
+        out_specs=[VMEM] * 3,
+        compiler_params=GRANT,
+    )(on_chip(b1), norm, on_chip(b3), qkv)
     out = pl.pallas_call(
         attend_kernel,
         out_shape=jax.ShapeDtypeStruct((frames, width, chans), BF16),
@@ -217,13 +242,15 @@
         out_specs=VMEM,
         compiler_params=GRANT,
         scratch_shapes=[
-            pltpu.VMEM((5, width, frames, chans), F32),
-            pltpu.VMEM((5, width, frames, chans), F32),
-            pltpu.VMEM((width, frames, chans), F32),
+            pltpu.VMEM((2, width, frames, chans), F32),
+            pltpu.VMEM((2, width, frames, chans), F32),
             pltpu.VMEM((width, HEADS * frames, 5 * frames), F32),
             pltpu.VMEM((width, frames, chans), F32),
         ],
-    )(window_gaps, *[on_chip(n) for n in near], resid, on_chip(qkv_weight), on_chip(out_weight), out_bias)
+    )(
+        window_gaps, on_chip(b4), on_chip(b0), *[on_chip(n) for n in early], on_chip(resid), qkv,
+        on_chip(out_weight), out_bias,
+    )
     return out.reshape(frames, 1, width, chans)
 
 

time: 89.5 us -> 85.2 us (0.952)
  waiting for transfers between devices: 13.4 us -> 3.24 us
  starting transfers between devices: 11 us -> 16.2 us
    ppermute x4, waiting for transfers between devices: 13.4 us -> 3.23 us  [passed(): return lax.ppermute(shard, 'frames', pairs)]
    ppermute x4, starting transfers between devices: 6.57 us -> 11.8 us  [passed(): return lax.ppermute(shard, 'frames', pairs)]
    pallas_call x0 -> x1, Pallas kernels: none -> 1.3 us  [on_device(): pl.pallas_call(early_kernel, out_shape=[own, mid, mid], in_specs=[VMEM] *...]
    pallas_call x1, Pallas kernels: 5.25 us -> 4.08 us  [on_device(): pl.pallas_call(attend_kernel, out_shape=jax.ShapeDtypeStruct((frames, wid...]
  transfers between devices with their start and end apart: 5 -> 5, of which waited for: 4 -> 2; matrix products, arithmetic and copies ran while one was open for 0% -> 0% of each run, Pallas kernels for 0% -> 2%
where the time goes in v3:
time: 85.2 us; the launch traced here: 84.2 us
  blocking collectives  52.2 us (61%)
  starting transfers between devices  16.2 us (19%)
  Pallas kernels  10.1 us (12%)
  waiting for transfers between devices  3.24 us (4%)
  local copies, waits for them, and re-layouts  2.27 us (3%)
    all_gather x1, blocking collectives, on_device(): weight = lax.all_gather(conv_weight.T, 'frames', axis=0, tiled=False)  41.3 us
    ppermute x4, starting transfers between devices, passed(): return lax.ppermute(shard, 'frames', pairs)  11.8 us
    all_to_all x1, blocking collectives, on_device(): parts = lax.all_to_all(parts, 'height', 0, 0, tiled=True)  11 us
    all_to_all x1, starting transfers between devices, on_device(): whole = lax.all_to_all(copies, 'height', 0, 0, tiled=True)  4.43 us
    pallas_call x1, Pallas kernels, on_device(): pl.pallas_call(conv_kernel, out_shape=jax.ShapeDtypeStruct((bands, outs,...  4.27 us
    pallas_call x1, Pallas kernels, on_device(): pl.pallas_call(attend_kernel, out_shape=jax.ShapeDtypeStruct((frames, wid...  4.08 us
    ppermute x4, waiting for transfers between devices, passed(): return lax.ppermute(shard, 'frames', pairs)  3.23 us
    broadcast_in_dim x1, local copies, waits for them, and re-layouts, on_device(): copies = jnp.broadcast_to(row[None], (bands, frames, width, chans))  2.13 us
  transfers between devices with their start and end apart: 5, of which 2 were waited for; matrix products, arithmetic and copies ran while one was open for 0% of the time, Pallas kernels for 2%

profile of v3, /device:TPU:24, one launch (start us, length us, event | category | flops | bytes accessed | tf_op | source)
XLA Modules:
  0.0 84.2 jit_solution(12311038351579316795)
XLA Ops:
  0.0 0.0 copy-start
  0.0 2.1 %broadcast_in_dim.11 = bf16[8,8,16,640]{3,2,1,0:T(8,128)(2,1)} broadcast(bf16[8,16,640]{2,1,0:T(8,128)(2,1)} %bitcast.9), dimensions={1,2,3} | broadcast | bytes 1474560 | tf_op jit(solution)/shard_map/broadcast_in_dim | solution.py:202
  2.1 0.0 copy-start.10
  2.1 0.0 copy-start.4
  2.1 0.0 copy-start.5
  2.1 4.4 %all-to-all-start = ((bf16[8,8,16,640]{3,2,1,0:T(8,128)(2,1)}), bf16[8,8,16,640]{3,2,1,0:T(8,128)(2,1)S(1)}, u32[]{:S(2)}, u32[]{:S(2)}) async-start(bf16[8,8,16,640]{3,2,1,0:T(8,128)(2,1)} %broadcast_in_dim.11), calls=%async_computation | async-start | bytes 2621440 | tf_op jit(solution)/shard_map/all_to_all | solution.py:203
  6.6 0.0 copy-done
  6.6 0.1 dynamic-slice_bitcast_fusion.cbias_ref
  6.7 0.0 copy-done.10
  6.7 41.3 %all-gather = bf16[1280,360]{1,0:T(8,128)(2,1)S(1)} all-gather(bf16[80,360]{1,0:T(8,128)(2,1)S(1)} %bitcast.11), channel_id=2, replica_groups=mesh['dp'=4,'frames'=16,'height'=8] {'frames'}, dimensions={0}, use_global_device_ids=true | all-gather | bytes 979200 | tf_op jit(solution)/shard_map/all_gather | solution.py:204
  47.9 0.0 all-to-all-done.cells_ref
  47.9 0.0 copy-done.4
  47.9 0.0 copy-done.5
  47.9 0.0 copy-start.3
  48.0 0.0 copy-start.6
  48.0 0.0 copy-start.7
  48.0 0.0 copy-start.1
  48.0 4.3 %shard_map.109 = bf16[8,80,128]{2,1,0:T(8,128)(2,1)S(1)} custom-call(bf16[8,8,16,640]{3,2,1,0:T(8,128)(2,1)S(1)} %all-to-all-done.cells_ref, bf16[16,80,360]{2,1,0:T(8,128)(2,1)S(1)} %bitcast.8, f32[640]{0:T(1024)S(1)} %copy-done.4, f32[640]{0:T(1024)S(1)} %copy-done.5, f32[1,80]{1,0:T(1,128)S(1)} %dynamic-slice_bitcast_fusion.cbias_ref), custom_call_target="tpu_custom_call" | custom-call | tf_op jit(solution)/shard_map/pallas_call | solution.py:206
  52.3 11.0 %all_to_all.10.part_ref = bf16[8,80,128]{2,1,0:T(8,128)(2,1)S(1)} all-to-all(bf16[8,80,128]{2,1,0:T(8,128)(2,1)S(1)} %shard_map.109), channel_id=1, replica_groups=mesh['dp'=4,'frames'=16,'height'=8] {'height'}, dimensions={0} | all-to-all | bytes 327680 | tf_op jit(solution)/shard_map/all_to_all | solution.py:218
  63.2 0.0 copy-done.3
  63.2 0.0 copy-done.6
  63.2 0.0 copy-done.7
  63.2 0.5 shard_map.110
  63.7 0.0 copy-start.2
  63.7 0.0 copy-start.8
  63.7 0.0 copy-start.9
  63.8 1.4 %collective-permute-start = (bf16[128,640]{1,0:T(8,128)(2,1)S(1)}, bf16[128,640]{1,0:T(8,128)(2,1)S(1)}, u32[]{:S(2)}, u32[]{:S(2)}) collective-permute-start(bf16[128,640]{1,0:T(8,128)(2,1)S(1)} %get-tuple-element.10.norm_ref), channel_id=1, source_target_pairs={{8,0},{16,8},{24,16},{32,24},{40,32},{48,40},{56,48},{64,56},{72,6... | collective-permute-start | bytes 491528 | tf_op jit(solution)/shard_map/ppermute | solution.py:189
  65.2 4.6 %collective-permute-start.2 = (bf16[128,640]{1,0:T(8,128)(2,1)S(1)}, bf16[128,640]{1,0:T(8,128)(2,1)S(1)}, u32[]{:S(2)}, u32[]{:S(2)}) collective-permute-start(bf16[128,640]{1,0:T(8,128)(2,1)S(1)} %get-tuple-element.10.norm_ref), channel_id=1, source_target_pairs={{0,8},{8,16},{16,24},{24,32},{32,40},{40,48},{48,56},{56,64},{64,7... | collective-permute-start | bytes 491528 | tf_op jit(solution)/shard_map/ppermute | solution.py:189
  69.8 1.7 %collective-permute-done.after_ref = bf16[128,640]{1,0:T(8,128)(2,1)S(1)} collective-permute-done((bf16[128,640]{1,0:T(8,128)(2,1)S(1)}, bf16[128,640]{1,0:T(8,128)(2,1)S(1)}, u32[]{:S(2)}, u32[]{:S(2)}) %collective-permute-start) | collective-permute-done | bytes 163872 | tf_op jit(solution)/shard_map/ppermute | solution.py:189
  71.5 1.3 %collective-permute-start.1 = (bf16[128,640]{1,0:T(8,128)(2,1)S(1)}, bf16[128,640]{1,0:T(8,128)(2,1)S(1)}, u32[]{:S(2)}, u32[]{:S(2)}) collective-permute-start(bf16[128,640]{1,0:T(8,128)(2,1)S(1)} %collective-permute-done.after_ref), channel_id=1, source_target_pairs={{8,0},{16,8},{24,16},{32,24},{40,32},{48,40},{56,48},{64,56},{72,6... | collective-permute-start | bytes 491528 | tf_op jit(solution)/shard_map/ppermute | solution.py:189
  72.8 0.0 collective-permute-done.2.before_ref
  72.8 4.6 %collective-permute-start.3 = (bf16[128,640]{1,0:T(8,128)(2,1)S(1)}, bf16[128,640]{1,0:T(8,128)(2,1)S(1)}, u32[]{:S(2)}, u32[]{:S(2)}) collective-permute-start(bf16[128,640]{1,0:T(8,128)(2,1)S(1)} %collective-permute-done.2.before_ref), channel_id=1, source_target_pairs={{0,8},{8,16},{16,24},{24,32},{32,40},{40,48},{48,56},{56,64},{64,7... | collective-permute-start | bytes 491528 | tf_op jit(solution)/shard_map/ppermute | solution.py:189
  77.4 0.0 copy-done.1
  77.4 1.3 %shard_map.111 = (f32[16,8,640]{2,1,0:T(8,128)S(1)}, f32[3,16,8,640]{3,2,1,0:T(8,128)S(1)}, f32[3,16,8,640]{3,2,1,0:T(8,128)S(1)}) custom-call(bf16[128,640]{1,0:T(8,128)(2,1)S(1)} %collective-permute-done.2.before_ref, bf16[128,640]{1,0:T(8,128)(2,1)S(1)} %get-tuple-element.10.norm_ref, bf16[128,640]{1,0:T(8,128)(2,1)S(1)} %collective-permute-done.after_ref, ...), custom_call_target="tpu_custom_call" | custom-call | tf_op jit(solution)/shard_map/pallas_call | solution.py:231
  78.7 0.0 collective-permute-done.1.b4_ref
  78.7 1.5 %collective-permute-done.3.b0_ref = bf16[128,640]{1,0:T(8,128)(2,1)S(1)} collective-permute-done((bf16[128,640]{1,0:T(8,128)(2,1)S(1)}, bf16[128,640]{1,0:T(8,128)(2,1)S(1)}, u32[]{:S(2)}, u32[]{:S(2)}) %collective-permute-start.3) | collective-permute-done | bytes 163872 | tf_op jit(solution)/shard_map/ppermute | solution.py:189
  80.2 0.0 copy-done.2
  80.2 0.0 copy-done.8
  80.2 0.0 copy-done.9
  80.2 4.1 %shard_map.112 = bf16[8,16,640]{2,1,0:T(8,128)(2,1)} custom-call(s32[28]{0:T(128)S(1)} %copy-done.9, bf16[128,640]{1,0:T(8,128)(2,1)S(1)} %collective-permute-done.1.b4_ref, bf16[128,640]{1,0:T(8,128)(2,1)S(1)} %collective-permute-done.3.b0_ref, f32[16,8,640]{2,1,0:T(8,128)S(1)} %get-tuple-element.11.query, ...), custom_call_target="tpu_custom_call" | custom-call | tf_op jit(solution)/shard_map/pallas_call | solution.py:238
Async XLA Ops:
  0.0 6.6 %copy-start = (f32[640]{0:T(1024)S(1)}, f32[640]{0:T(1024)}, u32[]{:S(2)}) copy-start(f32[640]{0:T(1024)} %param.16) | copy-start | bytes 7684
  2.1 4.5 %copy-start.10 = (bf16[360,80]{0,1:T(8,128)(2,1)S(1)}, bf16[360,80]{0,1:T(8,128)(2,1)}, u32[]{:S(2)}) copy-start(bf16[360,80]{0,1:T(8,128)(2,1)} %param.15) | copy-start | bytes 172804
  2.1 45.8 %copy-start.4 = (f32[640]{0:T(1024)S(1)}, f32[640]{0:T(1024)}, u32[]{:S(2)}) copy-start(f32[640]{0:T(1024)} %gain_ref.2) | copy-start | bytes 7684
  2.1 45.8 %copy-start.5 = (f32[640]{0:T(1024)S(1)}, f32[640]{0:T(1024)}, u32[]{:S(2)}) copy-start(f32[640]{0:T(1024)} %bias_ref.2) | copy-start | bytes 7684
  2.1 45.8 %all-to-all-start = ((bf16[8,8,16,640]{3,2,1,0:T(8,128)(2,1)}), bf16[8,8,16,640]{3,2,1,0:T(8,128)(2,1)S(1)}, u32[]{:S(2)}, u32[]{:S(2)}) async-start(bf16[8,8,16,640]{3,2,1,0:T(8,128)(2,1)} %broadcast_in_dim.11), calls=%async_computation | async-start | bytes 2621440 | tf_op jit(solution)/shard_map/all_to_all | solution.py:203
  47.9 15.3 %copy-start.3 = (bf16[8,1,16,640]{3,2,1,0:T(8,128)(2,1)S(1)}, bf16[8,1,16,640]{3,2,1,0:T(8,128)(2,1)}, u32[]{:S(2)}) copy-start(bf16[8,1,16,640]{3,2,1,0:T(8,128)(2,1)} %param.11) | copy-start | bytes 491524
  48.0 15.3 %copy-start.6 = (f32[640]{0:T(1024)S(1)}, f32[640]{0:T(1024)}, u32[]{:S(2)}) copy-start(f32[640]{0:T(1024)} %gain_ref.3) | copy-start | bytes 7684
  48.0 15.3 %copy-start.7 = (f32[640]{0:T(1024)S(1)}, f32[640]{0:T(1024)}, u32[]{:S(2)}) copy-start(f32[640]{0:T(1024)} %bias_ref.3) | copy-start | bytes 7684
  48.0 29.4 %copy-start.1 = (bf16[640,1920]{1,0:T(8,128)(2,1)S(1)}, bf16[640,1920]{1,0:T(8,128)(2,1)}, u32[]{:S(2)}) copy-start(bf16[640,1920]{1,0:T(8,128)(2,1)} %qkv_ref.3) | copy-start | bytes 7372804
  63.7 16.4 %copy-start.2 = (bf16[640,640]{1,0:T(8,128)(2,1)S(1)}, bf16[640,640]{1,0:T(8,128)(2,1)}, u32[]{:S(2)}) copy-start(bf16[640,640]{1,0:T(8,128)(2,1)} %out_w_ref.1) | copy-start | bytes 2457604
  63.7 16.4 %copy-start.8 = (f32[640]{0:T(1024)S(1)}, f32[640]{0:T(1024)}, u32[]{:S(2)}) copy-start(f32[640]{0:T(1024)} %out_b_ref.1) | copy-start | bytes 7684
  63.7 16.4 %copy-start.9 = (s32[28]{0:T(128)S(1)}, s32[28]{0:T(128)}, u32[]{:S(2)}) copy-start(s32[28]{0:T(128)} %gaps_ref.1) | copy-start | bytes 340
  63.8 7.7 %collective-permute-start = (bf16[128,640]{1,0:T(8,128)(2,1)S(1)}, bf16[128,640]{1,0:T(8,128)(2,1)S(1)}, u32[]{:S(2)}, u32[]{:S(2)}) collective-permute-start(bf16[128,640]{1,0:T(8,128)(2,1)S(1)} %get-tuple-element.10.norm_ref), channel_id=1, source_target_pairs={{8,0},{16,8},{24,16},{32,24},{40,32},{48,40},{56,48},{64,56},{72,6... | collective-permute-start | bytes 491528 | tf_op jit(solution)/shard_map/ppermute | solution.py:189
  65.2 7.6 %collective-permute-start.2 = (bf16[128,640]{1,0:T(8,128)(2,1)S(1)}, bf16[128,640]{1,0:T(8,128)(2,1)S(1)}, u32[]{:S(2)}, u32[]{:S(2)}) collective-permute-start(bf16[128,640]{1,0:T(8,128)(2,1)S(1)} %get-tuple-element.10.norm_ref), channel_id=1, source_target_pairs={{0,8},{8,16},{16,24},{24,32},{32,40},{40,48},{48,56},{56,64},{64,7... | collective-permute-start | bytes 491528 | tf_op jit(solution)/shard_map/ppermute | solution.py:189
  71.5 7.2 %collective-permute-start.1 = (bf16[128,640]{1,0:T(8,128)(2,1)S(1)}, bf16[128,640]{1,0:T(8,128)(2,1)S(1)}, u32[]{:S(2)}, u32[]{:S(2)}) collective-permute-start(bf16[128,640]{1,0:T(8,128)(2,1)S(1)} %collective-permute-done.after_ref), channel_id=1, source_target_pairs={{8,0},{16,8},{24,16},{32,24},{40,32},{48,40},{56,48},{64,56},{72,6... | collective-permute-start | bytes 491528 | tf_op jit(solution)/shard_map/ppermute | solution.py:189
  72.8 7.4 %collective-permute-start.3 = (bf16[128,640]{1,0:T(8,128)(2,1)S(1)}, bf16[128,640]{1,0:T(8,128)(2,1)S(1)}, u32[]{:S(2)}, u32[]{:S(2)}) collective-permute-start(bf16[128,640]{1,0:T(8,128)(2,1)S(1)} %collective-permute-done.2.before_ref), channel_id=1, source_target_pairs={{0,8},{8,16},{16,24},{24,32},{32,40},{40,48},{48,56},{56,64},{64,7... | collective-permute-start | bytes 491528 | tf_op jit(solution)/shard_map/ppermute | solution.py:189

commit v4 on v3

--- a/solution.py
+++ b/solution.py
@@ -26,10 +26,6 @@
 
 def dot(a, b):
     return jnp.dot(a, b, preferred_element_type=F32)
-
-
-def exact_dot(a, b, dims=(((1,), (0,)), ((), ()))):
-    return lax.dot_general(a, b, dims, precision=lax.Precision.HIGHEST, preferred_element_type=F32)
 
 
 def iota(shape, dim):
@@ -44,22 +40,41 @@
     for z in range(chunks):
         taps[:, z * chunk : (z + 1) * chunk] = weight_ref[z]
     groups = (iota((chans, LANES), 0).astype(F32) + 0.5) * (GROUPS / chans)
-    groups = (jnp.floor(groups) == iota((chans, LANES), 1).astype(F32)).astype(F32)
-    count = rows * width * (chans // GROUPS)
-
-    def group_mean(sums):
-        per_group = exact_dot(jnp.concatenate(sums, axis=0), groups) / count
-        return exact_dot(per_group, groups, NT)
-
-    def frame(f):
-        return cells_ref[:, f].reshape(rows * width, chans).astype(F32)
-
-    mean = group_mean([jnp.sum(frame(f), axis=0, keepdims=True) for f in range(frames)])
-    sums = []
+    groups = jnp.floor(groups) == iota((chans, LANES), 1).astype(F32)
+    groups = groups.astype(F32).astype(BF16)
+
+    def pieces_dot(sums, dims):
+        high = sums.astype(BF16)
+        rest = sums - high.astype(F32)
+        middle = rest.astype(BF16)
+        low = (rest - middle.astype(F32)).astype(BF16)
+        parts = jnp.concatenate([high, middle, low], axis=0)
+        parts = lax.dot_general(parts, groups, dims, preferred_element_type=F32)
+        count = sums.shape[0]
+        return parts[:count] + parts[count : 2 * count] + parts[2 * count :]
+
+    def group_mean(values):
+        per_group = pieces_dot(values, (((1,), (0,)), ((), ()))) * (GROUPS / chans)
+        return pieces_dot(per_group, NT)
+
+    pivots, firsts, seconds = [], [], []
     for f in range(frames):
-        centred = frame(f) - mean[f : f + 1]
-        sums.append(jnp.sum(centred * centred, axis=0, keepdims=True))
-    inverse = lax.rsqrt(group_mean(sums) + EPSILON)
+        pivot = cells_ref[0, f].astype(F32)[:1]
+        first = second = jnp.zeros((width, chans), F32)
+        for r in range(rows):
+            away = cells_ref[r, f].astype(F32) - pivot
+            first, second = first + away, second + away * away
+        pivots.append(pivot)
+        firsts.append(jnp.sum(first, axis=0, keepdims=True))
+        seconds.append(jnp.sum(second, axis=0, keepdims=True))
+    cell_count = rows * width
+    first = jnp.concatenate(firsts, axis=0) / cell_count
+    second = jnp.concatenate(seconds, axis=0) / cell_count
+    channel_mean = jnp.concatenate(pivots, axis=0) + first
+    mean = group_mean(channel_mean)
+    between = channel_mean - mean
+    variance = group_mean(jnp.maximum(second - first * first, 0.0) + between * between)
+    inverse = lax.rsqrt(variance + EPSILON)
     scale, bias = inverse * gain_ref[...].reshape(1, chans), bias_ref[...].reshape(1, chans)
     edge = jnp.zeros((frames, width, chans), BF16)
     padded[0] = edge
@@ -71,16 +86,15 @@
             padded[r + 1, f] = (normed + normed * jnp.tanh(normed)).astype(BF16)
     flat = rows * frames * width
     column = lax.rem(iota((flat, 1), 0), width)
-    total = None
-    for row in range(3):
-        tap = [taps[:, (3 * row + col) * chans : (3 * row + col + 1) * chans] for col in range(3)]
-        term = lax.dot_general(
-            padded[row : row + rows].reshape(flat, chans),
-            jnp.concatenate(tap, axis=0),
-            NT,
-            preferred_element_type=F32,
-        )
-        total = term if total is None else total + term
+    near = [padded[row : row + rows].reshape(flat, chans) for row in range(3)]
+    tap = [taps[:, i * chans : (i + 1) * chans] for i in range(9)]
+    tap = [jnp.concatenate(tap[3 * row : 3 * row + 3], axis=0) for row in range(3)]
+    total = lax.dot_general(
+        jnp.concatenate(near, axis=1),
+        jnp.concatenate(tap, axis=1),
+        NT,
+        preferred_element_type=F32,
+    )
     shifted[8 : 8 + flat] = total
     before = jnp.where(column == 0, 0.0, shifted[7 : 7 + flat, :outs])
     after = jnp.where(column == width - 1, 0.0, shifted[9 : 9 + flat, 2 * outs :])

time: 85.2 us -> 84.4 us (level)
    pallas_call x1, Pallas kernels: 4.27 us -> 3.41 us  [on_device(): pl.pallas_call(conv_kernel, out_shape=jax.ShapeDtypeStruct((bands, outs,...]
where the time goes in v4:
time: 84.4 us; the launch traced here: 83.4 us
  blocking collectives  52.2 us (62%)
  starting transfers between devices  16.2 us (19%)
  Pallas kernels  9.28 us (11%)
  waiting for transfers between devices  3.24 us (4%)
  local copies, waits for them, and re-layouts  2.27 us (3%)
    all_gather x1, blocking collectives, on_device(): weight = lax.all_gather(conv_weight.T, 'frames', axis=0, tiled=False)  41.3 us
    ppermute x4, starting transfers between devices, passed(): return lax.ppermute(shard, 'frames', pairs)  11.8 us
    all_to_all x1, blocking collectives, on_device(): parts = lax.all_to_all(parts, 'height', 0, 0, tiled=True)  11 us
    all_to_all x1, starting transfers between devices, on_device(): whole = lax.all_to_all(copies, 'height', 0, 0, tiled=True)  4.43 us
    pallas_call x1, Pallas kernels, on_device(): pl.pallas_call(attend_kernel, out_shape=jax.ShapeDtypeStruct((frames, wid...  4.08 us
    pallas_call x1, Pallas kernels, on_device(): pl.pallas_call(conv_kernel, out_shape=jax.ShapeDtypeStruct((bands, outs,...  3.41 us
    ppermute x4, waiting for transfers between devices, passed(): return lax.ppermute(shard, 'frames', pairs)  3.24 us
    broadcast_in_dim x1, local copies, waits for them, and re-layouts, on_device(): copies = jnp.broadcast_to(row[None], (bands, frames, width, chans))  2.13 us
  transfers between devices with their start and end apart: 5, of which 2 were waited for; matrix products, arithmetic and copies ran while one was open for 0% of the time, Pallas kernels for 2%

profile of v4, /device:TPU:24, one launch (start us, length us, event | category | flops | bytes accessed | tf_op | source)
XLA Modules:
  0.0 83.4 jit_solution(12106391405428584358)
XLA Ops:
  0.0 0.0 copy-start
  0.0 2.1 %broadcast_in_dim.11 = bf16[8,8,16,640]{3,2,1,0:T(8,128)(2,1)} broadcast(bf16[8,16,640]{2,1,0:T(8,128)(2,1)} %bitcast.9), dimensions={1,2,3} | broadcast | bytes 1474560 | tf_op jit(solution)/shard_map/broadcast_in_dim | solution.py:216
  2.1 0.0 copy-start.10
  2.1 0.0 copy-start.4
  2.1 0.0 copy-start.5
  2.1 4.4 %all-to-all-start = ((bf16[8,8,16,640]{3,2,1,0:T(8,128)(2,1)}), bf16[8,8,16,640]{3,2,1,0:T(8,128)(2,1)S(1)}, u32[]{:S(2)}, u32[]{:S(2)}) async-start(bf16[8,8,16,640]{3,2,1,0:T(8,128)(2,1)} %broadcast_in_dim.11), calls=%async_computation | async-start | bytes 2621440 | tf_op jit(solution)/shard_map/all_to_all | solution.py:217
  6.6 0.0 copy-done
  6.6 0.1 dynamic-slice_bitcast_fusion.cbias_ref
  6.7 0.0 copy-done.10
  6.7 41.3 %all-gather = bf16[1280,360]{1,0:T(8,128)(2,1)S(1)} all-gather(bf16[80,360]{1,0:T(8,128)(2,1)S(1)} %bitcast.11), channel_id=2, replica_groups=mesh['dp'=4,'frames'=16,'height'=8] {'frames'}, dimensions={0}, use_global_device_ids=true | all-gather | bytes 979200 | tf_op jit(solution)/shard_map/all_gather | solution.py:218
  47.9 0.0 all-to-all-done.cells_ref
  47.9 0.0 copy-done.4
  47.9 0.0 copy-done.5
  47.9 0.0 copy-start.3
  48.0 0.0 copy-start.6
  48.0 0.0 copy-start.7
  48.0 0.0 copy-start.1
  48.0 3.4 %shard_map.109 = bf16[8,80,128]{2,1,0:T(8,128)(2,1)S(1)} custom-call(bf16[8,8,16,640]{3,2,1,0:T(8,128)(2,1)S(1)} %all-to-all-done.cells_ref, bf16[16,80,360]{2,1,0:T(8,128)(2,1)S(1)} %bitcast.8, f32[640]{0:T(1024)S(1)} %copy-done.4, f32[640]{0:T(1024)S(1)} %copy-done.5, f32[1,80]{1,0:T(1,128)S(1)} %dynamic-slice_bitcast_fusion.cbias_ref), custom_call_target="tpu_custom_call" | custom-call | tf_op jit(solution)/shard_map/pallas_call | solution.py:220
  51.4 11.0 %all_to_all.10.part_ref = bf16[8,80,128]{2,1,0:T(8,128)(2,1)S(1)} all-to-all(bf16[8,80,128]{2,1,0:T(8,128)(2,1)S(1)} %shard_map.109), channel_id=1, replica_groups=mesh['dp'=4,'frames'=16,'height'=8] {'height'}, dimensions={0} | all-to-all | bytes 327680 | tf_op jit(solution)/shard_map/all_to_all | solution.py:232
  62.4 0.0 copy-done.3
  62.4 0.0 copy-done.6
  62.4 0.0 copy-done.7
  62.4 0.5 shard_map.110
  62.9 0.0 copy-start.2
  62.9 0.0 copy-start.8
  62.9 0.0 copy-start.9
  62.9 1.4 %collective-permute-start = (bf16[128,640]{1,0:T(8,128)(2,1)S(1)}, bf16[128,640]{1,0:T(8,128)(2,1)S(1)}, u32[]{:S(2)}, u32[]{:S(2)}) collective-permute-start(bf16[128,640]{1,0:T(8,128)(2,1)S(1)} %get-tuple-element.10.norm_ref), channel_id=1, source_target_pairs={{8,0},{16,8},{24,16},{32,24},{40,32},{48,40},{56,48},{64,56},{72,6... | collective-permute-start | bytes 491528 | tf_op jit(solution)/shard_map/ppermute | solution.py:203
  64.3 4.6 %collective-permute-start.2 = (bf16[128,640]{1,0:T(8,128)(2,1)S(1)}, bf16[128,640]{1,0:T(8,128)(2,1)S(1)}, u32[]{:S(2)}, u32[]{:S(2)}) collective-permute-start(bf16[128,640]{1,0:T(8,128)(2,1)S(1)} %get-tuple-element.10.norm_ref), channel_id=1, source_target_pairs={{0,8},{8,16},{16,24},{24,32},{32,40},{40,48},{48,56},{56,64},{64,7... | collective-permute-start | bytes 491528 | tf_op jit(solution)/shard_map/ppermute | solution.py:203
  68.9 1.7 %collective-permute-done.after_ref = bf16[128,640]{1,0:T(8,128)(2,1)S(1)} collective-permute-done((bf16[128,640]{1,0:T(8,128)(2,1)S(1)}, bf16[128,640]{1,0:T(8,128)(2,1)S(1)}, u32[]{:S(2)}, u32[]{:S(2)}) %collective-permute-start) | collective-permute-done | bytes 163872 | tf_op jit(solution)/shard_map/ppermute | solution.py:203
  70.6 1.3 %collective-permute-start.1 = (bf16[128,640]{1,0:T(8,128)(2,1)S(1)}, bf16[128,640]{1,0:T(8,128)(2,1)S(1)}, u32[]{:S(2)}, u32[]{:S(2)}) collective-permute-start(bf16[128,640]{1,0:T(8,128)(2,1)S(1)} %collective-permute-done.after_ref), channel_id=1, source_target_pairs={{8,0},{16,8},{24,16},{32,24},{40,32},{48,40},{56,48},{64,56},{72,6... | collective-permute-start | bytes 491528 | tf_op jit(solution)/shard_map/ppermute | solution.py:203
  71.9 0.0 collective-permute-done.2.before_ref
  71.9 4.6 %collective-permute-start.3 = (bf16[128,640]{1,0:T(8,128)(2,1)S(1)}, bf16[128,640]{1,0:T(8,128)(2,1)S(1)}, u32[]{:S(2)}, u32[]{:S(2)}) collective-permute-start(bf16[128,640]{1,0:T(8,128)(2,1)S(1)} %collective-permute-done.2.before_ref), channel_id=1, source_target_pairs={{0,8},{8,16},{16,24},{24,32},{32,40},{40,48},{48,56},{56,64},{64,7... | collective-permute-start | bytes 491528 | tf_op jit(solution)/shard_map/ppermute | solution.py:203
  76.5 0.0 copy-done.1
  76.5 1.3 %shard_map.111 = (f32[16,8,640]{2,1,0:T(8,128)S(1)}, f32[3,16,8,640]{3,2,1,0:T(8,128)S(1)}, f32[3,16,8,640]{3,2,1,0:T(8,128)S(1)}) custom-call(bf16[128,640]{1,0:T(8,128)(2,1)S(1)} %collective-permute-done.2.before_ref, bf16[128,640]{1,0:T(8,128)(2,1)S(1)} %get-tuple-element.10.norm_ref, bf16[128,640]{1,0:T(8,128)(2,1)S(1)} %collective-permute-done.after_ref, ...), custom_call_target="tpu_custom_call" | custom-call | tf_op jit(solution)/shard_map/pallas_call | solution.py:245
  77.8 0.0 collective-permute-done.1.b4_ref
  77.8 1.5 %collective-permute-done.3.b0_ref = bf16[128,640]{1,0:T(8,128)(2,1)S(1)} collective-permute-done((bf16[128,640]{1,0:T(8,128)(2,1)S(1)}, bf16[128,640]{1,0:T(8,128)(2,1)S(1)}, u32[]{:S(2)}, u32[]{:S(2)}) %collective-permute-start.3) | collective-permute-done | bytes 163872 | tf_op jit(solution)/shard_map/ppermute | solution.py:203
  79.3 0.0 copy-done.2
  79.3 0.0 copy-done.8
  79.3 0.0 copy-done.9
  79.3 4.1 %shard_map.112 = bf16[8,16,640]{2,1,0:T(8,128)(2,1)} custom-call(s32[28]{0:T(128)S(1)} %copy-done.9, bf16[128,640]{1,0:T(8,128)(2,1)S(1)} %collective-permute-done.1.b4_ref, bf16[128,640]{1,0:T(8,128)(2,1)S(1)} %collective-permute-done.3.b0_ref, f32[16,8,640]{2,1,0:T(8,128)S(1)} %get-tuple-element.11.query, ...), custom_call_target="tpu_custom_call" | custom-call | tf_op jit(solution)/shard_map/pallas_call | solution.py:252
Async XLA Ops:
  0.0 6.6 %copy-start = (f32[640]{0:T(1024)S(1)}, f32[640]{0:T(1024)}, u32[]{:S(2)}) copy-start(f32[640]{0:T(1024)} %param.16) | copy-start | bytes 7684
  2.1 4.5 %copy-start.10 = (bf16[360,80]{0,1:T(8,128)(2,1)S(1)}, bf16[360,80]{0,1:T(8,128)(2,1)}, u32[]{:S(2)}) copy-start(bf16[360,80]{0,1:T(8,128)(2,1)} %param.15) | copy-start | bytes 172804
  2.1 45.8 %copy-start.4 = (f32[640]{0:T(1024)S(1)}, f32[640]{0:T(1024)}, u32[]{:S(2)}) copy-start(f32[640]{0:T(1024)} %gain_ref.2) | copy-start | bytes 7684
  2.1 45.8 %copy-start.5 = (f32[640]{0:T(1024)S(1)}, f32[640]{0:T(1024)}, u32[]{:S(2)}) copy-start(f32[640]{0:T(1024)} %bias_ref.2) | copy-start | bytes 7684
  2.1 45.8 %all-to-all-start = ((bf16[8,8,16,640]{3,2,1,0:T(8,128)(2,1)}), bf16[8,8,16,640]{3,2,1,0:T(8,128)(2,1)S(1)}, u32[]{:S(2)}, u32[]{:S(2)}) async-start(bf16[8,8,16,640]{3,2,1,0:T(8,128)(2,1)} %broadcast_in_dim.11), calls=%async_computation | async-start | bytes 2621440 | tf_op jit(solution)/shard_map/all_to_all | solution.py:217
  47.9 14.4 %copy-start.3 = (bf16[8,1,16,640]{3,2,1,0:T(8,128)(2,1)S(1)}, bf16[8,1,16,640]{3,2,1,0:T(8,128)(2,1)}, u32[]{:S(2)}) copy-start(bf16[8,1,16,640]{3,2,1,0:T(8,128)(2,1)} %param.11) | copy-start | bytes 491524
  48.0 14.4 %copy-start.6 = (f32[640]{0:T(1024)S(1)}, f32[640]{0:T(1024)}, u32[]{:S(2)}) copy-start(f32[640]{0:T(1024)} %gain_ref.3) | copy-start | bytes 7684
  48.0 14.4 %copy-start.7 = (f32[640]{0:T(1024)S(1)}, f32[640]{0:T(1024)}, u32[]{:S(2)}) copy-start(f32[640]{0:T(1024)} %bias_ref.3) | copy-start | bytes 7684
  48.0 28.5 %copy-start.1 = (bf16[640,1920]{1,0:T(8,128)(2,1)S(1)}, bf16[640,1920]{1,0:T(8,128)(2,1)}, u32[]{:S(2)}) copy-start(bf16[640,1920]{1,0:T(8,128)(2,1)} %qkv_ref.3) | copy-start | bytes 7372804
  62.9 16.4 %copy-start.2 = (bf16[640,640]{1,0:T(8,128)(2,1)S(1)}, bf16[640,640]{1,0:T(8,128)(2,1)}, u32[]{:S(2)}) copy-start(bf16[640,640]{1,0:T(8,128)(2,1)} %out_w_ref.1) | copy-start | bytes 2457604
  62.9 16.4 %copy-start.8 = (f32[640]{0:T(1024)S(1)}, f32[640]{0:T(1024)}, u32[]{:S(2)}) copy-start(f32[640]{0:T(1024)} %out_b_ref.1) | copy-start | bytes 7684
  62.9 16.4 %copy-start.9 = (s32[28]{0:T(128)S(1)}, s32[28]{0:T(128)}, u32[]{:S(2)}) copy-start(s32[28]{0:T(128)} %gaps_ref.1) | copy-start | bytes 340
  62.9 7.7 %collective-permute-start = (bf16[128,640]{1,0:T(8,128)(2,1)S(1)}, bf16[128,640]{1,0:T(8,128)(2,1)S(1)}, u32[]{:S(2)}, u32[]{:S(2)}) collective-permute-start(bf16[128,640]{1,0:T(8,128)(2,1)S(1)} %get-tuple-element.10.norm_ref), channel_id=1, source_target_pairs={{8,0},{16,8},{24,16},{32,24},{40,32},{48,40},{56,48},{64,56},{72,6... | collective-permute-start | bytes 491528 | tf_op jit(solution)/shard_map/ppermute | solution.py:203
  64.3 7.6 %collective-permute-start.2 = (bf16[128,640]{1,0:T(8,128)(2,1)S(1)}, bf16[128,640]{1,0:T(8,128)(2,1)S(1)}, u32[]{:S(2)}, u32[]{:S(2)}) collective-permute-start(bf16[128,640]{1,0:T(8,128)(2,1)S(1)} %get-tuple-element.10.norm_ref), channel_id=1, source_target_pairs={{0,8},{8,16},{16,24},{24,32},{32,40},{40,48},{48,56},{56,64},{64,7... | collective-permute-start | bytes 491528 | tf_op jit(solution)/shard_map/ppermute | solution.py:203
  70.6 7.2 %collective-permute-start.1 = (bf16[128,640]{1,0:T(8,128)(2,1)S(1)}, bf16[128,640]{1,0:T(8,128)(2,1)S(1)}, u32[]{:S(2)}, u32[]{:S(2)}) collective-permute-start(bf16[128,640]{1,0:T(8,128)(2,1)S(1)} %collective-permute-done.after_ref), channel_id=1, source_target_pairs={{8,0},{16,8},{24,16},{32,24},{40,32},{48,40},{56,48},{64,56},{72,6... | collective-permute-start | bytes 491528 | tf_op jit(solution)/shard_map/ppermute | solution.py:203
  71.9 7.4 %collective-permute-start.3 = (bf16[128,640]{1,0:T(8,128)(2,1)S(1)}, bf16[128,640]{1,0:T(8,128)(2,1)S(1)}, u32[]{:S(2)}, u32[]{:S(2)}) collective-permute-start(bf16[128,640]{1,0:T(8,128)(2,1)S(1)} %collective-permute-done.2.before_ref), channel_id=1, source_target_pairs={{0,8},{8,16},{16,24},{24,32},{32,40},{40,48},{48,56},{56,64},{64,7... | collective-permute-start | bytes 491528 | tf_op jit(solution)/shard_map/ppermute | solution.py:203

commit v5 on v4

--- a/solution.py
+++ b/solution.py
@@ -33,7 +33,7 @@
 
 
 def conv_kernel(
-    cells_ref, weight_ref, gain_ref, bias_ref, cbias_ref, out_ref, padded, taps, shifted
+    cells_ref, weight_ref, gain_ref, bias_ref, cbias_ref, out_ref, padded, taps
 ):
     rows, frames, width, chans = cells_ref.shape
     chunks, outs, chunk = weight_ref.shape
@@ -85,23 +85,24 @@
             normed = 0.5 * (normed * scale[f : f + 1] + bias)
             padded[r + 1, f] = (normed + normed * jnp.tanh(normed)).astype(BF16)
     flat = rows * frames * width
-    column = lax.rem(iota((flat, 1), 0), width)
     near = [padded[row : row + rows].reshape(flat, chans) for row in range(3)]
     tap = [taps[:, i * chans : (i + 1) * chans] for i in range(9)]
     tap = [jnp.concatenate(tap[3 * row : 3 * row + 3], axis=0) for row in range(3)]
     total = lax.dot_general(
+        jnp.concatenate(tap, axis=1),
         jnp.concatenate(near, axis=1),
-        jnp.concatenate(tap, axis=1),
         NT,
         preferred_element_type=F32,
     )
-    shifted[8 : 8 + flat] = total
-    before = jnp.where(column == 0, 0.0, shifted[7 : 7 + flat, :outs])
-    after = jnp.where(column == width - 1, 0.0, shifted[9 : 9 + flat, 2 * outs :])
-    result = total[:, outs : 2 * outs] + before + after + cbias_ref[...]
-    result = result.reshape(rows, frames * width, outs)
+    lanes = frames * width
+    column = lax.rem(iota((1, lanes), 1), width)
     for r in range(rows):
-        out_ref[r] = result[r].T.astype(BF16)
+        left, middle, right = [
+            total[col * outs : (col + 1) * outs, r * lanes : (r + 1) * lanes] for col in range(3)
+        ]
+        left = jnp.where(column == 0, 0.0, pltpu.roll(left, 1, 1))
+        right = jnp.where(column == width - 1, 0.0, pltpu.roll(right, lanes - 1, 1))
+        out_ref[r] = (middle + left + right + cbias_ref[...]).astype(BF16)
 
 
 def swap_matrix(frames, width, back):
@@ -216,7 +217,7 @@
     copies = jnp.broadcast_to(row[None], (bands, frames, width, chans))
     whole = lax.all_to_all(copies, "height", 0, 0, tiled=True)
     weight = lax.all_gather(conv_weight.T, "frames", axis=0, tiled=False)
-    cbias = lax.dynamic_slice_in_dim(conv_bias, place * outs, outs)[None]
+    cbias = lax.dynamic_slice_in_dim(conv_bias, place * outs, outs)[:, None]
     parts = pl.pallas_call(
         conv_kernel,
         out_shape=jax.ShapeDtypeStruct((bands, outs, cells), BF16),
@@ -226,7 +227,6 @@
         scratch_shapes=[
             pltpu.VMEM((bands + 2, frames, width, chans), BF16),
             pltpu.VMEM((outs, 9 * chans), BF16),
-            pltpu.VMEM((bands * cells + 16, 3 * outs), F32),
         ],
     )(on_chip(whole), on_chip(weight), gn_gain, gn_bias, cbias)
     parts = lax.all_to_all(parts, "height", 0, 0, tiled=True)

time: 84.4 us -> 83.8 us (level)
  no operation moved by 1% of the time
where the time goes in v5:
time: 83.8 us; the launch traced here: 82.9 us
  blocking collectives  52.2 us (62%)
  starting transfers between devices  16.2 us (19%)
  Pallas kernels  8.64 us (10%)
  waiting for transfers between devices  3.23 us (4%)
  local copies, waits for them, and re-layouts  2.37 us (3%)
    all_gather x1, blocking collectives, on_device(): weight = lax.all_gather(conv_weight.T, 'frames', axis=0, tiled=False)  41.3 us
    ppermute x4, starting transfers between devices, passed(): return lax.ppermute(shard, 'frames', pairs)  11.8 us
    all_to_all x1, blocking collectives, on_device(): parts = lax.all_to_all(parts, 'height', 0, 0, tiled=True)  11 us
    all_to_all x1, starting transfers between devices, on_device(): whole = lax.all_to_all(copies, 'height', 0, 0, tiled=True)  4.43 us
    pallas_call x1, Pallas kernels, on_device(): pl.pallas_call(attend_kernel, out_shape=jax.ShapeDtypeStruct((frames, wid...  4.08 us
    ppermute x4, waiting for transfers between devices, passed(): return lax.ppermute(shard, 'frames', pairs)  3.23 us
    pallas_call x1, Pallas kernels, on_device(): pl.pallas_call(conv_kernel, out_shape=jax.ShapeDtypeStruct((bands, outs,...  2.78 us
    broadcast_in_dim x1, local copies, waits for them, and re-layouts, on_device(): copies = jnp.broadcast_to(row[None], (bands, frames, width, chans))  2.13 us
  transfers between devices with their start and end apart: 5, of which 2 were waited for; matrix products, arithmetic and copies ran while one was open for 0% of the time, Pallas kernels for 2%

profile of v5, /device:TPU:24, one launch (start us, length us, event | category | flops | bytes accessed | tf_op | source)
XLA Modules:
  0.0 82.9 jit_solution(18374148781113937444)
XLA Ops:
  0.0 0.0 copy-start
  0.0 2.1 %broadcast_in_dim.11 = bf16[8,8,16,640]{3,2,1,0:T(8,128)(2,1)} broadcast(bf16[8,16,640]{2,1,0:T(8,128)(2,1)} %bitcast.9), dimensions={1,2,3} | broadcast | bytes 1474560 | tf_op jit(solution)/shard_map/broadcast_in_dim | solution.py:217
  2.1 0.0 copy-start.10
  2.1 0.0 copy-start.4
  2.1 0.0 copy-start.5
  2.1 4.4 %all-to-all-start = ((bf16[8,8,16,640]{3,2,1,0:T(8,128)(2,1)}), bf16[8,8,16,640]{3,2,1,0:T(8,128)(2,1)S(1)}, u32[]{:S(2)}, u32[]{:S(2)}) async-start(bf16[8,8,16,640]{3,2,1,0:T(8,128)(2,1)} %broadcast_in_dim.11), calls=%async_computation | async-start | bytes 2621440 | tf_op jit(solution)/shard_map/all_to_all | solution.py:218
  6.6 0.0 copy-done
  6.6 0.1 dynamic-slice_bitcast_fusion
  6.7 0.1 copy.12.cbias_ref
  6.8 0.0 copy-done.10
  6.8 41.3 %all-gather = bf16[1280,360]{1,0:T(8,128)(2,1)S(1)} all-gather(bf16[80,360]{1,0:T(8,128)(2,1)S(1)} %bitcast.11), channel_id=2, replica_groups=mesh['dp'=4,'frames'=16,'height'=8] {'frames'}, dimensions={0}, use_global_device_ids=true | all-gather | bytes 979200 | tf_op jit(solution)/shard_map/all_gather | solution.py:219
  48.0 0.0 all-to-all-done.cells_ref
  48.1 0.0 copy-done.4
  48.1 0.0 copy-done.5
  48.1 0.0 copy-start.3
  48.1 0.0 copy-start.6
  48.1 0.0 copy-start.7
  48.1 0.0 copy-start.1
  48.1 2.8 %shard_map.109 = bf16[8,80,128]{2,1,0:T(8,128)(2,1)S(1)} custom-call(bf16[8,8,16,640]{3,2,1,0:T(8,128)(2,1)S(1)} %all-to-all-done.cells_ref, bf16[16,80,360]{2,1,0:T(8,128)(2,1)S(1)} %bitcast.8, f32[640]{0:T(1024)S(1)} %copy-done.4, f32[640]{0:T(1024)S(1)} %copy-done.5, f32[80,1]{1,0:T(8,128)S(1)} %copy.12.cbias_ref), custom_call_target="tpu_custom_call" | custom-call | tf_op jit(solution)/shard_map/pallas_call | solution.py:221
  50.9 11.0 %all_to_all.10.part_ref = bf16[8,80,128]{2,1,0:T(8,128)(2,1)S(1)} all-to-all(bf16[8,80,128]{2,1,0:T(8,128)(2,1)S(1)} %shard_map.109), channel_id=1, replica_groups=mesh['dp'=4,'frames'=16,'height'=8] {'height'}, dimensions={0} | all-to-all | bytes 327680 | tf_op jit(solution)/shard_map/all_to_all | solution.py:232
  61.8 0.0 copy-done.3
  61.8 0.0 copy-done.6
  61.8 0.0 copy-done.7
  61.9 0.5 shard_map.110
  62.3 0.0 copy-start.2
  62.4 0.0 copy-start.8
  62.4 0.0 copy-start.9
  62.4 1.4 %collective-permute-start = (bf16[128,640]{1,0:T(8,128)(2,1)S(1)}, bf16[128,640]{1,0:T(8,128)(2,1)S(1)}, u32[]{:S(2)}, u32[]{:S(2)}) collective-permute-start(bf16[128,640]{1,0:T(8,128)(2,1)S(1)} %get-tuple-element.10.norm_ref), channel_id=1, source_target_pairs={{8,0},{16,8},{24,16},{32,24},{40,32},{48,40},{56,48},{64,56},{72,6... | collective-permute-start | bytes 491528 | tf_op jit(solution)/shard_map/ppermute | solution.py:204
  63.8 4.6 %collective-permute-start.2 = (bf16[128,640]{1,0:T(8,128)(2,1)S(1)}, bf16[128,640]{1,0:T(8,128)(2,1)S(1)}, u32[]{:S(2)}, u32[]{:S(2)}) collective-permute-start(bf16[128,640]{1,0:T(8,128)(2,1)S(1)} %get-tuple-element.10.norm_ref), channel_id=1, source_target_pairs={{0,8},{8,16},{16,24},{24,32},{32,40},{40,48},{48,56},{56,64},{64,7... | collective-permute-start | bytes 491528 | tf_op jit(solution)/shard_map/ppermute | solution.py:204
  68.4 1.7 %collective-permute-done.after_ref = bf16[128,640]{1,0:T(8,128)(2,1)S(1)} collective-permute-done((bf16[128,640]{1,0:T(8,128)(2,1)S(1)}, bf16[128,640]{1,0:T(8,128)(2,1)S(1)}, u32[]{:S(2)}, u32[]{:S(2)}) %collective-permute-start) | collective-permute-done | bytes 163872 | tf_op jit(solution)/shard_map/ppermute | solution.py:204
  70.1 1.3 %collective-permute-start.1 = (bf16[128,640]{1,0:T(8,128)(2,1)S(1)}, bf16[128,640]{1,0:T(8,128)(2,1)S(1)}, u32[]{:S(2)}, u32[]{:S(2)}) collective-permute-start(bf16[128,640]{1,0:T(8,128)(2,1)S(1)} %collective-permute-done.after_ref), channel_id=1, source_target_pairs={{8,0},{16,8},{24,16},{32,24},{40,32},{48,40},{56,48},{64,56},{72,6... | collective-permute-start | bytes 491528 | tf_op jit(solution)/shard_map/ppermute | solution.py:204
  71.4 0.0 collective-permute-done.2.before_ref
  71.4 4.6 %collective-permute-start.3 = (bf16[128,640]{1,0:T(8,128)(2,1)S(1)}, bf16[128,640]{1,0:T(8,128)(2,1)S(1)}, u32[]{:S(2)}, u32[]{:S(2)}) collective-permute-start(bf16[128,640]{1,0:T(8,128)(2,1)S(1)} %collective-permute-done.2.before_ref), channel_id=1, source_target_pairs={{0,8},{8,16},{16,24},{24,32},{32,40},{40,48},{48,56},{56,64},{64,7... | collective-permute-start | bytes 491528 | tf_op jit(solution)/shard_map/ppermute | solution.py:204
  76.0 0.0 copy-done.1
  76.0 1.3 %shard_map.111 = (f32[16,8,640]{2,1,0:T(8,128)S(1)}, f32[3,16,8,640]{3,2,1,0:T(8,128)S(1)}, f32[3,16,8,640]{3,2,1,0:T(8,128)S(1)}) custom-call(bf16[128,640]{1,0:T(8,128)(2,1)S(1)} %collective-permute-done.2.before_ref, bf16[128,640]{1,0:T(8,128)(2,1)S(1)} %get-tuple-element.10.norm_ref, bf16[128,640]{1,0:T(8,128)(2,1)S(1)} %collective-permute-done.after_ref, ...), custom_call_target="tpu_custom_call" | custom-call | tf_op jit(solution)/shard_map/pallas_call | solution.py:245
  77.3 0.0 collective-permute-done.1.b4_ref
  77.3 1.5 %collective-permute-done.3.b0_ref = bf16[128,640]{1,0:T(8,128)(2,1)S(1)} collective-permute-done((bf16[128,640]{1,0:T(8,128)(2,1)S(1)}, bf16[128,640]{1,0:T(8,128)(2,1)S(1)}, u32[]{:S(2)}, u32[]{:S(2)}) %collective-permute-start.3) | collective-permute-done | bytes 163872 | tf_op jit(solution)/shard_map/ppermute | solution.py:204
  78.8 0.0 copy-done.2
  78.8 0.0 copy-done.8
  78.8 0.0 copy-done.9
  78.8 4.1 %shard_map.112 = bf16[8,16,640]{2,1,0:T(8,128)(2,1)} custom-call(s32[28]{0:T(128)S(1)} %copy-done.9, bf16[128,640]{1,0:T(8,128)(2,1)S(1)} %collective-permute-done.1.b4_ref, bf16[128,640]{1,0:T(8,128)(2,1)S(1)} %collective-permute-done.3.b0_ref, f32[16,8,640]{2,1,0:T(8,128)S(1)} %get-tuple-element.11.query, ...), custom_call_target="tpu_custom_call" | custom-call | tf_op jit(solution)/shard_map/pallas_call | solution.py:252
Async XLA Ops:
  0.0 6.6 %copy-start = (f32[640]{0:T(1024)S(1)}, f32[640]{0:T(1024)}, u32[]{:S(2)}) copy-start(f32[640]{0:T(1024)} %param.16) | copy-start | bytes 7684
  2.1 4.6 %copy-start.10 = (bf16[360,80]{0,1:T(8,128)(2,1)S(1)}, bf16[360,80]{0,1:T(8,128)(2,1)}, u32[]{:S(2)}) copy-start(bf16[360,80]{0,1:T(8,128)(2,1)} %param.15) | copy-start | bytes 172804
  2.1 45.9 %copy-start.4 = (f32[640]{0:T(1024)S(1)}, f32[640]{0:T(1024)}, u32[]{:S(2)}) copy-start(f32[640]{0:T(1024)} %gain_ref.2) | copy-start | bytes 7684
  2.1 45.9 %copy-start.5 = (f32[640]{0:T(1024)S(1)}, f32[640]{0:T(1024)}, u32[]{:S(2)}) copy-start(f32[640]{0:T(1024)} %bias_ref.2) | copy-start | bytes 7684
  2.1 45.9 %all-to-all-start = ((bf16[8,8,16,640]{3,2,1,0:T(8,128)(2,1)}), bf16[8,8,16,640]{3,2,1,0:T(8,128)(2,1)S(1)}, u32[]{:S(2)}, u32[]{:S(2)}) async-start(bf16[8,8,16,640]{3,2,1,0:T(8,128)(2,1)} %broadcast_in_dim.11), calls=%async_computation | async-start | bytes 2621440 | tf_op jit(solution)/shard_map/all_to_all | solution.py:218
  48.1 13.8 %copy-start.3 = (bf16[8,1,16,640]{3,2,1,0:T(8,128)(2,1)S(1)}, bf16[8,1,16,640]{3,2,1,0:T(8,128)(2,1)}, u32[]{:S(2)}) copy-start(bf16[8,1,16,640]{3,2,1,0:T(8,128)(2,1)} %param.11) | copy-start | bytes 491524
  48.1 13.8 %copy-start.6 = (f32[640]{0:T(1024)S(1)}, f32[640]{0:T(1024)}, u32[]{:S(2)}) copy-start(f32[640]{0:T(1024)} %gain_ref.3) | copy-start | bytes 7684
  48.1 13.8 %copy-start.7 = (f32[640]{0:T(1024)S(1)}, f32[640]{0:T(1024)}, u32[]{:S(2)}) copy-start(f32[640]{0:T(1024)} %bias_ref.3) | copy-start | bytes 7684
  48.1 27.9 %copy-start.1 = (bf16[640,1920]{1,0:T(8,128)(2,1)S(1)}, bf16[640,1920]{1,0:T(8,128)(2,1)}, u32[]{:S(2)}) copy-start(bf16[640,1920]{1,0:T(8,128)(2,1)} %qkv_ref.3) | copy-start | bytes 7372804
  62.3 16.4 %copy-start.2 = (bf16[640,640]{1,0:T(8,128)(2,1)S(1)}, bf16[640,640]{1,0:T(8,128)(2,1)}, u32[]{:S(2)}) copy-start(bf16[640,640]{1,0:T(8,128)(2,1)} %out_w_ref.1) | copy-start | bytes 2457604
  62.4 16.4 %copy-start.8 = (f32[640]{0:T(1024)S(1)}, f32[640]{0:T(1024)}, u32[]{:S(2)}) copy-start(f32[640]{0:T(1024)} %out_b_ref.1) | copy-start | bytes 7684
  62.4 16.4 %copy-start.9 = (s32[28]{0:T(128)S(1)}, s32[28]{0:T(128)}, u32[]{:S(2)}) copy-start(s32[28]{0:T(128)} %gaps_ref.1) | copy-start | bytes 340
  62.4 7.7 %collective-permute-start = (bf16[128,640]{1,0:T(8,128)(2,1)S(1)}, bf16[128,640]{1,0:T(8,128)(2,1)S(1)}, u32[]{:S(2)}, u32[]{:S(2)}) collective-permute-start(bf16[128,640]{1,0:T(8,128)(2,1)S(1)} %get-tuple-element.10.norm_ref), channel_id=1, source_target_pairs={{8,0},{16,8},{24,16},{32,24},{40,32},{48,40},{56,48},{64,56},{72,6... | collective-permute-start | bytes 491528 | tf_op jit(solution)/shard_map/ppermute | solution.py:204
  63.8 7.6 %collective-permute-start.2 = (bf16[128,640]{1,0:T(8,128)(2,1)S(1)}, bf16[128,640]{1,0:T(8,128)(2,1)S(1)}, u32[]{:S(2)}, u32[]{:S(2)}) collective-permute-start(bf16[128,640]{1,0:T(8,128)(2,1)S(1)} %get-tuple-element.10.norm_ref), channel_id=1, source_target_pairs={{0,8},{8,16},{16,24},{24,32},{32,40},{40,48},{48,56},{56,64},{64,7... | collective-permute-start | bytes 491528 | tf_op jit(solution)/shard_map/ppermute | solution.py:204
  70.1 7.2 %collective-permute-start.1 = (bf16[128,640]{1,0:T(8,128)(2,1)S(1)}, bf16[128,640]{1,0:T(8,128)(2,1)S(1)}, u32[]{:S(2)}, u32[]{:S(2)}) collective-permute-start(bf16[128,640]{1,0:T(8,128)(2,1)S(1)} %collective-permute-done.after_ref), channel_id=1, source_target_pairs={{8,0},{16,8},{24,16},{32,24},{40,32},{48,40},{56,48},{64,56},{72,6... | collective-permute-start | bytes 491528 | tf_op jit(solution)/shard_map/ppermute | solution.py:204
  71.4 7.4 %collective-permute-start.3 = (bf16[128,640]{1,0:T(8,128)(2,1)S(1)}, bf16[128,640]{1,0:T(8,128)(2,1)S(1)}, u32[]{:S(2)}, u32[]{:S(2)}) collective-permute-start(bf16[128,640]{1,0:T(8,128)(2,1)S(1)} %collective-permute-done.2.before_ref), channel_id=1, source_target_pairs={{0,8},{8,16},{16,24},{24,32},{32,40},{40,48},{48,56},{56,64},{64,7... | collective-permute-start | bytes 491528 | tf_op jit(solution)/shard_map/ppermute | solution.py:204

commit v6 on v5

--- a/solution.py
+++ b/solution.py
@@ -132,38 +132,40 @@
     return product.astype(BF16).astype(F32).reshape(shape)
 
 
-def early_kernel(before_ref, norm_ref, after_ref, qkv_ref, query_ref, key_ref, value_ref):
+def early_kernel(
+    gaps_ref, before_ref, norm_ref, after_ref, qkv_ref, member_ref, query_ref, key_ref, value_ref
+):
     chans = norm_ref.shape[1]
-    shape = query_ref.shape
-    query_ref[...] = by_cell(dot(norm_ref[...], qkv_ref[:, :chans]), shape)
-    for b, ref in enumerate((before_ref, norm_ref, after_ref)):
-        key_ref[b] = by_cell(dot(ref[...], qkv_ref[:, chans : 2 * chans]), shape)
-        value_ref[b] = by_cell(dot(ref[...], qkv_ref[:, 2 * chans :]), shape)
-
-
-def attend_kernel(
-    gaps_ref, b4_ref, b0_ref, query, mid_keys, mid_values, resid_ref, qkv_ref, out_w_ref,
-    out_b_ref, out_ref, far_keys, far_values, scores, mixed,
-):
-    mids, width, frames, chans = mid_keys.shape
-    near = (mids + 2) * frames
-    stack = HEADS * frames
-    shape = (width, frames, chans)
-    for b, ref in enumerate((b0_ref, b4_ref)):
-        far_keys[b] = by_cell(dot(ref[...], qkv_ref[:, chans : 2 * chans]), shape)
-        far_values[b] = by_cell(dot(ref[...], qkv_ref[:, 2 * chans :]), shape)
-
-    def at_cell(far, mid, c):
-        blocks = [far[0, c]] + [mid[b, c] for b in range(mids)] + [far[1, c]]
-        return jnp.concatenate(blocks, axis=0).astype(BF16)
-
+    query_ref[...] = by_cell(dot(norm_ref[...], qkv_ref[:, :chans]), query_ref.shape)
+    rows = jnp.concatenate([before_ref[...], norm_ref[...], after_ref[...]], axis=0)
+    key_ref[...] = by_cell(dot(rows, qkv_ref[:, chans : 2 * chans]), key_ref.shape)
+    value_ref[...] = by_cell(dot(rows, qkv_ref[:, 2 * chans :]), value_ref.shape)
+    frames = query_ref.shape[1]
     window = iota((1, LANES), 1)
     start, starts = jnp.int32(0), jnp.where(window == 0, 0, -(1 << 20))
     for w in range(gaps_ref.shape[0]):
         start = start + gaps_ref[w]
         starts = jnp.where(window == w + 1, start, starts)
-    ids = (lax.axis_index("frames") - 2) * frames + iota((near, LANES), 0)
-    member = ((ids >= starts) & (ids < starts + WIN)).astype(F32)
+    ids = (lax.axis_index("frames") - 2) * frames + iota(member_ref.shape, 0)
+    member_ref[...] = ((ids >= starts) & (ids < starts + WIN)).astype(F32)
+
+
+def attend_kernel(
+    b4_ref, b0_ref, member_ref, query, mid_keys, mid_values, resid_ref, qkv_ref, out_w_ref,
+    out_b_ref, out_ref, far_keys, far_values, scores, mixed,
+):
+    mids, width, frames, chans = mid_keys.shape
+    near = (mids + 2) * frames
+    stack = HEADS * frames
+    rows = jnp.concatenate([b0_ref[...], b4_ref[...]], axis=0)
+    far_keys[...] = by_cell(dot(rows, qkv_ref[:, chans : 2 * chans]), far_keys.shape)
+    far_values[...] = by_cell(dot(rows, qkv_ref[:, 2 * chans :]), far_values.shape)
+
+    def at_cell(far, mid, c):
+        blocks = [far[0, c]] + [mid[b, c] for b in range(mids)] + [far[1, c]]
+        return jnp.concatenate(blocks, axis=0).astype(BF16)
+
+    member = member_ref[...]
     cover = member[2 * frames : 3 * frames][None]
     member = member.astype(BF16)
     head_of = lax.div(iota((HEADS, 1, chans), 2), HEAD_DIM) == iota((HEADS, 1, chans), 0)
@@ -176,7 +178,7 @@
     expo = jnp.exp(scores[...].reshape(flat, near) * HEAD_DIM ** (-0.5))
 
     def split_dot(a, dims):
-        high = a.astype(BF16)
+        high = jnp.minimum(a, float(jnp.finfo(BF16).max)).astype(BF16)
         rest = (a - high.astype(F32)).astype(BF16)
         return lax.dot_general(high, member, dims, preferred_element_type=F32) + lax.dot_general(
             rest, member, dims, preferred_element_type=F32
@@ -244,15 +246,15 @@
     mid = jax.ShapeDtypeStruct((3, width, frames, chans), F32)
     early = pl.pallas_call(
         early_kernel,
-        out_shape=[own, mid, mid],
-        in_specs=[VMEM] * 4,
-        out_specs=[VMEM] * 3,
-        compiler_params=GRANT,
-    )(on_chip(b1), norm, on_chip(b3), qkv)
+        out_shape=[jax.ShapeDtypeStruct((5 * frames, LANES), F32), own, mid, mid],
+        in_specs=[SMEM] + [VMEM] * 4,
+        out_specs=[VMEM] * 4,
+        compiler_params=GRANT,
+    )(window_gaps, on_chip(b1), norm, on_chip(b3), qkv)
     out = pl.pallas_call(
         attend_kernel,
         out_shape=jax.ShapeDtypeStruct((frames, width, chans), BF16),
-        in_specs=[SMEM] + [VMEM] * 9,
+        in_specs=[VMEM] * 10,
         out_specs=VMEM,
         compiler_params=GRANT,
         scratch_shapes=[
@@ -262,8 +264,8 @@
             pltpu.VMEM((width, frames, chans), F32),
         ],
     )(
-        window_gaps, on_chip(b4), on_chip(b0), *[on_chip(n) for n in early], on_chip(resid), qkv,
-        on_chip(out_weight), out_bias,
+        on_chip(b4), on_chip(b0), *[on_chip(n) for n in early], on_chip(resid), qkv,
+        on_chip(out_weight), on_chip(out_bias),
     )
     return out.reshape(frames, 1, width, chans)
 

time: 83.8 us -> 83.3 us (level)
  no operation moved by 1% of the time
where the time goes in v6:
time: 83.3 us; the launch traced here: 82.3 us
  blocking collectives  52.2 us (63%)
  starting transfers between devices  16.2 us (19%)
  Pallas kernels  8.55 us (10%)
  waiting for transfers between devices  2.77 us (3%)
  local copies, waits for them, and re-layouts  2.37 us (3%)
    all_gather x1, blocking collectives, on_device(): weight = lax.all_gather(conv_weight.T, 'frames', axis=0, tiled=False)  41.3 us
    ppermute x4, starting transfers between devices, passed(): return lax.ppermute(shard, 'frames', pairs)  11.8 us
    all_to_all x1, blocking collectives, on_device(): parts = lax.all_to_all(parts, 'height', 0, 0, tiled=True)  10.9 us
    all_to_all x1, starting transfers between devices, on_device(): whole = lax.all_to_all(copies, 'height', 0, 0, tiled=True)  4.43 us
    pallas_call x1, Pallas kernels, on_device(): pl.pallas_call(attend_kernel, out_shape=jax.ShapeDtypeStruct((frames, wid...  3.53 us
    pallas_call x1, Pallas kernels, on_device(): pl.pallas_call(conv_kernel, out_shape=jax.ShapeDtypeStruct((bands, outs,...  2.78 us
    ppermute x4, waiting for transfers between devices, passed(): return lax.ppermute(shard, 'frames', pairs)  2.76 us
    broadcast_in_dim x1, local copies, waits for them, and re-layouts, on_device(): copies = jnp.broadcast_to(row[None], (bands, frames, width, chans))  2.13 us
  transfers between devices with their start and end apart: 5, of which 2 were waited for; matrix products, arithmetic and copies ran while one was open for 0% of the time, Pallas kernels for 2%

profile of v6, /device:TPU:24, one launch (start us, length us, event | category | flops | bytes accessed | tf_op | source)
XLA Modules:
  0.0 82.3 jit_solution(692659644369009203)
XLA Ops:
  0.0 0.0 copy-start
  0.0 2.1 %broadcast_in_dim.11 = bf16[8,8,16,640]{3,2,1,0:T(8,128)(2,1)} broadcast(bf16[8,16,640]{2,1,0:T(8,128)(2,1)} %bitcast.9), dimensions={1,2,3} | broadcast | bytes 1474560 | tf_op jit(solution)/shard_map/broadcast_in_dim | solution.py:219
  2.1 0.0 copy-start.10
  2.1 0.0 copy-start.4
  2.1 0.0 copy-start.5
  2.1 4.4 %all-to-all-start = ((bf16[8,8,16,640]{3,2,1,0:T(8,128)(2,1)}), bf16[8,8,16,640]{3,2,1,0:T(8,128)(2,1)S(1)}, u32[]{:S(2)}, u32[]{:S(2)}) async-start(bf16[8,8,16,640]{3,2,1,0:T(8,128)(2,1)} %broadcast_in_dim.11), calls=%async_computation | async-start | bytes 2621440 | tf_op jit(solution)/shard_map/all_to_all | solution.py:220
  6.6 0.0 copy-done
  6.6 0.1 dynamic-slice_bitcast_fusion
  6.7 0.1 copy.12.cbias_ref
  6.8 0.0 copy-done.10
  6.8 41.3 %all-gather = bf16[1280,360]{1,0:T(8,128)(2,1)S(1)} all-gather(bf16[80,360]{1,0:T(8,128)(2,1)S(1)} %bitcast.11), channel_id=2, replica_groups=mesh['dp'=4,'frames'=16,'height'=8] {'frames'}, dimensions={0}, use_global_device_ids=true | all-gather | bytes 979200 | tf_op jit(solution)/shard_map/all_gather | solution.py:221
  48.0 0.0 all-to-all-done.cells_ref
  48.1 0.0 copy-done.4
  48.1 0.0 copy-done.5
  48.1 0.0 copy-start.3
  48.1 0.0 copy-start.6
  48.1 0.0 copy-start.7
  48.1 0.0 copy-start.1
  48.1 0.0 copy-start.9
  48.1 2.8 %shard_map.109 = bf16[8,80,128]{2,1,0:T(8,128)(2,1)S(1)} custom-call(bf16[8,8,16,640]{3,2,1,0:T(8,128)(2,1)S(1)} %all-to-all-done.cells_ref, bf16[16,80,360]{2,1,0:T(8,128)(2,1)S(1)} %bitcast.8, f32[640]{0:T(1024)S(1)} %copy-done.4, f32[640]{0:T(1024)S(1)} %copy-done.5, f32[80,1]{1,0:T(8,128)S(1)} %copy.12.cbias_ref), custom_call_target="tpu_custom_call" | custom-call | tf_op jit(solution)/shard_map/pallas_call | solution.py:223
  50.9 10.9 %all_to_all.10.part_ref = bf16[8,80,128]{2,1,0:T(8,128)(2,1)S(1)} all-to-all(bf16[8,80,128]{2,1,0:T(8,128)(2,1)S(1)} %shard_map.109), channel_id=1, replica_groups=mesh['dp'=4,'frames'=16,'height'=8] {'height'}, dimensions={0} | all-to-all | bytes 327680 | tf_op jit(solution)/shard_map/all_to_all | solution.py:234
  61.9 0.0 copy-done.3
  61.9 0.0 copy-done.6
  61.9 0.0 copy-done.7
  61.9 0.5 shard_map.110
  62.4 0.0 copy-start.2
  62.4 0.0 copy-start.8
  62.4 1.4 %collective-permute-start = (bf16[128,640]{1,0:T(8,128)(2,1)S(1)}, bf16[128,640]{1,0:T(8,128)(2,1)S(1)}, u32[]{:S(2)}, u32[]{:S(2)}) collective-permute-start(bf16[128,640]{1,0:T(8,128)(2,1)S(1)} %get-tuple-element.11.norm_ref), channel_id=1, source_target_pairs={{8,0},{16,8},{24,16},{32,24},{40,32},{48,40},{56,48},{64,56},{72,6... | collective-permute-start | bytes 491528 | tf_op jit(solution)/shard_map/ppermute | solution.py:206
  63.8 4.6 %collective-permute-start.2 = (bf16[128,640]{1,0:T(8,128)(2,1)S(1)}, bf16[128,640]{1,0:T(8,128)(2,1)S(1)}, u32[]{:S(2)}, u32[]{:S(2)}) collective-permute-start(bf16[128,640]{1,0:T(8,128)(2,1)S(1)} %get-tuple-element.11.norm_ref), channel_id=1, source_target_pairs={{0,8},{8,16},{16,24},{24,32},{32,40},{40,48},{48,56},{56,64},{64,7... | collective-permute-start | bytes 491528 | tf_op jit(solution)/shard_map/ppermute | solution.py:206
  68.4 1.7 %collective-permute-done.after_ref = bf16[128,640]{1,0:T(8,128)(2,1)S(1)} collective-permute-done((bf16[128,640]{1,0:T(8,128)(2,1)S(1)}, bf16[128,640]{1,0:T(8,128)(2,1)S(1)}, u32[]{:S(2)}, u32[]{:S(2)}) %collective-permute-start) | collective-permute-done | bytes 163872 | tf_op jit(solution)/shard_map/ppermute | solution.py:206
  70.1 1.3 %collective-permute-start.1 = (bf16[128,640]{1,0:T(8,128)(2,1)S(1)}, bf16[128,640]{1,0:T(8,128)(2,1)S(1)}, u32[]{:S(2)}, u32[]{:S(2)}) collective-permute-start(bf16[128,640]{1,0:T(8,128)(2,1)S(1)} %collective-permute-done.after_ref), channel_id=1, source_target_pairs={{8,0},{16,8},{24,16},{32,24},{40,32},{48,40},{56,48},{64,56},{72,6... | collective-permute-start | bytes 491528 | tf_op jit(solution)/shard_map/ppermute | solution.py:206
  71.4 0.0 collective-permute-done.2.before_ref
  71.4 4.6 %collective-permute-start.3 = (bf16[128,640]{1,0:T(8,128)(2,1)S(1)}, bf16[128,640]{1,0:T(8,128)(2,1)S(1)}, u32[]{:S(2)}, u32[]{:S(2)}) collective-permute-start(bf16[128,640]{1,0:T(8,128)(2,1)S(1)} %collective-permute-done.2.before_ref), channel_id=1, source_target_pairs={{0,8},{8,16},{16,24},{24,32},{32,40},{40,48},{48,56},{56,64},{64,7... | collective-permute-start | bytes 491528 | tf_op jit(solution)/shard_map/ppermute | solution.py:206
  76.0 0.0 copy-done.1
  76.0 0.0 copy-done.9
  76.0 1.8 %shard_map.111 = (f32[40,128]{1,0:T(8,128)S(1)}, f32[16,8,640]{2,1,0:T(8,128)S(1)}, f32[3,16,8,640]{3,2,1,0:T(8,128)S(1)}, f32[3,16,8,640]{3,2,1,0:T(8,128)S(1)}) custom-call(s32[28]{0:T(128)S(1)} %copy-done.9, bf16[128,640]{1,0:T(8,128)(2,1)S(1)} %collective-permute-done.2.before_ref, bf16[128,640]{1,0:T(8,128)(2,1)S(1)} %get-tuple-element.11.norm_ref, ...), custom_call_target="tpu_custom_call" | custom-call | tf_op jit(solution)/shard_map/pallas_call | solution.py:247
  77.8 0.0 collective-permute-done.1.b4_ref
  77.8 1.0 %collective-permute-done.3.b0_ref = bf16[128,640]{1,0:T(8,128)(2,1)S(1)} collective-permute-done((bf16[128,640]{1,0:T(8,128)(2,1)S(1)}, bf16[128,640]{1,0:T(8,128)(2,1)S(1)}, u32[]{:S(2)}, u32[]{:S(2)}) %collective-permute-start.3) | collective-permute-done | bytes 163872 | tf_op jit(solution)/shard_map/ppermute | solution.py:206
  78.8 0.0 copy-done.2
  78.8 0.0 copy-done.8
  78.8 3.5 %shard_map.112 = bf16[8,16,640]{2,1,0:T(8,128)(2,1)} custom-call(bf16[128,640]{1,0:T(8,128)(2,1)S(1)} %collective-permute-done.1.b4_ref, bf16[128,640]{1,0:T(8,128)(2,1)S(1)} %collective-permute-done.3.b0_ref, f32[40,128]{1,0:T(8,128)S(1)} %get-tuple-element.12.member_ref, f32[16,8,640]{2,1,0:T(8,128)S(1)} %get-tuple-element.13.query, ...), custom_call_target="tpu_custom_call" | custom-call | tf_op jit(solution)/shard_map/pallas_call | solution.py:254
Async XLA Ops:
  0.0 6.6 %copy-start = (f32[640]{0:T(1024)S(1)}, f32[640]{0:T(1024)}, u32[]{:S(2)}) copy-start(f32[640]{0:T(1024)} %param.16) | copy-start | bytes 7684
  2.1 4.6 %copy-start.10 = (bf16[360,80]{0,1:T(8,128)(2,1)S(1)}, bf16[360,80]{0,1:T(8,128)(2,1)}, u32[]{:S(2)}) copy-start(bf16[360,80]{0,1:T(8,128)(2,1)} %param.15) | copy-start | bytes 172804
  2.1 45.9 %copy-start.4 = (f32[640]{0:T(1024)S(1)}, f32[640]{0:T(1024)}, u32[]{:S(2)}) copy-start(f32[640]{0:T(1024)} %gain_ref.2) | copy-start | bytes 7684
  2.1 45.9 %copy-start.5 = (f32[640]{0:T(1024)S(1)}, f32[640]{0:T(1024)}, u32[]{:S(2)}) copy-start(f32[640]{0:T(1024)} %bias_ref.2) | copy-start | bytes 7684
  2.1 45.9 %all-to-all-start = ((bf16[8,8,16,640]{3,2,1,0:T(8,128)(2,1)}), bf16[8,8,16,640]{3,2,1,0:T(8,128)(2,1)S(1)}, u32[]{:S(2)}, u32[]{:S(2)}) async-start(bf16[8,8,16,640]{3,2,1,0:T(8,128)(2,1)} %broadcast_in_dim.11), calls=%async_computation | async-start | bytes 2621440 | tf_op jit(solution)/shard_map/all_to_all | solution.py:220
  48.1 13.8 %copy-start.3 = (bf16[8,1,16,640]{3,2,1,0:T(8,128)(2,1)S(1)}, bf16[8,1,16,640]{3,2,1,0:T(8,128)(2,1)}, u32[]{:S(2)}) copy-start(bf16[8,1,16,640]{3,2,1,0:T(8,128)(2,1)} %param.11) | copy-start | bytes 491524
  48.1 13.8 %copy-start.6 = (f32[640]{0:T(1024)S(1)}, f32[640]{0:T(1024)}, u32[]{:S(2)}) copy-start(f32[640]{0:T(1024)} %gain_ref.3) | copy-start | bytes 7684
  48.1 13.8 %copy-start.7 = (f32[640]{0:T(1024)S(1)}, f32[640]{0:T(1024)}, u32[]{:S(2)}) copy-start(f32[640]{0:T(1024)} %bias_ref.3) | copy-start | bytes 7684
  48.1 27.9 %copy-start.1 = (bf16[640,1920]{1,0:T(8,128)(2,1)S(1)}, bf16[640,1920]{1,0:T(8,128)(2,1)}, u32[]{:S(2)}) copy-start(bf16[640,1920]{1,0:T(8,128)(2,1)} %qkv_ref.3) | copy-start | bytes 7372804
  48.1 27.9 %copy-start.9 = (s32[28]{0:T(128)S(1)}, s32[28]{0:T(128)}, u32[]{:S(2)}) copy-start(s32[28]{0:T(128)} %gaps_ref.1) | copy-start | bytes 340
  62.4 16.4 %copy-start.2 = (bf16[640,640]{1,0:T(8,128)(2,1)S(1)}, bf16[640,640]{1,0:T(8,128)(2,1)}, u32[]{:S(2)}) copy-start(bf16[640,640]{1,0:T(8,128)(2,1)} %out_w_ref.1) | copy-start | bytes 2457604
  62.4 16.4 %copy-start.8 = (f32[640]{0:T(1024)S(1)}, f32[640]{0:T(1024)}, u32[]{:S(2)}) copy-start(f32[640]{0:T(1024)} %out_b_ref.1) | copy-start | bytes 7684
  62.4 7.7 %collective-permute-start = (bf16[128,640]{1,0:T(8,128)(2,1)S(1)}, bf16[128,640]{1,0:T(8,128)(2,1)S(1)}, u32[]{:S(2)}, u32[]{:S(2)}) collective-permute-start(bf16[128,640]{1,0:T(8,128)(2,1)S(1)} %get-tuple-element.11.norm_ref), channel_id=1, source_target_pairs={{8,0},{16,8},{24,16},{32,24},{40,32},{48,40},{56,48},{64,56},{72,6... | collective-permute-start | bytes 491528 | tf_op jit(solution)/shard_map/ppermute | solution.py:206
  63.8 7.6 %collective-permute-start.2 = (bf16[128,640]{1,0:T(8,128)(2,1)S(1)}, bf16[128,640]{1,0:T(8,128)(2,1)S(1)}, u32[]{:S(2)}, u32[]{:S(2)}) collective-permute-start(bf16[128,640]{1,0:T(8,128)(2,1)S(1)} %get-tuple-element.11.norm_ref), channel_id=1, source_target_pairs={{0,8},{8,16},{16,24},{24,32},{32,40},{40,48},{48,56},{56,64},{64,7... | collective-permute-start | bytes 491528 | tf_op jit(solution)/shard_map/ppermute | solution.py:206
  70.1 7.6 %collective-permute-start.1 = (bf16[128,640]{1,0:T(8,128)(2,1)S(1)}, bf16[128,640]{1,0:T(8,128)(2,1)S(1)}, u32[]{:S(2)}, u32[]{:S(2)}) collective-permute-start(bf16[128,640]{1,0:T(8,128)(2,1)S(1)} %collective-permute-done.after_ref), channel_id=1, source_target_pairs={{8,0},{16,8},{24,16},{32,24},{40,32},{48,40},{56,48},{64,56},{72,6... | collective-permute-start | bytes 491528 | tf_op jit(solution)/shard_map/ppermute | solution.py:206
  71.4 7.4 %collective-permute-start.3 = (bf16[128,640]{1,0:T(8,128)(2,1)S(1)}, bf16[128,640]{1,0:T(8,128)(2,1)S(1)}, u32[]{:S(2)}, u32[]{:S(2)}) collective-permute-start(bf16[128,640]{1,0:T(8,128)(2,1)S(1)} %collective-permute-done.2.before_ref), channel_id=1, source_target_pairs={{0,8},{8,16},{16,24},{24,32},{32,40},{40,48},{48,56},{56,64},{64,7... | collective-permute-start | bytes 491528 | tf_op jit(solution)/shard_map/ppermute | solution.py:206

commit v7 on v6

--- a/solution.py
+++ b/solution.py
@@ -95,6 +95,7 @@
         preferred_element_type=F32,
     )
     lanes = frames * width
+    cbias = jnp.broadcast_to(cbias_ref[...], (8, outs)).T[:, :1]
     column = lax.rem(iota((1, lanes), 1), width)
     for r in range(rows):
         left, middle, right = [
@@ -102,7 +103,7 @@
         ]
         left = jnp.where(column == 0, 0.0, pltpu.roll(left, 1, 1))
         right = jnp.where(column == width - 1, 0.0, pltpu.roll(right, lanes - 1, 1))
-        out_ref[r] = (middle + left + right + cbias_ref[...]).astype(BF16)
+        out_ref[r] = (middle + left + right + cbias).astype(BF16)
 
 
 def swap_matrix(frames, width, back):
@@ -219,7 +220,7 @@
     copies = jnp.broadcast_to(row[None], (bands, frames, width, chans))
     whole = lax.all_to_all(copies, "height", 0, 0, tiled=True)
     weight = lax.all_gather(conv_weight.T, "frames", axis=0, tiled=False)
-    cbias = lax.dynamic_slice_in_dim(conv_bias, place * outs, outs)[:, None]
+    cbias = lax.dynamic_slice_in_dim(conv_bias, place * outs, outs)[None]
     parts = pl.pallas_call(
         conv_kernel,
         out_shape=jax.ShapeDtypeStruct((bands, outs, cells), BF16),
@@ -240,7 +241,7 @@
         compiler_params=GRANT,
     )(on_chip(parts), row, ln_gain, ln_bias)
     b3, b1 = passed(norm, -1), passed(norm, 1)
-    b4, b0 = passed(b3, -1), passed(b1, 1)
+    b4, b0 = passed(b3, -1), passed(norm, 2)
     qkv = on_chip(qkv_weight)
     own = jax.ShapeDtypeStruct((width, frames, chans), F32)
     mid = jax.ShapeDtypeStruct((3, width, frames, chans), F32)

time: 83.3 us -> 81.5 us (0.978)
  starting transfers between devices: 16.2 us -> 13.9 us
  waiting for transfers between devices: 2.77 us -> 4.16 us
    ppermute x4, starting transfers between devices: 11.8 us -> 9.43 us  [passed(): return lax.ppermute(shard, 'frames', pairs)]
    ppermute x4, waiting for transfers between devices: 2.76 us -> 4.16 us  [passed(): return lax.ppermute(shard, 'frames', pairs)]
  transfers between devices with their start and end apart: 5 -> 5, of which waited for: 2 -> 3; matrix products, arithmetic and copies ran while one was open for 0% -> 0% of each run, Pallas kernels for 2% -> 2%
where the time goes in v7:
time: 81.5 us; the launch traced here: 81.2 us
  blocking collectives  52.2 us (64%)
  starting transfers between devices  13.9 us (17%)
  Pallas kernels  8.53 us (10%)
  waiting for transfers between devices  4.16 us (5%)
  local copies, waits for them, and re-layouts  2.27 us (3%)
    all_gather x1, blocking collectives, on_device(): weight = lax.all_gather(conv_weight.T, 'frames', axis=0, tiled=False)  41.3 us
    all_to_all x1, blocking collectives, on_device(): parts = lax.all_to_all(parts, 'height', 0, 0, tiled=True)  11 us
    ppermute x4, starting transfers between devices, passed(): return lax.ppermute(shard, 'frames', pairs)  9.43 us
    all_to_all x1, starting transfers between devices, on_device(): whole = lax.all_to_all(copies, 'height', 0, 0, tiled=True)  4.43 us
    ppermute x4, waiting for transfers between devices, passed(): return lax.ppermute(shard, 'frames', pairs)  4.16 us
    pallas_call x1, Pallas kernels, on_device(): pl.pallas_call(attend_kernel, out_shape=jax.ShapeDtypeStruct((frames, wid...  3.53 us
    pallas_call x1, Pallas kernels, on_device(): pl.pallas_call(conv_kernel, out_shape=jax.ShapeDtypeStruct((bands, outs,...  2.76 us
    broadcast_in_dim x1, local copies, waits for them, and re-layouts, on_device(): copies = jnp.broadcast_to(row[None], (bands, frames, width, chans))  2.13 us
  transfers between devices with their start and end apart: 5, of which 3 were waited for; matrix products, arithmetic and copies ran while one was open for 0% of the time, Pallas kernels for 2%

profile of v7, /device:TPU:24, one launch (start us, length us, event | category | flops | bytes accessed | tf_op | source)
XLA Modules:
  0.0 81.2 jit_solution(15483685530973834764)
XLA Ops:
  0.0 0.0 copy-start
  0.0 2.1 %broadcast_in_dim.11 = bf16[8,8,16,640]{3,2,1,0:T(8,128)(2,1)} broadcast(bf16[8,16,640]{2,1,0:T(8,128)(2,1)} %bitcast.9), dimensions={1,2,3} | broadcast | bytes 1474560 | tf_op jit(solution)/shard_map/broadcast_in_dim | solution.py:220
  2.1 0.0 copy-start.10
  2.1 0.0 copy-start.4
  2.1 0.0 copy-start.5
  2.1 4.4 %all-to-all-start = ((bf16[8,8,16,640]{3,2,1,0:T(8,128)(2,1)}), bf16[8,8,16,640]{3,2,1,0:T(8,128)(2,1)S(1)}, u32[]{:S(2)}, u32[]{:S(2)}) async-start(bf16[8,8,16,640]{3,2,1,0:T(8,128)(2,1)} %broadcast_in_dim.11), calls=%async_computation | async-start | bytes 2621440 | tf_op jit(solution)/shard_map/all_to_all | solution.py:221
  6.6 0.0 copy-done
  6.6 0.1 dynamic-slice_bitcast_fusion.cbias_ref
  6.7 0.0 copy-done.10
  6.7 41.3 %all-gather = bf16[1280,360]{1,0:T(8,128)(2,1)S(1)} all-gather(bf16[80,360]{1,0:T(8,128)(2,1)S(1)} %bitcast.11), channel_id=2, replica_groups=mesh['dp'=4,'frames'=16,'height'=8] {'frames'}, dimensions={0}, use_global_device_ids=true | all-gather | bytes 979200 | tf_op jit(solution)/shard_map/all_gather | solution.py:222
  47.9 0.0 all-to-all-done.cells_ref
  47.9 0.0 copy-done.4
  47.9 0.0 copy-done.5
  47.9 0.0 copy-start.3
  48.0 0.0 copy-start.6
  48.0 0.0 copy-start.7
  48.0 0.0 copy-start.1
  48.0 0.0 copy-start.9
  48.0 2.8 %shard_map.109 = bf16[8,80,128]{2,1,0:T(8,128)(2,1)S(1)} custom-call(bf16[8,8,16,640]{3,2,1,0:T(8,128)(2,1)S(1)} %all-to-all-done.cells_ref, bf16[16,80,360]{2,1,0:T(8,128)(2,1)S(1)} %bitcast.8, f32[640]{0:T(1024)S(1)} %copy-done.4, f32[640]{0:T(1024)S(1)} %copy-done.5, f32[1,80]{1,0:T(1,128)S(1)} %dynamic-slice_bitcast_fusion.cbias_ref), custom_call_target="tpu_custom_call" | custom-call | tf_op jit(solution)/shard_map/pallas_call | solution.py:224
  50.8 11.0 %all_to_all.10.part_ref = bf16[8,80,128]{2,1,0:T(8,128)(2,1)S(1)} all-to-all(bf16[8,80,128]{2,1,0:T(8,128)(2,1)S(1)} %shard_map.109), channel_id=1, replica_groups=mesh['dp'=4,'frames'=16,'height'=8] {'height'}, dimensions={0} | all-to-all | bytes 327680 | tf_op jit(solution)/shard_map/all_to_all | solution.py:235
  61.7 0.0 copy-done.3
  61.7 0.0 copy-done.6
  61.7 0.0 copy-done.7
  61.7 0.5 shard_map.110
  62.2 0.0 copy-start.2
  62.2 0.0 copy-start.8
  62.2 1.4 %collective-permute-start = (bf16[128,640]{1,0:T(8,128)(2,1)S(1)}, bf16[128,640]{1,0:T(8,128)(2,1)S(1)}, u32[]{:S(2)}, u32[]{:S(2)}) collective-permute-start(bf16[128,640]{1,0:T(8,128)(2,1)S(1)} %get-tuple-element.11.norm_ref), channel_id=1, source_target_pairs={{8,0},{16,8},{24,16},{32,24},{40,32},{48,40},{56,48},{64,56},{72,6... | collective-permute-start | bytes 491528 | tf_op jit(solution)/shard_map/ppermute | solution.py:207
  63.7 4.6 %collective-permute-start.3 = (bf16[128,640]{1,0:T(8,128)(2,1)S(1)}, bf16[128,640]{1,0:T(8,128)(2,1)S(1)}, u32[]{:S(2)}, u32[]{:S(2)}) collective-permute-start(bf16[128,640]{1,0:T(8,128)(2,1)S(1)} %get-tuple-element.11.norm_ref), channel_id=1, source_target_pairs={{0,8},{8,16},{16,24},{24,32},{32,40},{40,48},{48,56},{56,64},{64,7... | collective-permute-start | bytes 491528 | tf_op jit(solution)/shard_map/ppermute | solution.py:207
  68.2 2.2 %collective-permute-start.2 = (bf16[128,640]{1,0:T(8,128)(2,1)S(1)}, bf16[128,640]{1,0:T(8,128)(2,1)S(1)}, u32[]{:S(2)}, u32[]{:S(2)}) collective-permute-start(bf16[128,640]{1,0:T(8,128)(2,1)S(1)} %get-tuple-element.11.norm_ref), channel_id=1, source_target_pairs={{0,16},{8,24},{16,32},{24,40},{32,48},{40,56},{48,64},{56,72},{64,... | collective-permute-start | bytes 491528 | tf_op jit(solution)/shard_map/ppermute | solution.py:207
  70.4 0.0 collective-permute-done.after_ref
  70.4 1.3 %collective-permute-start.1 = (bf16[128,640]{1,0:T(8,128)(2,1)S(1)}, bf16[128,640]{1,0:T(8,128)(2,1)S(1)}, u32[]{:S(2)}, u32[]{:S(2)}) collective-permute-start(bf16[128,640]{1,0:T(8,128)(2,1)S(1)} %collective-permute-done.after_ref), channel_id=1, source_target_pairs={{8,0},{16,8},{24,16},{32,24},{40,32},{48,40},{56,48},{64,56},{72,6... | collective-permute-start | bytes 491528 | tf_op jit(solution)/shard_map/ppermute | solution.py:207
  71.7 1.1 %collective-permute-done.3.before_ref = bf16[128,640]{1,0:T(8,128)(2,1)S(1)} collective-permute-done((bf16[128,640]{1,0:T(8,128)(2,1)S(1)}, bf16[128,640]{1,0:T(8,128)(2,1)S(1)}, u32[]{:S(2)}, u32[]{:S(2)}) %collective-permute-start.3) | collective-permute-done | bytes 163872 | tf_op jit(solution)/shard_map/ppermute | solution.py:207
  72.8 0.0 copy-done.1
  72.8 0.0 copy-done.9
  72.8 1.7 %shard_map.111 = (f32[40,128]{1,0:T(8,128)S(1)}, f32[16,8,640]{2,1,0:T(8,128)S(1)}, f32[3,16,8,640]{3,2,1,0:T(8,128)S(1)}, f32[3,16,8,640]{3,2,1,0:T(8,128)S(1)}) custom-call(s32[28]{0:T(128)S(1)} %copy-done.9, bf16[128,640]{1,0:T(8,128)(2,1)S(1)} %collective-permute-done.3.before_ref, bf16[128,640]{1,0:T(8,128)(2,1)S(1)} %get-tuple-element.11.norm_ref, ...), custom_call_target="tpu_custom_call" | custom-call | tf_op jit(solution)/shard_map/pallas_call | solution.py:248
  74.5 0.2 collective-permute-done.2.b0_ref
  74.7 2.9 %collective-permute-done.1.b4_ref = bf16[128,640]{1,0:T(8,128)(2,1)S(1)} collective-permute-done((bf16[128,640]{1,0:T(8,128)(2,1)S(1)}, bf16[128,640]{1,0:T(8,128)(2,1)S(1)}, u32[]{:S(2)}, u32[]{:S(2)}) %collective-permute-start.1) | collective-permute-done | bytes 163872 | tf_op jit(solution)/shard_map/ppermute | solution.py:207
  77.6 0.0 copy-done.2
  77.6 0.0 copy-done.8
  77.6 3.5 %shard_map.112 = bf16[8,16,640]{2,1,0:T(8,128)(2,1)} custom-call(bf16[128,640]{1,0:T(8,128)(2,1)S(1)} %collective-permute-done.1.b4_ref, bf16[128,640]{1,0:T(8,128)(2,1)S(1)} %collective-permute-done.2.b0_ref, f32[40,128]{1,0:T(8,128)S(1)} %get-tuple-element.12.member_ref, f32[16,8,640]{2,1,0:T(8,128)S(1)} %get-tuple-element.13.query, ...), custom_call_target="tpu_custom_call" | custom-call | tf_op jit(solution)/shard_map/pallas_call | solution.py:255
Async XLA Ops:
  0.0 6.6 %copy-start = (f32[640]{0:T(1024)S(1)}, f32[640]{0:T(1024)}, u32[]{:S(2)}) copy-start(f32[640]{0:T(1024)} %param.16) | copy-start | bytes 7684
  2.1 4.5 %copy-start.10 = (bf16[360,80]{0,1:T(8,128)(2,1)S(1)}, bf16[360,80]{0,1:T(8,128)(2,1)}, u32[]{:S(2)}) copy-start(bf16[360,80]{0,1:T(8,128)(2,1)} %param.15) | copy-start | bytes 172804
  2.1 45.8 %copy-start.4 = (f32[640]{0:T(1024)S(1)}, f32[640]{0:T(1024)}, u32[]{:S(2)}) copy-start(f32[640]{0:T(1024)} %gain_ref.2) | copy-start | bytes 7684
  2.1 45.8 %copy-start.5 = (f32[640]{0:T(1024)S(1)}, f32[640]{0:T(1024)}, u32[]{:S(2)}) copy-start(f32[640]{0:T(1024)} %bias_ref.2) | copy-start | bytes 7684
  2.1 45.8 %all-to-all-start = ((bf16[8,8,16,640]{3,2,1,0:T(8,128)(2,1)}), bf16[8,8,16,640]{3,2,1,0:T(8,128)(2,1)S(1)}, u32[]{:S(2)}, u32[]{:S(2)}) async-start(bf16[8,8,16,640]{3,2,1,0:T(8,128)(2,1)} %broadcast_in_dim.11), calls=%async_computation | async-start | bytes 2621440 | tf_op jit(solution)/shard_map/all_to_all | solution.py:221
  47.9 13.8 %copy-start.3 = (bf16[8,1,16,640]{3,2,1,0:T(8,128)(2,1)S(1)}, bf16[8,1,16,640]{3,2,1,0:T(8,128)(2,1)}, u32[]{:S(2)}) copy-start(bf16[8,1,16,640]{3,2,1,0:T(8,128)(2,1)} %param.11) | copy-start | bytes 491524
  48.0 13.8 %copy-start.6 = (f32[640]{0:T(1024)S(1)}, f32[640]{0:T(1024)}, u32[]{:S(2)}) copy-start(f32[640]{0:T(1024)} %gain_ref.3) | copy-start | bytes 7684
  48.0 13.8 %copy-start.7 = (f32[640]{0:T(1024)S(1)}, f32[640]{0:T(1024)}, u32[]{:S(2)}) copy-start(f32[640]{0:T(1024)} %bias_ref.3) | copy-start | bytes 7684
  48.0 24.8 %copy-start.1 = (bf16[640,1920]{1,0:T(8,128)(2,1)S(1)}, bf16[640,1920]{1,0:T(8,128)(2,1)}, u32[]{:S(2)}) copy-start(bf16[640,1920]{1,0:T(8,128)(2,1)} %qkv_ref.3) | copy-start | bytes 7372804
  48.0 24.8 %copy-start.9 = (s32[28]{0:T(128)S(1)}, s32[28]{0:T(128)}, u32[]{:S(2)}) copy-start(s32[28]{0:T(128)} %gaps_ref.1) | copy-start | bytes 340
  62.2 15.4 %copy-start.2 = (bf16[640,640]{1,0:T(8,128)(2,1)S(1)}, bf16[640,640]{1,0:T(8,128)(2,1)}, u32[]{:S(2)}) copy-start(bf16[640,640]{1,0:T(8,128)(2,1)} %out_w_ref.1) | copy-start | bytes 2457604
  62.2 15.4 %copy-start.8 = (f32[640]{0:T(1024)S(1)}, f32[640]{0:T(1024)}, u32[]{:S(2)}) copy-start(f32[640]{0:T(1024)} %out_b_ref.1) | copy-start | bytes 7684
  62.2 8.2 %collective-permute-start = (bf16[128,640]{1,0:T(8,128)(2,1)S(1)}, bf16[128,640]{1,0:T(8,128)(2,1)S(1)}, u32[]{:S(2)}, u32[]{:S(2)}) collective-permute-start(bf16[128,640]{1,0:T(8,128)(2,1)S(1)} %get-tuple-element.11.norm_ref), channel_id=1, source_target_pairs={{8,0},{16,8},{24,16},{32,24},{40,32},{48,40},{56,48},{64,56},{72,6... | collective-permute-start | bytes 491528 | tf_op jit(solution)/shard_map/ppermute | solution.py:207
  63.7 9.1 %collective-permute-start.3 = (bf16[128,640]{1,0:T(8,128)(2,1)S(1)}, bf16[128,640]{1,0:T(8,128)(2,1)S(1)}, u32[]{:S(2)}, u32[]{:S(2)}) collective-permute-start(bf16[128,640]{1,0:T(8,128)(2,1)S(1)} %get-tuple-element.11.norm_ref), channel_id=1, source_target_pairs={{0,8},{8,16},{16,24},{24,32},{32,40},{40,48},{48,56},{56,64},{64,7... | collective-permute-start | bytes 491528 | tf_op jit(solution)/shard_map/ppermute | solution.py:207
  68.2 6.5 %collective-permute-start.2 = (bf16[128,640]{1,0:T(8,128)(2,1)S(1)}, bf16[128,640]{1,0:T(8,128)(2,1)S(1)}, u32[]{:S(2)}, u32[]{:S(2)}) collective-permute-start(bf16[128,640]{1,0:T(8,128)(2,1)S(1)} %get-tuple-element.11.norm_ref), channel_id=1, source_target_pairs={{0,16},{8,24},{16,32},{24,40},{32,48},{40,56},{48,64},{56,72},{64,... | collective-permute-start | bytes 491528 | tf_op jit(solution)/shard_map/ppermute | solution.py:207
  70.4 7.2 %collective-permute-start.1 = (bf16[128,640]{1,0:T(8,128)(2,1)S(1)}, bf16[128,640]{1,0:T(8,128)(2,1)S(1)}, u32[]{:S(2)}, u32[]{:S(2)}) collective-permute-start(bf16[128,640]{1,0:T(8,128)(2,1)S(1)} %collective-permute-done.after_ref), channel_id=1, source_target_pairs={{8,0},{16,8},{24,16},{32,24},{40,32},{48,40},{56,48},{64,56},{72,6... | collective-permute-start | bytes 491528 | tf_op jit(solution)/shard_map/ppermute | solution.py:207
